TPU v7x, 512 devices: a whole 4x4x16 slice. The times are simulated.
512 devices in a mesh: ctx: 64 (over x, z), tp: 8 (over y, core).
Axes of the slice: x: 4, y: 4, z: 16, core: 2. Of those that a mesh axis runs over, the one named last changes fastest.
Arguments:
- section_token_rows: bfloat16 [32768, 7168], P(('ctx', 'tp')), may hold values from -6 to 6
- row_target: int32 [32768], P(('ctx', 'tp')), may hold values from 0 to 32767, as said below
- doc_lengths: int32 [128], replicated, may hold values from 1 to 512, as said below
Outputs:
- attn_out: bfloat16 [32768, 5120], P(('ctx', 'tp'))
Inputs may be any that keep to these rules, and one draw needn't show every extreme that they name: row_target is a permutation of the 32768 pack positions; for every block of 512 consecutive previous-section rows and every block of 512 consecutive pack positions, exactly 8 rows of the first go to the second. `doc_lengths`: the lengths sum to 32768; the longest is exactly 512.
All inputs are finite; a program needn't handle non-finite values.
Results may differ from a plain program's by a relative error of at most 0.0029.
Values may be sent and summed in bfloat16 or wider, within the bound.
No kernel may reach another device: no remote copies, remote signals or barrier semaphores. Data moves between devices by JAX's collectives and lax.ppermute only.
A program may use at most 64 MiB of HBM per device.

v0:
```python
import math

import jax
import jax.numpy as jnp
from jax import lax
from jax.sharding import PartitionSpec as P

HEAD_SIZE = 128
QUERY_PER_KEY = 5


def passed_along(block, axis, distance):
    devices = range(lax.axis_size(axis))
    route = [(i - distance, i) for i in devices if i - distance in devices]
    return lax.ppermute(block, axis, route)


def doc_start_of(positions, doc_lengths):
    doc_ends = jnp.cumsum(doc_lengths)
    doc_starts = doc_ends - doc_lengths
    covered = doc_starts[None, :] <= positions[:, None]
    return jnp.max(jnp.where(covered, doc_starts[None, :], 0), axis=1)


def attend(queries, window, query_pos, key_pos, starts):
    allowed = (key_pos[None, :] >= starts[:, None]) & (key_pos[None, :] <= query_pos[:, None])
    score_scale = 1.0 / math.sqrt(HEAD_SIZE)
    outputs = []
    key_rows = window[:, 0:HEAD_SIZE]
    value_rows = window[:, HEAD_SIZE : 2 * HEAD_SIZE]
    for head_at in range(QUERY_PER_KEY):
        scores = (
            jnp.einsum(
                "qd,kd->qk", queries[:, 0, head_at], key_rows, preferred_element_type=jnp.float32
            )
            * score_scale
        )
        scores = jnp.where(allowed, scores, -jnp.inf)
        row_max = jnp.max(scores, axis=1, keepdims=True)
        weights = jnp.exp(scores - row_max)
        row_total = jnp.sum(weights, axis=1, keepdims=True)
        weighted = jnp.dot(
            weights.astype(jnp.bfloat16), value_rows, preferred_element_type=jnp.float32
        )
        outputs.append((weighted / row_total).astype(jnp.bfloat16))
    return jnp.concatenate(outputs, axis=1)


def per_device(section_token_rows, row_target, doc_lengths):
    tp_count = lax.axis_size("tp")
    ctx_count = lax.axis_size("ctx")
    local_rows = section_token_rows.shape[0]
    tok_dev = local_rows * tp_count
    per_pair = tok_dev // ctx_count
    row_width = section_token_rows.shape[1] // tp_count
    groups_here = row_width // ((QUERY_PER_KEY + 2) * HEAD_SIZE)
    kv_width = groups_here * 2 * HEAD_SIZE
    spread_target = jnp.broadcast_to(row_target[:, None], (local_rows, tp_count))
    group_rows, group_target = (
        lax.all_to_all(section_token_rows, "tp", split_axis=1, concat_axis=0, tiled=True),
        lax.all_to_all(spread_target, "tp", split_axis=1, concat_axis=0, tiled=True),
    )
    group_target = group_target[:, 0]
    sort_order = jnp.argsort(group_target)
    sorted_rows = group_rows[sort_order].reshape(ctx_count, per_pair, row_width)
    sorted_target = group_target[sort_order].reshape(ctx_count, per_pair)
    first_pos = lax.axis_index("ctx") * tok_dev
    got_rows, got_target = (
        lax.all_to_all(sorted_rows, "ctx", split_axis=0, concat_axis=0, tiled=True),
        lax.all_to_all(sorted_target, "ctx", split_axis=0, concat_axis=0, tiled=True),
    )
    local_pos = got_target.reshape(tok_dev) - first_pos
    slot_here = (
        jnp.zeros((tok_dev,), jnp.int32).at[local_pos].set(jnp.arange(tok_dev, dtype=jnp.int32))
    )
    packed_tokens = got_rows.reshape(tok_dev, row_width)[slot_here]
    packed_split = packed_tokens.reshape(tok_dev, groups_here, QUERY_PER_KEY + 2, HEAD_SIZE)
    queries = packed_split[:, :, :QUERY_PER_KEY]
    own_kv = packed_split[:, :, QUERY_PER_KEY:].reshape(tok_dev, kv_width)
    earlier = passed_along(own_kv, "ctx", 1)
    window = jnp.concatenate([earlier, own_kv], axis=0)
    query_pos = first_pos + jnp.arange(tok_dev, dtype=jnp.int32)
    key_pos = first_pos - tok_dev + jnp.arange(2 * tok_dev, dtype=jnp.int32)
    starts = doc_start_of(query_pos, doc_lengths)
    results = attend(queries, window, query_pos, key_pos, starts)
    out_width = results.shape[1]
    sendback = results[local_pos].reshape(ctx_count, per_pair, out_width)
    returned = lax.all_to_all(sendback, "ctx", split_axis=0, concat_axis=0, tiled=True).reshape(
        tok_dev, out_width
    )
    group_out = jnp.zeros_like(returned).at[sort_order].set(returned)
    return lax.all_to_all(group_out, "tp", split_axis=0, concat_axis=1, tiled=True)


def solution(mesh):
    placed = (P(("ctx", "tp"), None), P(("ctx", "tp")), P())
    return jax.shard_map(
        per_device, mesh=mesh, in_specs=placed, out_specs=P(("ctx", "tp"), None), check_vma=False
    )
```

profile of v0, /device:TPU:1, one launch (start us, length us, event | category | flops | bytes accessed | tf_op | source)
XLA Modules:
  0.0 197.9 jit_solution(8758262856762758810)
XLA Ops:
  0.0 1.2 broadcast_in_dim.27
  1.2 10.1 %all-to-all-start = ((s32[64,8,1]{0,2,1:T(1,128)}), s32[64,8,1]{0,2,1:T(1,128)S(1)}, u32[]{:S(2)}, u32[]{:S(2)}) async-start(s32[64,8,1]{0,2,1:T(1,128)} %broadcast_in_dim.27), calls=%async_computation | async-start | bytes 8192 | tf_op jit(solution)/shard_map/all_to_all | solution.py:61
  11.3 2.2 %copy.51 = bf16[8,8,8,896]{3,2,0,1:T(8,128)(2,1)} copy(bf16[8,8,8,896]{3,2,1,0:T(8,128)(2,1)} %bitcast.77) | data formatting | bytes 1835008 | tf_op jit(solution)/shard_map/all_to_all | solution.py:60
  13.5 2.3 %all-to-all-done = s32[64,8,1]{0,2,1:T(1,128)S(1)} async-done(((s32[64,8,1]{0,2,1:T(1,128)}), s32[64,8,1]{0,2,1:T(1,128)S(1)}, u32[]{:S(2)}, u32[]{:S(2)}) %all-to-all-start) | async-done | bytes 2080 | tf_op jit(solution)/shard_map/all_to_all | solution.py:61
  15.8 4.1 %all-to-all-start.1 = ((bf16[64,8,896]{2,0,1:T(8,128)(2,1)}), bf16[64,8,896]{2,0,1:T(8,128)(2,1)S(1)}, u32[]{:S(2)}, u32[]{:S(2)}) async-start(bf16[64,8,896]{2,0,1:T(8,128)(2,1)} %bitcast.63), calls=%async_computation.1 | async-start | bytes 1835008 | tf_op jit(solution)/shard_map/all_to_all | solution.py:60
  20.1 3.8 %sort.17 = (s32[512]{0:T(512)}, s32[512]{0:T(512)S(1)}) sort(s32[512]{0:T(512)S(1)} %squeeze.18, s32[512]{0:T(512)S(1)} %iota.17), dimensions={0}, to_apply=%region_0.0 | sort | flops 4608 | bytes 8192 | tf_op jit(solution)/shard_map/jit(argsort)/sort | solution.py:64
  23.9 3.5 %gather_fusion.1 = s32[512]{0:T(512)S(1)} fusion(s32[512]{0:T(512)S(1)} %squeeze.18, s32[1024]{0:T(1024)S(1)} %pad_clamp_fusion.2), kind=kCustom, calls=%fused_computation.1 | custom fusion | bytes 6144 | tf_op jit(solution)/shard_map/gather | solution.py:66
  28.1 5.5 %all-to-all-done.1 = bf16[64,8,896]{2,0,1:T(8,128)(2,1)S(1)} async-done(((bf16[64,8,896]{2,0,1:T(8,128)(2,1)}), bf16[64,8,896]{2,0,1:T(8,128)(2,1)S(1)}, u32[]{:S(2)}, u32[]{:S(2)}) %all-to-all-start.1) | async-done | bytes 917536 | tf_op jit(solution)/shard_map/all_to_all | solution.py:60
  33.6 14.2 %all-to-all-start.3 = ((s32[64,1,8]{2,1,0:T(1,128)}), s32[64,1,8]{2,1,0:T(1,128)S(1)}, u32[]{:S(2)}, u32[]{:S(2)}) async-start(s32[64,1,8]{2,1,0:T(1,128)} %bitcast.6), calls=%async_computation.3 | async-start | bytes 65536 | tf_op jit(solution)/shard_map/all_to_all | solution.py:70
  47.8 2.8 %gather_fusion = bf16[512,896]{1,0:T(8,128)(2,1)} fusion(bf16[512,896]{1,0:T(8,128)(2,1)S(1)} %bitcast.65, s32[1024]{0:T(1024)S(1)} %pad_clamp_fusion.2), kind=kCustom, calls=%fused_computation | custom fusion | bytes 1837056 | tf_op jit(solution)/shard_map/gather | solution.py:65
  50.5 10.5 %all-to-all-done.3 = s32[64,1,8]{2,1,0:T(1,128)S(1)} async-done(((s32[64,1,8]{2,1,0:T(1,128)}), s32[64,1,8]{2,1,0:T(1,128)S(1)}, u32[]{:S(2)}, u32[]{:S(2)}) %all-to-all-start.3) | async-done | bytes 2080 | tf_op jit(solution)/shard_map/all_to_all | solution.py:70
  61.0 4.6 %all-to-all-start.2 = ((bf16[64,8,896]{2,1,0:T(8,128)(2,1)}), bf16[64,8,896]{2,1,0:T(8,128)(2,1)S(1)}, u32[]{:S(2)}, u32[]{:S(2)}) async-start(bf16[64,8,896]{2,1,0:T(8,128)(2,1)} %bitcast.4), calls=%async_computation.2 | async-start | bytes 1835008 | tf_op jit(solution)/shard_map/all_to_all | solution.py:69
  65.9 2.4 %scatter_custom_fusion = s32[512]{0:T(512)S(1)} fusion(s32[512]{0:T(512)S(1)} %bitcast.78, s32[512]{0:T(512)S(1)} %iota.20, s32[]{:T(128)} %constant.11.clone.1), kind=kCustom, calls=%fused_computation.71 | custom fusion | bytes 2052 | tf_op jit(solution)/shard_map/scatter | solution.py:74
  68.4 41.2 %all-to-all-done.2 = bf16[64,8,896]{2,1,0:T(8,128)(2,1)S(1)} async-done(((bf16[64,8,896]{2,1,0:T(8,128)(2,1)}), bf16[64,8,896]{2,1,0:T(8,128)(2,1)S(1)}, u32[]{:S(2)}, u32[]{:S(2)}) %all-to-all-start.2) | async-done | bytes 917536 | tf_op jit(solution)/shard_map/all_to_all | solution.py:69
  109.5 2.0 %gather_fusion.2 = bf16[512,896]{1,0:T(8,128)(2,1)S(1)} fusion(bf16[512,896]{1,0:T(8,128)(2,1)S(1)} %bitcast.64, s32[1024]{0:T(1024)S(1)} %pad_clamp_fusion.1), kind=kCustom, calls=%fused_computation.2 | custom fusion | bytes 1837056 | tf_op jit(solution)/shard_map/gather | solution.py:76
  112.2 6.1 %collective-permute-start = (bf16[512,256]{0,1:T(8,128)(2,1)S(1)}, bf16[512,256]{0,1:T(8,128)(2,1)S(1)}, u32[]{:S(2)}, u32[]{:S(2)}) collective-permute-start(bf16[512,256]{0,1:T(8,128)(2,1)S(1)} %bitcast.75), channel_id=1, source_target_pairs={{0,8},{8,16},{16,24},{24,32},{32,40},{40,48},{48,56},{56,64},{64,7... | collective-permute-start | bytes 786440 | tf_op jit(solution)/shard_map/ppermute | solution.py:15
  119.0 2.4 %collective-permute-done = bf16[512,256]{0,1:T(8,128)(2,1)S(1)} collective-permute-done((bf16[512,256]{0,1:T(8,128)(2,1)S(1)}, bf16[512,256]{0,1:T(8,128)(2,1)S(1)}, u32[]{:S(2)}, u32[]{:S(2)}) %collective-permute-start) | collective-permute-done | bytes 262176 | tf_op jit(solution)/shard_map/ppermute | solution.py:15
  122.2 0.7 fusion.37
  122.9 0.7 fusion.38
  130.8 2.0 %gather_fusion.3 = bf16[512,640]{1,0:T(8,128)(2,1)S(1)} fusion(bf16[512,640]{1,0:T(8,128)(2,1)S(1)} %copy.46, s32[1024]{0:T(1024)S(1)} %pad_clamp_fusion), kind=kCustom, calls=%fused_computation.3 | custom fusion | bytes 1312768 | tf_op jit(solution)/shard_map/gather | solution.py:87
  132.9 43.4 %all_to_all.70 = bf16[64,8,640]{2,1,0:T(8,128)(2,1)S(1)} all-to-all(bf16[64,8,640]{2,1,0:T(8,128)(2,1)S(1)} %bitcast.68), channel_id=1, replica_groups=mesh['ctx'=64,'tp'=8] {'ctx'}, dimensions={0} | all-to-all | bytes 1310720 | tf_op jit(solution)/shard_map/all_to_all | solution.py:88
  176.3 2.8 %scatter_custom_fusion.1 = bf16[512,640]{1,0:T(8,128)(2,1)S(1)} fusion(s32[512]{0:T(512)S(1)} %compare_select_fusion.2, bf16[64,8,640]{2,1,0:T(8,128)(2,1)S(1)} %all_to_all.70, bf16[]{:T(256)} %constant.10.clone.1), kind=kCustom, calls=%fused_computation.48 | custom fusion | bytes 1310722 | tf_op jit(solution)/shard_map/scatter | solution.py:91
  179.1 17.9 %all_to_all.71 = bf16[8,64,640]{2,1,0:T(8,128)(2,1)S(1)} all-to-all(bf16[8,64,640]{2,1,0:T(8,128)(2,1)S(1)} %bitcast.66), channel_id=1, replica_groups=mesh['ctx'=64,'tp'=8] {'tp'}, dimensions={0} | all-to-all | bytes 1310720 | tf_op jit(solution)/shard_map/all_to_all | solution.py:92
  197.0 0.9 copy.49
  (39 shorter events, 10.2 us)
Async XLA Ops:
  1.2 14.6 %all-to-all-start = ((s32[64,8,1]{0,2,1:T(1,128)}), s32[64,8,1]{0,2,1:T(1,128)S(1)}, u32[]{:S(2)}, u32[]{:S(2)}) async-start(s32[64,8,1]{0,2,1:T(1,128)} %broadcast_in_dim.27), calls=%async_computation | async-start | bytes 8192 | tf_op jit(solution)/shard_map/all_to_all | solution.py:61
  15.8 17.7 %all-to-all-start.1 = ((bf16[64,8,896]{2,0,1:T(8,128)(2,1)}), bf16[64,8,896]{2,0,1:T(8,128)(2,1)S(1)}, u32[]{:S(2)}, u32[]{:S(2)}) async-start(bf16[64,8,896]{2,0,1:T(8,128)(2,1)} %bitcast.63), calls=%async_computation.1 | async-start | bytes 1835008 | tf_op jit(solution)/shard_map/all_to_all | solution.py:60
  33.6 27.4 %all-to-all-start.3 = ((s32[64,1,8]{2,1,0:T(1,128)}), s32[64,1,8]{2,1,0:T(1,128)S(1)}, u32[]{:S(2)}, u32[]{:S(2)}) async-start(s32[64,1,8]{2,1,0:T(1,128)} %bitcast.6), calls=%async_computation.3 | async-start | bytes 65536 | tf_op jit(solution)/shard_map/all_to_all | solution.py:70
  61.0 48.5 %all-to-all-start.2 = ((bf16[64,8,896]{2,1,0:T(8,128)(2,1)}), bf16[64,8,896]{2,1,0:T(8,128)(2,1)S(1)}, u32[]{:S(2)}, u32[]{:S(2)}) async-start(bf16[64,8,896]{2,1,0:T(8,128)(2,1)} %bitcast.4), calls=%async_computation.2 | async-start | bytes 1835008 | tf_op jit(solution)/shard_map/all_to_all | solution.py:69
  111.6 6.7 %copy-start = (s32[128]{0:T(128)S(1)}, s32[128]{0:T(128)}, u32[]{:S(2)}) copy-start(s32[128]{0:T(128)} %param.5) | copy-start | bytes 1540
  112.2 9.2 %collective-permute-start = (bf16[512,256]{0,1:T(8,128)(2,1)S(1)}, bf16[512,256]{0,1:T(8,128)(2,1)S(1)}, u32[]{:S(2)}, u32[]{:S(2)}) collective-permute-start(bf16[512,256]{0,1:T(8,128)(2,1)S(1)} %bitcast.75), channel_id=1, source_target_pairs={{0,8},{8,16},{16,24},{24,32},{32,40},{40,48},{48,56},{56,64},{64,7... | collective-permute-start | bytes 786440 | tf_op jit(solution)/shard_map/ppermute | solution.py:15
where the time goes:
time: 198 us
  waiting for transfers between devices  61.9 us (31%)
  blocking collectives  61.4 us (31%)
  starting transfers between devices  39.2 us (20%)
  local copies, waits for them, and re-layouts  21.8 us (11%)
  other arithmetic  7 us (4%)
  matrix products  6.5 us (3%)
    all_to_all x1, blocking collectives, per_device(): lax.all_to_all(sendback, 'ctx', split_axis=0, concat_axis=0, tiled=True)  43.4 us
    all_to_all x1, waiting for transfers between devices, per_device(): lax.all_to_all(sorted_rows, 'ctx', split_axis=0, concat_axis=0, tiled=True)  41.2 us
    all_to_all x1, blocking collectives, per_device(): lax.all_to_all(group_out, 'tp', split_axis=0, concat_axis=1, tiled=True)  17.9 us
    all_to_all x1, starting transfers between devices, per_device(): lax.all_to_all(sorted_target, 'ctx', split_axis=0, concat_axis=0, tiled=T...  14.2 us
    all_to_all x1, waiting for transfers between devices, per_device(): lax.all_to_all(sorted_target, 'ctx', split_axis=0, concat_axis=0, tiled=T...  10.5 us
    all_to_all x1, starting transfers between devices, per_device(): lax.all_to_all(spread_target, 'tp', split_axis=1, concat_axis=0, tiled=True)  10.1 us
    ppermute x1, starting transfers between devices, passed_along(): return lax.ppermute(block, axis, route)  6.13 us
    all_to_all x1, waiting for transfers between devices, per_device(): lax.all_to_all(section_token_rows, 'tp', split_axis=1, concat_axis=0, til...  5.51 us
  transfers between devices with their start and end apart: 5, of which 5 were waited for; matrix products, arithmetic and copies ran while one was open for 8% of the time, Pallas kernels for 0%

commit v1 on v0

v1 whole, which is shorter than its diff:
```python
import functools
import math

import jax
import jax.numpy as jnp
from jax import lax
from jax.experimental import pallas as pl
from jax.experimental.pallas import tpu as pltpu
from jax.sharding import PartitionSpec as P

HEAD_SIZE = 128
QUERY_PER_KEY = 5
LANES = 128
QUERY_WIDTH = QUERY_PER_KEY * HEAD_SIZE
KV_WIDTH = 2 * HEAD_SIZE
KEY_CHUNK = KV_WIDTH + LANES
MASKED = -1e30
QUERY_ROWS = 128
VMEM_LIMIT = 24 * 1024 * 1024


def whole(n):
    return [pl.BlockSpec(memory_space=pltpu.VMEM)] * n


def params():
    return pltpu.CompilerParams(vmem_limit_bytes=VMEM_LIMIT)


def cost(flops, moved):
    return pl.CostEstimate(flops=flops, bytes_accessed=moved, transcendentals=0)


def eye(n):
    return lax.broadcasted_iota(jnp.int32, (n, n), 0) == lax.broadcasted_iota(jnp.int32, (n, n), 1)


def column_to_row(column):
    n = column.shape[0]
    return jnp.sum(jnp.where(eye(n), column, 0.0), axis=0, keepdims=True)


def position_column(chunk_ref):
    high = chunk_ref[:, KV_WIDTH : KV_WIDTH + LANES].astype(jnp.float32)
    return high[:, 0:1] * 256.0 + high[:, 1:2]


def split_kernel(target_ref, rows_ref, keys_ref, queries_ref):
    n = rows_ref.shape[0]
    target = jnp.sum(jnp.where(eye(n), target_ref[...], 0), axis=1, keepdims=True)
    lane = lax.broadcasted_iota(jnp.int32, (n, LANES), 1)
    coded = jnp.where(lane == 0, target >> 8, jnp.where(lane == 1, target & 255, 0))
    queries_ref[0] = rows_ref[:, :QUERY_WIDTH]
    keys_ref[0, :, :KV_WIDTH] = rows_ref[:, QUERY_WIDTH:]
    keys_ref[0, :, KV_WIDTH:] = coded.astype(jnp.float32).astype(jnp.bfloat16)


def split_rows(rows, target, groups):
    n, width = rows.shape
    return pl.pallas_call(
        split_kernel,
        grid=(groups,),
        in_specs=[
            pl.BlockSpec((1, n), lambda g: (0, 0)),
            pl.BlockSpec((n, width // groups), lambda g: (0, g)),
        ],
        out_specs=[
            pl.BlockSpec((1, n, KEY_CHUNK), lambda g: (g, 0, 0)),
            pl.BlockSpec((1, n, QUERY_WIDTH), lambda g: (g, 0, 0)),
        ],
        out_shape=[
            jax.ShapeDtypeStruct((groups, n, KEY_CHUNK), rows.dtype),
            jax.ShapeDtypeStruct((groups, n, QUERY_WIDTH), rows.dtype),
        ],
        compiler_params=params(),
        cost_estimate=cost(0, 2 * rows.size * 2),
        name="split_rows",
    )(target.reshape(1, n), rows)


def sort_kernel(chunk_ref, sorted_ref, forward_ref, backward_ref):
    n = chunk_ref.shape[0]
    column = position_column(chunk_ref)
    row = column_to_row(column)
    rank_row = jnp.sum(jnp.where(column < row, 1.0, 0.0), axis=0, keepdims=True)
    rank_column = jnp.sum(jnp.where(row < column, 1.0, 0.0), axis=1, keepdims=True)
    down = lax.broadcasted_iota(jnp.int32, (n, n), 0).astype(jnp.float32)
    across = lax.broadcasted_iota(jnp.int32, (n, n), 1).astype(jnp.float32)
    forward = jnp.where(rank_row == down, 1.0, 0.0).astype(jnp.bfloat16)
    forward_ref[...] = forward
    backward_ref[...] = jnp.where(rank_column == across, 1.0, 0.0).astype(jnp.bfloat16)
    sorted_ref[...] = jnp.dot(
        forward, chunk_ref[...], preferred_element_type=jnp.float32
    ).astype(sorted_ref.dtype)


def sort_chunk(chunk):
    n = chunk.shape[0]
    return pl.pallas_call(
        sort_kernel,
        in_specs=whole(1),
        out_specs=whole(3),
        out_shape=[
            jax.ShapeDtypeStruct(chunk.shape, chunk.dtype),
            jax.ShapeDtypeStruct((n, n), jnp.bfloat16),
            jax.ShapeDtypeStruct((n, n), jnp.bfloat16),
        ],
        compiler_params=params(),
        cost_estimate=cost(2 * n * chunk.size, 4 * chunk.size),
        name="sort_chunk",
    )(chunk)


def permute_kernel(order_ref, chunk_ref, out_ref):
    out_ref[...] = jnp.dot(
        order_ref[...], chunk_ref[...], preferred_element_type=jnp.float32
    ).astype(out_ref.dtype)


def permute_rows(order, chunk, name):
    return pl.pallas_call(
        permute_kernel,
        in_specs=whole(2),
        out_specs=pl.BlockSpec(memory_space=pltpu.VMEM),
        out_shape=jax.ShapeDtypeStruct(chunk.shape, chunk.dtype),
        compiler_params=params(),
        cost_estimate=cost(2 * chunk.shape[0] * chunk.size, 4 * chunk.size),
        name=name,
    )(order, chunk)


def attend_kernel(heads, starts_ref, own_ref, earlier_ref, query_ref, out_ref, bias_ref):
    n = own_ref.shape[0]
    own_column = position_column(own_ref)
    own_row = column_to_row(own_column)
    earlier_row = column_to_row(position_column(earlier_ref))
    starts = starts_ref[...].astype(jnp.float32)
    start = jnp.max(jnp.where(starts <= own_column, starts, 0.0), axis=1, keepdims=True)
    for half, keys in enumerate((earlier_row, own_row)):
        allowed = (keys >= start) & (keys <= own_column)
        bias_ref[:, half * n : (half + 1) * n] = jnp.where(allowed, 0.0, MASKED)
    scale = math.log2(math.e) / math.sqrt(HEAD_SIZE)
    keys = jnp.concatenate([earlier_ref[:, :HEAD_SIZE], own_ref[:, :HEAD_SIZE]], axis=0)
    values = jnp.concatenate(
        [earlier_ref[:, HEAD_SIZE:KV_WIDTH], own_ref[:, HEAD_SIZE:KV_WIDTH]], axis=0
    )
    for at, head in enumerate(heads):
        for first in range(0, n, QUERY_ROWS):
            rows = slice(first, first + QUERY_ROWS)
            query = query_ref[rows, head * HEAD_SIZE : (head + 1) * HEAD_SIZE]
            scores = lax.dot_general(
                query, keys, (((1,), (1,)), ((), ())), preferred_element_type=jnp.float32
            )
            scores = scores * scale + bias_ref[rows, :]
            weights = jnp.exp2(scores - jnp.max(scores, axis=1, keepdims=True))
            total = jnp.sum(weights, axis=1, keepdims=True)
            weighted = jnp.dot(
                weights.astype(jnp.bfloat16), values, preferred_element_type=jnp.float32
            )
            out_ref[rows, at * HEAD_SIZE : (at + 1) * HEAD_SIZE] = (weighted / total).astype(
                out_ref.dtype
            )


def attend(heads, starts, own, earlier, queries):
    n = own.shape[0]
    width = len(heads) * HEAD_SIZE
    return pl.pallas_call(
        functools.partial(attend_kernel, heads),
        in_specs=whole(4),
        out_specs=pl.BlockSpec(memory_space=pltpu.VMEM),
        out_shape=jax.ShapeDtypeStruct((n, width), own.dtype),
        scratch_shapes=[pltpu.VMEM((n, 2 * n), jnp.float32)],
        compiler_params=params(),
        cost_estimate=cost(8 * n * n * width, 2 * (2 * own.size + 2 * n * width)),
        name="attend",
    )(starts, own, earlier, queries)


def join_kernel(*refs):
    out_ref = refs[-1]
    at = 0
    for ref in refs[:-1]:
        out_ref[:, at : at + ref.shape[2]] = ref[0]
        at += ref.shape[2]


def join_groups(pieces):
    groups, n, _ = pieces[0].shape
    widths = [piece.shape[2] for piece in pieces]
    return pl.pallas_call(
        join_kernel,
        grid=(groups,),
        in_specs=[pl.BlockSpec((1, n, w), lambda g: (g, 0, 0)) for w in widths],
        out_specs=pl.BlockSpec((n, sum(widths)), lambda g: (0, g)),
        out_shape=jax.ShapeDtypeStruct((n, groups * sum(widths)), pieces[0].dtype),
        compiler_params=params(),
        cost_estimate=cost(0, 4 * groups * n * sum(widths)),
        name="join_groups",
    )(*pieces)


def exchange(blocks, axis):
    return lax.all_to_all(blocks, axis, split_axis=0, concat_axis=0, tiled=True)


OUT_CHUNKS = ((0, 1), (2, 3, 4))


def per_device(section_token_rows, row_target, doc_lengths):
    tp_count = lax.axis_size("tp")
    ctx_count = lax.axis_size("ctx")
    local_rows = section_token_rows.shape[0]
    tok_dev = local_rows * tp_count
    per_pair = tok_dev // ctx_count
    starts = (jnp.cumsum(doc_lengths) - doc_lengths).reshape(1, -1)

    keys_out, queries_out = split_rows(section_token_rows, row_target, tp_count)
    keys_in = exchange(keys_out, "tp").reshape(tok_dev, KEY_CHUNK)
    queries_in = exchange(queries_out, "tp").reshape(tok_dev, QUERY_WIDTH)
    keys_sorted, forward, backward = sort_chunk(keys_in)
    queries_sorted = permute_rows(forward, queries_in, "sort_queries")

    own = exchange(keys_sorted.reshape(ctx_count, per_pair, KEY_CHUNK), "ctx")
    own = own.reshape(tok_dev, KEY_CHUNK)
    queries = exchange(queries_sorted.reshape(ctx_count, per_pair, QUERY_WIDTH), "ctx")
    queries = queries.reshape(tok_dev, QUERY_WIDTH)
    route = [(i, (i + 1) % ctx_count) for i in range(ctx_count)]
    earlier = lax.ppermute(own, "ctx", route)

    pieces = []
    for heads in OUT_CHUNKS:
        done = attend(heads, starts, own, earlier, queries)
        width = done.shape[1]
        back = exchange(done.reshape(ctx_count, per_pair, width), "ctx").reshape(tok_dev, width)
        back = permute_rows(backward, back, "unsort")
        pieces.append(exchange(back.reshape(tp_count, local_rows, width), "tp"))
    return join_groups(pieces)


def solution(mesh):
    placed = (P(("ctx", "tp"), None), P(("ctx", "tp")), P())
    return jax.shard_map(
        per_device, mesh=mesh, in_specs=placed, out_specs=P(("ctx", "tp"), None), check_vma=False
    )
```

time: 198 us -> 219 us (1.11)
  waiting for transfers between devices: 61.9 us -> 112 us
  blocking collectives: 61.4 us -> 28.7 us
  local copies, waits for them, and re-layouts: 21.8 us -> 1.95 us
  Pallas kernels: 0 us -> 19 us
  starting transfers between devices: 39.2 us -> 55.6 us
  other arithmetic: 7 us -> 0.28 us
  matrix products: 6.5 us -> 0 us
    ppermute x1, waiting for transfers between devices: 2.42 us -> 37.9 us  [per_device(): earlier = lax.ppermute(own, 'ctx', route)]
    all_to_all x2, blocking collectives: 61.4 us -> 28.7 us  [exchange(): return lax.all_to_all(blocks, axis, split_axis=0, concat_axis=0, tiled=True)]
    all_to_all x4 -> x6, starting transfers between devices: 33 us -> 52.7 us  [exchange(): return lax.all_to_all(blocks, axis, split_axis=0, concat_axis=0, tiled=True)]
    pallas_call x0 -> x8, Pallas kernels: none -> 19 us  [the longest x2 9.21 us: attend(): pl.pallas_call(functools.partial(attend_kernel, heads), in_specs=whole(4)...]
    all_to_all x4 -> x6, waiting for transfers between devices: 59.5 us -> 74.2 us  [exchange(): return lax.all_to_all(blocks, axis, split_axis=0, concat_axis=0, tiled=True)]
    gather x5 -> x0, local copies, waits for them, and re-layouts: 10.8 us -> none  [the longest x1 3.49 us: per_device(): sorted_target = group_target[sort_order].reshape(ctx_count, per_pair)]
    dot_general x10 -> x0, matrix products: 6.5 us -> none  [the longest x5 3.57 us: attend(): jnp.einsum('qd,kd->qk', queries[:, 0, head_at], key_rows, preferred_eleme...]
    scatter x2 -> x0, local copies, waits for them, and re-layouts: 5.23 us -> none  [the longest x1 2.8 us: per_device(): group_out = jnp.zeros_like(returned).at[sort_order].set(returned)]
  transfers between devices with their start and end apart: 5 -> 7, of which waited for: 5 -> 6; matrix products, arithmetic and copies ran while one was open for 8% -> 0% of each run, Pallas kernels for 0% -> 4%
where the time goes in v1:
time: 219 us; the launch traced here: 218 us
  waiting for transfers between devices  112 us (51%)
  starting transfers between devices  55.6 us (25%)
  blocking collectives  28.7 us (13%)
  Pallas kernels  19 us (9%)
    all_to_all x6, waiting for transfers between devices, exchange(): return lax.all_to_all(blocks, axis, split_axis=0, concat_axis=0, tiled=True)  74.2 us
    all_to_all x6, starting transfers between devices, exchange(): return lax.all_to_all(blocks, axis, split_axis=0, concat_axis=0, tiled=True)  52.7 us
    ppermute x1, waiting for transfers between devices, per_device(): earlier = lax.ppermute(own, 'ctx', route)  37.9 us
    all_to_all x2, blocking collectives, exchange(): return lax.all_to_all(blocks, axis, split_axis=0, concat_axis=0, tiled=True)  28.7 us
    pallas_call x2, Pallas kernels, attend(): pl.pallas_call(functools.partial(attend_kernel, heads), in_specs=whole(4)...  9.21 us
  transfers between devices with their start and end apart: 7, of which 6 were waited for; matrix products, arithmetic and copies ran while one was open for 0% of the time, Pallas kernels for 4%

profile of v1, /device:TPU:1, one launch (start us, length us, event | category | flops | bytes accessed | tf_op | source)
XLA Modules:
  0.0 217.8 jit_solution(498196787459034785)
XLA Ops:
  0.0 0.7 copy-done.1
  0.7 1.2 copy-done
  1.8 2.8 %split_rows.1 = (bf16[8,64,384]{2,1,0:T(8,128)(2,1)S(1)}, bf16[8,64,640]{2,1,0:T(8,128)(2,1)}) custom-call(s32[1,64]{1,0:T(1,128)S(1)} %bitcast.26, bf16[64,7168]{1,0:T(8,128)(2,1)S(1)} %copy-done), custom_call_target="tpu_custom_call" | custom-call | bytes 1835008 | tf_op jit(solution)/shard_map/split_rows/pallas_call | solution.py:60
  4.6 17.3 %all_to_all.40 = bf16[8,64,384]{2,1,0:T(8,128)(2,1)S(1)} all-to-all(bf16[8,64,384]{2,1,0:T(8,128)(2,1)S(1)} %get-tuple-element.10), channel_id=1, replica_groups=mesh['ctx'=64,'tp'=8] {'tp'}, dimensions={0} | all-to-all | bytes 786432 | tf_op jit(solution)/shard_map/all_to_all | solution.py:204
  21.9 4.3 %all-to-all-start.2 = ((bf16[8,64,640]{2,1,0:T(8,128)(2,1)}), bf16[8,64,640]{2,1,0:T(8,128)(2,1)S(1)}, u32[]{:S(2)}, u32[]{:S(2)}) async-start(bf16[8,64,640]{2,1,0:T(8,128)(2,1)} %get-tuple-element.14), calls=%async_computation.2 | async-start | bytes 1310720 | tf_op jit(solution)/shard_map/all_to_all | solution.py:204
  26.2 1.6 sort_chunk.1
  27.8 9.2 %all-to-all-done.2 = bf16[8,64,640]{2,1,0:T(8,128)(2,1)S(1)} async-done(((bf16[8,64,640]{2,1,0:T(8,128)(2,1)}), bf16[8,64,640]{2,1,0:T(8,128)(2,1)S(1)}, u32[]{:S(2)}, u32[]{:S(2)}) %all-to-all-start.2) | async-done | bytes 655392 | tf_op jit(solution)/shard_map/all_to_all | solution.py:204
  37.0 14.8 %all-to-all-start.1 = ((bf16[64,8,384]{2,1,0:T(8,128)(2,1)}), bf16[64,8,384]{2,1,0:T(8,128)(2,1)S(1)}, u32[]{:S(2)}, u32[]{:S(2)}) async-start(bf16[64,8,384]{2,1,0:T(8,128)(2,1)} %bitcast.4), calls=%async_computation.1 | async-start | bytes 786432 | tf_op jit(solution)/shard_map/all_to_all | solution.py:204
  51.8 1.4 sort_queries.1
  53.2 22.8 %all-to-all-done.1 = bf16[64,8,384]{2,1,0:T(8,128)(2,1)S(1)} async-done(((bf16[64,8,384]{2,1,0:T(8,128)(2,1)}), bf16[64,8,384]{2,1,0:T(8,128)(2,1)S(1)}, u32[]{:S(2)}, u32[]{:S(2)}) %all-to-all-start.1) | async-done | bytes 393248 | tf_op jit(solution)/shard_map/all_to_all | solution.py:204
  76.0 8.0 %all-to-all-start.3 = ((bf16[64,8,640]{2,1,0:T(8,128)(2,1)}), bf16[64,8,640]{2,1,0:T(8,128)(2,1)S(1)}, u32[]{:S(2)}, u32[]{:S(2)}) async-start(bf16[64,8,640]{2,1,0:T(8,128)(2,1)} %bitcast.7), calls=%async_computation.3 | async-start | bytes 1310720 | tf_op jit(solution)/shard_map/all_to_all | solution.py:204
  84.1 2.9 %collective-permute-start = (bf16[512,384]{1,0:T(8,128)(2,1)S(1)}, bf16[512,384]{1,0:T(8,128)(2,1)S(1)}, u32[]{:S(2)}, u32[]{:S(2)}) collective-permute-start(bf16[512,384]{1,0:T(8,128)(2,1)S(1)} %bitcast.22), channel_id=1, source_target_pairs={{0,8},{8,16},{16,24},{24,32},{32,40},{40,48},{48,56},{56,64},{64,7... | collective-permute-start | bytes 1179656 | tf_op jit(solution)/shard_map/ppermute | solution.py:229
  87.4 37.9 %collective-permute-done.earlier_ref = bf16[512,384]{1,0:T(8,128)(2,1)S(1)} collective-permute-done((bf16[512,384]{1,0:T(8,128)(2,1)S(1)}, bf16[512,384]{1,0:T(8,128)(2,1)S(1)}, u32[]{:S(2)}, u32[]{:S(2)}) %collective-permute-start) | collective-permute-done | bytes 393248 | tf_op jit(solution)/shard_map/ppermute | solution.py:229
  125.3 3.9 %attend.2 = bf16[512,256]{1,0:T(8,128)(2,1)} custom-call(s32[1,128]{1,0:T(1,128)S(1)} %subtract_bitcast_fusion.starts_ref, bf16[512,384]{1,0:T(8,128)(2,1)S(1)} %bitcast.23, bf16[512,384]{1,0:T(8,128)(2,1)S(1)} %collective-permute-done.earlier_ref, bf16[512,640]{1,0:T(8,128)(2,1)S(1)} %bitcast.20), custom_call_target="tpu_custom_call" | custom-call | flops 536870912 | bytes 1310720 | tf_op jit(solution)/shard_map/attend/pallas_call | solution.py:168
  129.2 10.7 %all-to-all-start.4 = ((bf16[64,8,256]{2,1,0:T(8,128)(2,1)}), bf16[64,8,256]{2,1,0:T(8,128)(2,1)S(1)}, u32[]{:S(2)}, u32[]{:S(2)}) async-start(bf16[64,8,256]{2,1,0:T(8,128)(2,1)} %bitcast.9), calls=%async_computation.4 | async-start | bytes 524288 | tf_op jit(solution)/shard_map/all_to_all | solution.py:204
  139.9 5.3 %attend.3 = bf16[512,384]{1,0:T(8,128)(2,1)} custom-call(s32[1,128]{1,0:T(1,128)S(1)} %subtract_bitcast_fusion.starts_ref, bf16[512,384]{1,0:T(8,128)(2,1)S(1)} %bitcast.24, bf16[512,384]{1,0:T(8,128)(2,1)S(1)} %collective-permute-done.earlier_ref, bf16[512,640]{1,0:T(8,128)(2,1)S(1)} %bitcast.21), custom_call_target="tpu_custom_call" | custom-call | flops 805306368 | bytes 1572864 | tf_op jit(solution)/shard_map/attend/pallas_call | solution.py:168
  145.2 13.6 %all-to-all-done.4 = bf16[64,8,256]{2,1,0:T(8,128)(2,1)S(1)} async-done(((bf16[64,8,256]{2,1,0:T(8,128)(2,1)}), bf16[64,8,256]{2,1,0:T(8,128)(2,1)S(1)}, u32[]{:S(2)}, u32[]{:S(2)}) %all-to-all-start.4) | async-done | bytes 262176 | tf_op jit(solution)/shard_map/all_to_all | solution.py:204
  158.8 7.8 %all-to-all-start.6 = ((bf16[64,8,384]{2,1,0:T(8,128)(2,1)}), bf16[64,8,384]{2,1,0:T(8,128)(2,1)S(1)}, u32[]{:S(2)}, u32[]{:S(2)}) async-start(bf16[64,8,384]{2,1,0:T(8,128)(2,1)} %bitcast.12), calls=%async_computation.6 | async-start | bytes 786432 | tf_op jit(solution)/shard_map/all_to_all | solution.py:204
  166.7 1.0 unsort.2
  167.7 22.5 %all-to-all-done.6 = bf16[64,8,384]{2,1,0:T(8,128)(2,1)S(1)} async-done(((bf16[64,8,384]{2,1,0:T(8,128)(2,1)}), bf16[64,8,384]{2,1,0:T(8,128)(2,1)S(1)}, u32[]{:S(2)}, u32[]{:S(2)}) %all-to-all-start.6) | async-done | bytes 393248 | tf_op jit(solution)/shard_map/all_to_all | solution.py:204
  190.2 7.1 %all-to-all-start.5 = ((bf16[8,64,256]{2,1,0:T(8,128)(2,1)}), bf16[8,64,256]{2,1,0:T(8,128)(2,1)S(1)}, u32[]{:S(2)}, u32[]{:S(2)}) async-start(bf16[8,64,256]{2,1,0:T(8,128)(2,1)} %bitcast.11), calls=%async_computation.5 | async-start | bytes 524288 | tf_op jit(solution)/shard_map/all_to_all | solution.py:204
  197.7 6.1 %all-to-all-done.5.refs_0_ = bf16[8,64,256]{2,1,0:T(8,128)(2,1)S(1)} async-done(((bf16[8,64,256]{2,1,0:T(8,128)(2,1)}), bf16[8,64,256]{2,1,0:T(8,128)(2,1)S(1)}, u32[]{:S(2)}, u32[]{:S(2)}) %all-to-all-start.5) | async-done | bytes 262176 | tf_op jit(solution)/shard_map/all_to_all | solution.py:204
  203.8 11.5 %all_to_all.41.refs_1_ = bf16[8,64,384]{2,1,0:T(8,128)(2,1)S(1)} all-to-all(bf16[8,64,384]{2,1,0:T(8,128)(2,1)S(1)} %bitcast.18), channel_id=1, replica_groups=mesh['ctx'=64,'tp'=8] {'tp'}, dimensions={0} | all-to-all | bytes 786432 | tf_op jit(solution)/shard_map/all_to_all | solution.py:204
  215.2 2.6 %join_groups.1 = bf16[64,5120]{1,0:T(8,128)(2,1)} custom-call(bf16[8,64,256]{2,1,0:T(8,128)(2,1)S(1)} %all-to-all-done.5.refs_0_, bf16[8,64,384]{2,1,0:T(8,128)(2,1)S(1)} %all_to_all.41.refs_1_), custom_call_target="tpu_custom_call" | custom-call | bytes 1310720 | tf_op jit(solution)/shard_map/join_groups/pallas_call | solution.py:191
  (10 shorter events, 0.8 us)
Async XLA Ops:
  0.0 0.7 copy-start.1
  0.7 1.2 copy-start
  21.9 15.1 %all-to-all-start.2 = ((bf16[8,64,640]{2,1,0:T(8,128)(2,1)}), bf16[8,64,640]{2,1,0:T(8,128)(2,1)S(1)}, u32[]{:S(2)}, u32[]{:S(2)}) async-start(bf16[8,64,640]{2,1,0:T(8,128)(2,1)} %get-tuple-element.14), calls=%async_computation.2 | async-start | bytes 1310720 | tf_op jit(solution)/shard_map/all_to_all | solution.py:204
  37.0 39.1 %all-to-all-start.1 = ((bf16[64,8,384]{2,1,0:T(8,128)(2,1)}), bf16[64,8,384]{2,1,0:T(8,128)(2,1)S(1)}, u32[]{:S(2)}, u32[]{:S(2)}) async-start(bf16[64,8,384]{2,1,0:T(8,128)(2,1)} %bitcast.4), calls=%async_computation.1 | async-start | bytes 786432 | tf_op jit(solution)/shard_map/all_to_all | solution.py:204
  76.0 49.2 %all-to-all-start.3 = ((bf16[64,8,640]{2,1,0:T(8,128)(2,1)}), bf16[64,8,640]{2,1,0:T(8,128)(2,1)S(1)}, u32[]{:S(2)}, u32[]{:S(2)}) async-start(bf16[64,8,640]{2,1,0:T(8,128)(2,1)} %bitcast.7), calls=%async_computation.3 | async-start | bytes 1310720 | tf_op jit(solution)/shard_map/all_to_all | solution.py:204
  84.1 2.9 %copy-start.2 = (s32[128]{0:T(128)S(1)}, s32[128]{0:T(128)}, u32[]{:S(2)}) copy-start(s32[128]{0:T(128)} %param.5) | copy-start | bytes 1540
  84.1 41.2 %collective-permute-start = (bf16[512,384]{1,0:T(8,128)(2,1)S(1)}, bf16[512,384]{1,0:T(8,128)(2,1)S(1)}, u32[]{:S(2)}, u32[]{:S(2)}) collective-permute-start(bf16[512,384]{1,0:T(8,128)(2,1)S(1)} %bitcast.22), channel_id=1, source_target_pairs={{0,8},{8,16},{16,24},{24,32},{32,40},{40,48},{48,56},{56,64},{64,7... | collective-permute-start | bytes 1179656 | tf_op jit(solution)/shard_map/ppermute | solution.py:229
  129.2 29.6 %all-to-all-start.4 = ((bf16[64,8,256]{2,1,0:T(8,128)(2,1)}), bf16[64,8,256]{2,1,0:T(8,128)(2,1)S(1)}, u32[]{:S(2)}, u32[]{:S(2)}) async-start(bf16[64,8,256]{2,1,0:T(8,128)(2,1)} %bitcast.9), calls=%async_computation.4 | async-start | bytes 524288 | tf_op jit(solution)/shard_map/all_to_all | solution.py:204
  158.8 31.3 %all-to-all-start.6 = ((bf16[64,8,384]{2,1,0:T(8,128)(2,1)}), bf16[64,8,384]{2,1,0:T(8,128)(2,1)S(1)}, u32[]{:S(2)}, u32[]{:S(2)}) async-start(bf16[64,8,384]{2,1,0:T(8,128)(2,1)} %bitcast.12), calls=%async_computation.6 | async-start | bytes 786432 | tf_op jit(solution)/shard_map/all_to_all | solution.py:204
  190.2 13.6 %all-to-all-start.5 = ((bf16[8,64,256]{2,1,0:T(8,128)(2,1)}), bf16[8,64,256]{2,1,0:T(8,128)(2,1)S(1)}, u32[]{:S(2)}, u32[]{:S(2)}) async-start(bf16[8,64,256]{2,1,0:T(8,128)(2,1)} %bitcast.11), calls=%async_computation.5 | async-start | bytes 524288 | tf_op jit(solution)/shard_map/all_to_all | solution.py:204

commit v2 on v1

--- a/solution.py
+++ b/solution.py
@@ -13,7 +13,8 @@
 LANES = 128
 QUERY_WIDTH = QUERY_PER_KEY * HEAD_SIZE
 KV_WIDTH = 2 * HEAD_SIZE
-KEY_CHUNK = KV_WIDTH + LANES
+WIDTH = KV_WIDTH + LANES + QUERY_WIDTH
+QUERIES_AT = KV_WIDTH + LANES
 MASKED = -1e30
 QUERY_ROWS = 128
 VMEM_LIMIT = 24 * 1024 * 1024
@@ -45,14 +46,14 @@
     return high[:, 0:1] * 256.0 + high[:, 1:2]
 
 
-def split_kernel(target_ref, rows_ref, keys_ref, queries_ref):
+def split_kernel(target_ref, rows_ref, out_ref):
     n = rows_ref.shape[0]
     target = jnp.sum(jnp.where(eye(n), target_ref[...], 0), axis=1, keepdims=True)
     lane = lax.broadcasted_iota(jnp.int32, (n, LANES), 1)
     coded = jnp.where(lane == 0, target >> 8, jnp.where(lane == 1, target & 255, 0))
-    queries_ref[0] = rows_ref[:, :QUERY_WIDTH]
-    keys_ref[0, :, :KV_WIDTH] = rows_ref[:, QUERY_WIDTH:]
-    keys_ref[0, :, KV_WIDTH:] = coded.astype(jnp.float32).astype(jnp.bfloat16)
+    out_ref[0, :, QUERIES_AT:] = rows_ref[:, :QUERY_WIDTH]
+    out_ref[0, :, :KV_WIDTH] = rows_ref[:, QUERY_WIDTH:]
+    out_ref[0, :, KV_WIDTH:QUERIES_AT] = coded.astype(jnp.float32).astype(jnp.bfloat16)
 
 
 def split_rows(rows, target, groups):
@@ -64,21 +65,15 @@
             pl.BlockSpec((1, n), lambda g: (0, 0)),
             pl.BlockSpec((n, width // groups), lambda g: (0, g)),
         ],
-        out_specs=[
-            pl.BlockSpec((1, n, KEY_CHUNK), lambda g: (g, 0, 0)),
-            pl.BlockSpec((1, n, QUERY_WIDTH), lambda g: (g, 0, 0)),
-        ],
-        out_shape=[
-            jax.ShapeDtypeStruct((groups, n, KEY_CHUNK), rows.dtype),
-            jax.ShapeDtypeStruct((groups, n, QUERY_WIDTH), rows.dtype),
-        ],
+        out_specs=pl.BlockSpec((1, n, WIDTH), lambda g: (g, 0, 0)),
+        out_shape=jax.ShapeDtypeStruct((groups, n, WIDTH), rows.dtype),
         compiler_params=params(),
         cost_estimate=cost(0, 2 * rows.size * 2),
         name="split_rows",
     )(target.reshape(1, n), rows)
 
 
-def sort_kernel(chunk_ref, sorted_ref, forward_ref, backward_ref):
+def sort_kernel(chunk_ref, sorted_ref, backward_ref):
     n = chunk_ref.shape[0]
     column = position_column(chunk_ref)
     row = column_to_row(column)
@@ -87,7 +82,6 @@
     down = lax.broadcasted_iota(jnp.int32, (n, n), 0).astype(jnp.float32)
     across = lax.broadcasted_iota(jnp.int32, (n, n), 1).astype(jnp.float32)
     forward = jnp.where(rank_row == down, 1.0, 0.0).astype(jnp.bfloat16)
-    forward_ref[...] = forward
     backward_ref[...] = jnp.where(rank_column == across, 1.0, 0.0).astype(jnp.bfloat16)
     sorted_ref[...] = jnp.dot(
         forward, chunk_ref[...], preferred_element_type=jnp.float32
@@ -99,10 +93,9 @@
     return pl.pallas_call(
         sort_kernel,
         in_specs=whole(1),
-        out_specs=whole(3),
+        out_specs=whole(2),
         out_shape=[
             jax.ShapeDtypeStruct(chunk.shape, chunk.dtype),
-            jax.ShapeDtypeStruct((n, n), jnp.bfloat16),
             jax.ShapeDtypeStruct((n, n), jnp.bfloat16),
         ],
         compiler_params=params(),
@@ -129,7 +122,7 @@
     )(order, chunk)
 
 
-def attend_kernel(heads, starts_ref, own_ref, earlier_ref, query_ref, out_ref, bias_ref):
+def attend_kernel(heads, starts_ref, own_ref, earlier_ref, out_ref, bias_ref):
     n = own_ref.shape[0]
     own_column = position_column(own_ref)
     own_row = column_to_row(own_column)
@@ -147,7 +140,8 @@
     for at, head in enumerate(heads):
         for first in range(0, n, QUERY_ROWS):
             rows = slice(first, first + QUERY_ROWS)
-            query = query_ref[rows, head * HEAD_SIZE : (head + 1) * HEAD_SIZE]
+            at_column = QUERIES_AT + head * HEAD_SIZE
+            query = own_ref[rows, at_column : at_column + HEAD_SIZE]
             scores = lax.dot_general(
                 query, keys, (((1,), (1,)), ((), ())), preferred_element_type=jnp.float32
             )
@@ -162,19 +156,19 @@
             )
 
 
-def attend(heads, starts, own, earlier, queries):
+def attend(heads, starts, own, earlier):
     n = own.shape[0]
     width = len(heads) * HEAD_SIZE
     return pl.pallas_call(
         functools.partial(attend_kernel, heads),
-        in_specs=whole(4),
+        in_specs=whole(3),
         out_specs=pl.BlockSpec(memory_space=pltpu.VMEM),
         out_shape=jax.ShapeDtypeStruct((n, width), own.dtype),
         scratch_shapes=[pltpu.VMEM((n, 2 * n), jnp.float32)],
         compiler_params=params(),
         cost_estimate=cost(8 * n * n * width, 2 * (2 * own.size + 2 * n * width)),
         name="attend",
-    )(starts, own, earlier, queries)
+    )(starts, own, earlier)
 
 
 def join_kernel(*refs):
@@ -204,7 +198,7 @@
     return lax.all_to_all(blocks, axis, split_axis=0, concat_axis=0, tiled=True)
 
 
-OUT_CHUNKS = ((0, 1), (2, 3, 4))
+OUT_CHUNKS = ((0, 1, 2, 3, 4),)
 
 
 def per_device(section_token_rows, row_target, doc_lengths):
@@ -215,22 +209,16 @@
     per_pair = tok_dev // ctx_count
     starts = (jnp.cumsum(doc_lengths) - doc_lengths).reshape(1, -1)
 
-    keys_out, queries_out = split_rows(section_token_rows, row_target, tp_count)
-    keys_in = exchange(keys_out, "tp").reshape(tok_dev, KEY_CHUNK)
-    queries_in = exchange(queries_out, "tp").reshape(tok_dev, QUERY_WIDTH)
-    keys_sorted, forward, backward = sort_chunk(keys_in)
-    queries_sorted = permute_rows(forward, queries_in, "sort_queries")
-
-    own = exchange(keys_sorted.reshape(ctx_count, per_pair, KEY_CHUNK), "ctx")
-    own = own.reshape(tok_dev, KEY_CHUNK)
-    queries = exchange(queries_sorted.reshape(ctx_count, per_pair, QUERY_WIDTH), "ctx")
-    queries = queries.reshape(tok_dev, QUERY_WIDTH)
+    rows = split_rows(section_token_rows, row_target, tp_count)
+    rows = exchange(rows, "tp").reshape(tok_dev, WIDTH)
+    rows, backward = sort_chunk(rows)
+    own = exchange(rows.reshape(ctx_count, per_pair, WIDTH), "ctx").reshape(tok_dev, WIDTH)
     route = [(i, (i + 1) % ctx_count) for i in range(ctx_count)]
-    earlier = lax.ppermute(own, "ctx", route)
+    earlier = lax.ppermute(own[:, :QUERIES_AT], "ctx", route)
 
     pieces = []
     for heads in OUT_CHUNKS:
-        done = attend(heads, starts, own, earlier, queries)
+        done = attend(heads, starts, own, earlier)
         width = done.shape[1]
         back = exchange(done.reshape(ctx_count, per_pair, width), "ctx").reshape(tok_dev, width)
         back = permute_rows(backward, back, "unsort")

time: 219 us -> 178 us (0.81)
  blocking collectives: 28.7 us -> 151 us
  waiting for transfers between devices: 112 us -> 6.28 us
  starting transfers between devices: 55.6 us -> 5.14 us
  Pallas kernels: 19 us -> 12.6 us
    all_to_all x2 -> x4, blocking collectives: 28.7 us -> 151 us  [exchange(): return lax.all_to_all(blocks, axis, split_axis=0, concat_axis=0, tiled=True)]
    all_to_all x6 -> x0, waiting for transfers between devices: 74.2 us -> none  [exchange(): return lax.all_to_all(blocks, axis, split_axis=0, concat_axis=0, tiled=True)]
    all_to_all x6 -> x0, starting transfers between devices: 52.7 us -> none  [exchange(): return lax.all_to_all(blocks, axis, split_axis=0, concat_axis=0, tiled=True)]
    ppermute x1, waiting for transfers between devices: 37.9 us -> 6.28 us  [per_device(): earlier = lax.ppermute(own[:, :QUERIES_AT], 'ctx', route)]
    pallas_call x3 -> x2, Pallas kernels: 10.8 us -> 8.4 us  [the longest x1 7.3 us: attend(): pl.pallas_call(functools.partial(attend_kernel, heads), in_specs=whole(3)...]
    pallas_call x3 -> x1, Pallas kernels: 2.86 us -> 0.57 us  [permute_rows(): pl.pallas_call(permute_kernel, in_specs=whole(2), out_specs=pl.BlockSpec(...]
    ppermute x1, starting transfers between devices: 2.92 us -> 5.14 us  [per_device(): earlier = lax.ppermute(own[:, :QUERIES_AT], 'ctx', route)]
  transfers between devices with their start and end apart: 7 -> 1, of which waited for: 6 -> 1; matrix products, arithmetic and copies ran while one was open for 0% -> 0% of each run, Pallas kernels for 4% -> 0%
where the time goes in v2:
time: 178 us; the launch traced here: 177 us
  blocking collectives  151 us (85%)
  Pallas kernels  12.6 us (7%)
  waiting for transfers between devices  6.28 us (4%)
  starting transfers between devices  5.14 us (3%)
  local copies, waits for them, and re-layouts  1.99 us (1%)
    all_to_all x4, blocking collectives, exchange(): return lax.all_to_all(blocks, axis, split_axis=0, concat_axis=0, tiled=True)  151 us
    pallas_call x1, Pallas kernels, attend(): pl.pallas_call(functools.partial(attend_kernel, heads), in_specs=whole(3)...  7.3 us
    ppermute x1, waiting for transfers between devices, per_device(): earlier = lax.ppermute(own[:, :QUERIES_AT], 'ctx', route)  6.28 us
    ppermute x1, starting transfers between devices, per_device(): earlier = lax.ppermute(own[:, :QUERIES_AT], 'ctx', route)  5.14 us
  transfers between devices with their start and end apart: 1, of which 1 were waited for; matrix products, arithmetic and copies ran while one was open for 0% of the time, Pallas kernels for 0%

profile of v2, /device:TPU:1, one launch (start us, length us, event | category | flops | bytes accessed | tf_op | source)
XLA Modules:
  0.0 177.3 jit_solution(1871790961459630932)
XLA Ops:
  0.0 0.0 copy-start.1
  0.0 0.7 copy-done.1
  0.7 0.0 copy-start
  0.7 1.2 copy-done
  1.8 1.0 split_rows.1
  2.8 24.2 %all_to_all.20 = bf16[8,64,1024]{2,1,0:T(8,128)(2,1)S(1)} all-to-all(bf16[8,64,1024]{2,1,0:T(8,128)(2,1)S(1)} %split_rows.1), channel_id=1, replica_groups=mesh['ctx'=64,'tp'=8] {'tp'}, dimensions={0} | all-to-all | bytes 2097152 | tf_op jit(solution)/shard_map/all_to_all | solution.py:198
  27.0 1.1 sort_chunk.1
  28.1 64.8 %all_to_all.21 = bf16[64,8,1024]{2,1,0:T(8,128)(2,1)S(1)} all-to-all(bf16[64,8,1024]{2,1,0:T(8,128)(2,1)S(1)} %bitcast.15), channel_id=1, replica_groups=mesh['ctx'=64,'tp'=8] {'ctx'}, dimensions={0} | all-to-all | bytes 2097152 | tf_op jit(solution)/shard_map/all_to_all | solution.py:198
  93.0 0.0 copy-start.2
  93.0 5.1 %collective-permute-start = (bf16[512,384]{1,0:T(8,128)(2,1)S(1)}, bf16[512,384]{1,0:T(8,128)(2,1)S(1)}, u32[]{:S(2)}, u32[]{:S(2)}) collective-permute-start(bf16[512,384]{1,0:T(8,128)(2,1)S(1)} %slice.4), channel_id=1, source_target_pairs={{0,8},{8,16},{16,24},{24,32},{32,40},{40,48},{48,56},{56,64},{64,7... | collective-permute-start | bytes 1179656 | tf_op jit(solution)/shard_map/ppermute | solution.py:217
  98.1 0.0 copy-done.2
  98.1 0.1 copy.5
  98.2 0.2 reduce-window.9
  98.4 0.1 reduce
  98.5 6.3 %collective-permute-done.earlier_ref = bf16[512,384]{1,0:T(8,128)(2,1)S(1)} collective-permute-done((bf16[512,384]{1,0:T(8,128)(2,1)S(1)}, bf16[512,384]{1,0:T(8,128)(2,1)S(1)}, u32[]{:S(2)}, u32[]{:S(2)}) %collective-permute-start) | collective-permute-done | bytes 393248 | tf_op jit(solution)/shard_map/ppermute | solution.py:217
  104.8 7.3 %attend.1 = bf16[512,640]{1,0:T(8,128)(2,1)S(1)} custom-call(s32[1,128]{1,0:T(1,128)S(1)} %subtract_bitcast_fusion.starts_ref, bf16[512,1024]{1,0:T(8,128)(2,1)S(1)} %bitcast.13, bf16[512,384]{1,0:T(8,128)(2,1)S(1)} %collective-permute-done.earlier_ref), custom_call_target="tpu_custom_call" | custom-call | flops 1342177280 | bytes 3407872 | tf_op jit(solution)/shard_map/attend/pallas_call | solution.py:162
  112.1 44.2 %all_to_all.22 = bf16[64,8,640]{2,1,0:T(8,128)(2,1)S(1)} all-to-all(bf16[64,8,640]{2,1,0:T(8,128)(2,1)S(1)} %bitcast.16), channel_id=1, replica_groups=mesh['ctx'=64,'tp'=8] {'ctx'}, dimensions={0} | all-to-all | bytes 1310720 | tf_op jit(solution)/shard_map/all_to_all | solution.py:198
  156.3 0.6 unsort.1
  156.8 17.8 %all_to_all.23.refs_0_ = bf16[8,64,640]{2,1,0:T(8,128)(2,1)S(1)} all-to-all(bf16[8,64,640]{2,1,0:T(8,128)(2,1)S(1)} %bitcast.11), channel_id=1, replica_groups=mesh['ctx'=64,'tp'=8] {'tp'}, dimensions={0} | all-to-all | bytes 1310720 | tf_op jit(solution)/shard_map/all_to_all | solution.py:198
  174.7 2.6 %join_groups.1 = bf16[64,5120]{1,0:T(8,128)(2,1)} custom-call(bf16[8,64,640]{2,1,0:T(8,128)(2,1)S(1)} %all_to_all.23.refs_0_), custom_call_target="tpu_custom_call" | custom-call | bytes 1310720 | tf_op jit(solution)/shard_map/join_groups/pallas_call | solution.py:185
  (2 shorter events, 0.0 us)
Async XLA Ops:
  0.0 0.7 copy-start.1
  0.7 1.2 copy-start
  93.0 5.2 %copy-start.2 = (s32[128]{0:T(128)S(1)}, s32[128]{0:T(128)}, u32[]{:S(2)}) copy-start(s32[128]{0:T(128)} %param.5) | copy-start | bytes 1540
  93.0 11.8 %collective-permute-start = (bf16[512,384]{1,0:T(8,128)(2,1)S(1)}, bf16[512,384]{1,0:T(8,128)(2,1)S(1)}, u32[]{:S(2)}, u32[]{:S(2)}) collective-permute-start(bf16[512,384]{1,0:T(8,128)(2,1)S(1)} %slice.4), channel_id=1, source_target_pairs={{0,8},{8,16},{16,24},{24,32},{32,40},{40,48},{48,56},{56,64},{64,7... | collective-permute-start | bytes 1179656 | tf_op jit(solution)/shard_map/ppermute | solution.py:217

commit v3 on v1

v3 whole, which is shorter than its diff:
```python
import functools
import math

import jax
import jax.numpy as jnp
from jax import lax
from jax.experimental import pallas as pl
from jax.experimental.pallas import tpu as pltpu
from jax.sharding import Mesh
from jax.sharding import PartitionSpec as P

HEAD_SIZE = 128
QUERY_PER_KEY = 5
LANES = 128
BLOCK = 512
QUERY_WIDTH = QUERY_PER_KEY * HEAD_SIZE
KV_WIDTH = 2 * HEAD_SIZE
KEY_CHUNK = KV_WIDTH + LANES
MASKED = -1e30
VMEM_LIMIT = 24 * 1024 * 1024
AXES = ("x", "zh", "zl", "tp")
PART = ("x", "zl")
RING = ("zh", "zl")


def whole(n):
    return [pl.BlockSpec(memory_space=pltpu.VMEM)] * n


def params():
    return pltpu.CompilerParams(vmem_limit_bytes=VMEM_LIMIT)


def cost(flops, moved):
    return pl.CostEstimate(flops=flops, bytes_accessed=moved, transcendentals=0)


def iota(shape, axis):
    return lax.broadcasted_iota(jnp.int32, shape, axis)


def eye(n):
    return iota((n, n), 0) == iota((n, n), 1)


def column_to_row(column):
    n = column.shape[0]
    return jnp.sum(jnp.where(eye(n), column, 0.0), axis=0, keepdims=True)


def split_kernel(target_ref, rows_ref, keys_ref, queries_ref):
    n = rows_ref.shape[0]
    target = jnp.sum(jnp.where(eye(n), target_ref[...], 0), axis=1, keepdims=True)
    lane = iota((n, LANES), 1)
    coded = jnp.where(lane == 0, target >> 8, jnp.where(lane == 1, target & 255, 0))
    queries_ref[0] = rows_ref[:, :QUERY_WIDTH]
    keys_ref[0, :, :KV_WIDTH] = rows_ref[:, QUERY_WIDTH:]
    keys_ref[0, :, KV_WIDTH:] = coded.astype(jnp.float32).astype(jnp.bfloat16)


def split_rows(rows, target, groups):
    n, width = rows.shape
    return pl.pallas_call(
        split_kernel,
        grid=(groups,),
        in_specs=[
            pl.BlockSpec((1, n), lambda g: (0, 0)),
            pl.BlockSpec((n, width // groups), lambda g: (0, g)),
        ],
        out_specs=[
            pl.BlockSpec((1, n, KEY_CHUNK), lambda g: (g, 0, 0)),
            pl.BlockSpec((1, n, QUERY_WIDTH), lambda g: (g, 0, 0)),
        ],
        out_shape=[
            jax.ShapeDtypeStruct((groups, n, KEY_CHUNK), rows.dtype),
            jax.ShapeDtypeStruct((groups, n, QUERY_WIDTH), rows.dtype),
        ],
        compiler_params=params(),
        cost_estimate=cost(0, 2 * rows.size * 2),
        name="split_rows",
    )(target.reshape(1, n), rows)


def sort_kernel(per_pair, chunk_ref, keys_ref, forward_ref, backward_ref):
    n = chunk_ref.shape[0]
    parts, padded, _ = keys_ref.shape
    coded = chunk_ref[:, KV_WIDTH:].astype(jnp.float32)
    column = coded[:, 0:1] * 256.0 + coded[:, 1:2]
    row = column_to_row(column)
    rank_row = jnp.sum(jnp.where(column < row, 1.0, 0.0), axis=0, keepdims=True)
    rank_column = jnp.sum(jnp.where(row < column, 1.0, 0.0), axis=1, keepdims=True)
    down = iota((n, n), 0).astype(jnp.float32)
    across = iota((n, n), 1).astype(jnp.float32)
    forward_ref[...] = jnp.where(rank_row == down, 1.0, 0.0).astype(jnp.bfloat16)
    backward_ref[...] = jnp.where(rank_column == across, 1.0, 0.0).astype(jnp.bfloat16)
    local = jnp.where(coded[:, 0:1] - 2.0 * jnp.floor(coded[:, 0:1] * 0.5) > 0.5, 0.0, -256.0)
    local = local + coded[:, 1:2]
    tile = jnp.where(iota((n, LANES), 1) == 0, local, 0.0).astype(jnp.bfloat16)
    wanted = jnp.concatenate(
        [(iota((padded, n), 0) + (p * (n // parts) - per_pair)) & (n - 1) for p in range(parts)],
        axis=0,
    ).astype(jnp.float32)
    order = jnp.where(rank_row == wanted, 1.0, 0.0).astype(jnp.bfloat16)
    keys = jnp.dot(order, chunk_ref[:, :KV_WIDTH], preferred_element_type=jnp.float32)
    places = jnp.dot(order, tile, preferred_element_type=jnp.float32)
    for p in range(parts):
        rows = slice(p * padded, (p + 1) * padded)
        keys_ref[p, :, :KV_WIDTH] = keys[rows].astype(keys_ref.dtype)
        keys_ref[p, :, KV_WIDTH:] = places[rows].astype(keys_ref.dtype)


def sort_rows(chunk, parts, per_pair):
    n = chunk.shape[0]
    padded = n // parts + per_pair
    return pl.pallas_call(
        functools.partial(sort_kernel, per_pair),
        in_specs=whole(1),
        out_specs=whole(3),
        out_shape=[
            jax.ShapeDtypeStruct((parts, padded, KEY_CHUNK), chunk.dtype),
            jax.ShapeDtypeStruct((n, n), jnp.bfloat16),
            jax.ShapeDtypeStruct((n, n), jnp.bfloat16),
        ],
        compiler_params=params(),
        cost_estimate=cost(2 * n * chunk.size, 4 * chunk.size),
        name="sort_rows",
    )(chunk)


def permute_kernel(order_ref, chunk_ref, out_ref):
    out_ref[...] = jnp.dot(
        order_ref[...], chunk_ref[...], preferred_element_type=jnp.float32
    ).astype(out_ref.dtype)


def permute_rows(order, chunk, name):
    return pl.pallas_call(
        permute_kernel,
        in_specs=whole(2),
        out_specs=pl.BlockSpec(memory_space=pltpu.VMEM),
        out_shape=jax.ShapeDtypeStruct(chunk.shape, chunk.dtype),
        compiler_params=params(),
        cost_estimate=cost(2 * chunk.shape[0] * chunk.size, 4 * chunk.size),
        name=name,
    )(order, chunk)


def arrange_kernel(per_pair, got_ref, load_ref, place_ref):
    sources, padded, _ = got_ref.shape
    blocks = padded // per_pair
    span = sources * per_pair
    pieces = [got_ref[s].astype(jnp.float32) for s in range(sources)]
    places = []
    for b in range(blocks):
        rows = slice(b * per_pair, (b + 1) * per_pair)
        block = jnp.concatenate([piece[rows] for piece in pieces], axis=0)
        load_ref[b * span : (b + 1) * span, :] = block[:, :KV_WIDTH].astype(load_ref.dtype)
        places.append(block[:, KV_WIDTH:])
        place_ref[b * span : (b + 1) * span, :] = places[b]
    rows = jnp.zeros((16, LANES), jnp.float32)
    for b in range(1, blocks):
        pair = jnp.concatenate([places[b - 1], places[b]], axis=0)[:, 0:1]
        rows = jnp.where(iota((16, LANES), 0) == b - 1, column_to_row(pair), rows)
    load_ref[blocks * span :, :LANES] = rows.astype(load_ref.dtype)
    load_ref[blocks * span :, LANES:] = jnp.zeros((16, LANES), load_ref.dtype)


def arrange(got, per_pair):
    sources, padded, _ = got.shape
    rows = sources * padded
    return pl.pallas_call(
        functools.partial(arrange_kernel, per_pair),
        in_specs=whole(1),
        out_specs=whole(2),
        out_shape=[
            jax.ShapeDtypeStruct((rows + 16, KV_WIDTH), got.dtype),
            jax.ShapeDtypeStruct((rows, LANES), jnp.float32),
        ],
        compiler_params=params(),
        cost_estimate=cost(0, 4 * got.size),
        name="arrange",
    )(got)


def attend_kernel(per_pair, loads, starts_ref, place_ref, query_ref, *refs):
    load_refs, (out_ref, key_ref, value_ref, done_ref) = refs[:loads], refs[loads:]
    sources = out_ref.shape[0]
    span = sources * per_pair
    blocks = out_ref.shape[1] // per_pair
    pair = 2 * span
    scale = math.log2(math.e) / math.sqrt(HEAD_SIZE)
    half = float(BLOCK // 2)
    lane = iota((1, pair), 1)
    shift = jnp.where(lane < span, half - BLOCK, half)
    starts = starts_ref[...]
    for b in range(blocks):
        rows = slice(b * span, b * span + pair)
        for at, load_ref in enumerate(load_refs):
            key_ref[at * pair : (at + 1) * pair, :] = load_ref[rows, :HEAD_SIZE]
            value_ref[at * pair : (at + 1) * pair, :] = load_ref[rows, HEAD_SIZE:]
        key_place = jnp.concatenate(
            [
                load_ref[(blocks + 1) * span :, :LANES].astype(jnp.float32)[b : b + 1] + shift
                for load_ref in load_refs
            ],
            axis=1,
        )
        place = place_ref[(b + 1) * span : (b + 2) * span, 0:1] + half
        base = float(b * BLOCK)
        start = jnp.max(
            jnp.where(starts <= place + base, starts, -1e9), axis=1, keepdims=True
        )
        allowed = (key_place >= start - base) & (key_place <= place)
        bias = jnp.where(allowed, 0.0, MASKED)
        query = query_ref[b * span : (b + 1) * span, :]
        query = jnp.concatenate(
            [query[:, h * HEAD_SIZE : (h + 1) * HEAD_SIZE] for h in range(QUERY_PER_KEY)], axis=0
        )
        scores = lax.dot_general(
            query, key_ref[...], (((1,), (1,)), ((), ())), preferred_element_type=jnp.float32
        )
        scores = scores.reshape(QUERY_PER_KEY, span, loads * pair) * scale + bias[None]
        weights = jnp.exp2(scores - jnp.max(scores, axis=2, keepdims=True))
        total = jnp.sum(weights, axis=2, keepdims=True).reshape(QUERY_PER_KEY * span, 1)
        weights = weights.astype(jnp.bfloat16).reshape(QUERY_PER_KEY * span, loads * pair)
        done = jnp.dot(weights, value_ref[...], preferred_element_type=jnp.float32) / total
        for h in range(QUERY_PER_KEY):
            for s in range(sources):
                first = h * span + s * per_pair
                done_ref[
                    s, b * per_pair : (b + 1) * per_pair, h * HEAD_SIZE : (h + 1) * HEAD_SIZE
                ] = done[first : first + per_pair]
    out_ref[...] = done_ref[...].astype(out_ref.dtype)


def attend(starts, places, queries, loads, sources, per_pair):
    n = queries.shape[0]
    keys = len(loads) * 2 * sources * per_pair
    shape = (sources, n // sources, QUERY_WIDTH)
    return pl.pallas_call(
        functools.partial(attend_kernel, per_pair, len(loads)),
        in_specs=whole(3 + len(loads)),
        out_specs=pl.BlockSpec(memory_space=pltpu.VMEM),
        out_shape=jax.ShapeDtypeStruct(shape, queries.dtype),
        scratch_shapes=[
            pltpu.VMEM((keys, HEAD_SIZE), queries.dtype),
            pltpu.VMEM((keys, HEAD_SIZE), queries.dtype),
            pltpu.VMEM(shape, jnp.float32),
        ],
        compiler_params=params(),
        cost_estimate=cost(4 * n * keys * QUERY_WIDTH, 4 * n * QUERY_WIDTH),
        name="attend",
    )(starts, places, queries, *loads)


def exchange(blocks, axis):
    return lax.all_to_all(blocks, axis, split_axis=0, concat_axis=0, tiled=True)


def per_device(section_token_rows, row_target, doc_lengths):
    tp_count = lax.axis_size("tp")
    slabs = lax.axis_size("zh")
    parts = lax.axis_size("x") * lax.axis_size("zl")
    local_rows = section_token_rows.shape[0]
    tok_dev = local_rows * tp_count
    per_pair = tok_dev // (parts * slabs)
    part = lax.axis_index("x") * lax.axis_size("zl") + lax.axis_index("zl")
    starts = (jnp.cumsum(doc_lengths) - doc_lengths - part * (slabs * tok_dev)).reshape(1, -1)
    starts = starts.astype(jnp.float32)

    keys, queries = split_rows(section_token_rows, row_target, tp_count)
    keys = exchange(keys, "tp").reshape(tok_dev, KEY_CHUNK)
    keys, forward, backward = sort_rows(keys, parts, per_pair)
    got = exchange(keys, PART)
    got, queries = lax.optimization_barrier((got, queries))
    load, places = arrange(got, per_pair)

    queries = exchange(queries, "tp").reshape(tok_dev, QUERY_WIDTH)
    queries = permute_rows(forward, queries, "sort_queries")
    queries = exchange(queries.reshape(parts, tok_dev // parts, QUERY_WIDTH), PART)
    queries = queries.reshape(parts, slabs, per_pair, QUERY_WIDTH).transpose(1, 0, 2, 3)
    queries = queries.reshape(tok_dev, QUERY_WIDTH)

    route = []
    for at in range(slabs):
        for low in range(2):
            to = (at + 1 - 2 * low) % slabs
            route.append((at * 2 + low, to * 2 + low))
    loads = [load]
    for _ in range(slabs - 1):
        loads.append(lax.ppermute(loads[-1], RING, route))

    done = attend(starts, places, queries, loads, parts, per_pair)
    back = exchange(done, PART).reshape(tok_dev, QUERY_WIDTH)
    back = permute_rows(backward, back, "unsort").reshape(tp_count, local_rows, QUERY_WIDTH)
    back = exchange(back, "tp")
    return back.transpose(1, 0, 2).reshape(local_rows, tp_count * QUERY_WIDTH)


def solution(mesh):
    shape = (4, 8, 2, mesh.shape["tp"])
    ring_mesh = Mesh(mesh.devices.reshape(shape), AXES)
    placed = (P(AXES, None), P(AXES), P())
    return jax.shard_map(
        per_device, mesh=ring_mesh, in_specs=placed, out_specs=P(AXES, None), check_vma=False
    )
```

time: 219 us -> 176 us (0.80)
  blocking collectives: 28.7 us -> 77.4 us
  waiting for transfers between devices: 112 us -> 64.1 us
  starting transfers between devices: 55.6 us -> 19.9 us
  Pallas kernels: 19 us -> 9.02 us
  local copies, waits for them, and re-layouts: 1.95 us -> 4.64 us
    all_to_all x6 -> x1, waiting for transfers between devices: 74.2 us -> 0.01 us  [exchange(): return lax.all_to_all(blocks, axis, split_axis=0, concat_axis=0, tiled=True)]
    all_to_all x2 -> x5, blocking collectives: 28.7 us -> 77.4 us  [exchange(): return lax.all_to_all(blocks, axis, split_axis=0, concat_axis=0, tiled=True)]
    all_to_all x6 -> x1, starting transfers between devices: 52.7 us -> 4.2 us  [exchange(): return lax.all_to_all(blocks, axis, split_axis=0, concat_axis=0, tiled=True)]
    ppermute x1 -> x7, waiting for transfers between devices: 37.9 us -> 64.1 us  [per_device(): loads.append(lax.ppermute(loads[-1], RING, route))]
    ppermute x1 -> x7, starting transfers between devices: 2.92 us -> 15.7 us  [per_device(): loads.append(lax.ppermute(loads[-1], RING, route))]
    pallas_call x4 -> x3, Pallas kernels: 13.4 us -> 6.04 us  [the longest x1 4.86 us: attend(): pl.pallas_call(functools.partial(attend_kernel, per_pair, len(loads)), in...]
  transfers between devices with their start and end apart: 7 -> 8, of which waited for: 6 -> 7; matrix products, arithmetic and copies ran while one was open for 0% -> 1% of each run, Pallas kernels for 4% -> 0%
where the time goes in v3:
time: 176 us
  blocking collectives  77.4 us (44%)
  waiting for transfers between devices  64.1 us (36%)
  starting transfers between devices  19.9 us (11%)
  Pallas kernels  9.02 us (5%)
  local copies, waits for them, and re-layouts  4.64 us (3%)
    all_to_all x5, blocking collectives, exchange(): return lax.all_to_all(blocks, axis, split_axis=0, concat_axis=0, tiled=True)  77.4 us
    ppermute x7, waiting for transfers between devices, per_device(): loads.append(lax.ppermute(loads[-1], RING, route))  64.1 us
    ppermute x7, starting transfers between devices, per_device(): loads.append(lax.ppermute(loads[-1], RING, route))  15.7 us
    pallas_call x1, Pallas kernels, attend(): pl.pallas_call(functools.partial(attend_kernel, per_pair, len(loads)), in...  4.86 us
    all_to_all x1, starting transfers between devices, exchange(): return lax.all_to_all(blocks, axis, split_axis=0, concat_axis=0, tiled=True)  4.2 us
  transfers between devices with their start and end apart: 8, of which 7 were waited for; matrix products, arithmetic and copies ran while one was open for 1% of the time, Pallas kernels for 0%

profile of v3, /device:TPU:1, one launch (start us, length us, event | category | flops | bytes accessed | tf_op | source)
XLA Modules:
  0.0 175.5 jit_solution(12484276337926771904)
XLA Ops:
  0.7 1.2 copy-done
  2.8 17.3 %all_to_all.30 = bf16[8,64,384]{2,1,0:T(8,128)(2,1)S(1)} all-to-all(bf16[8,64,384]{2,1,0:T(8,128)(2,1)S(1)} %get-tuple-element.14), channel_id=1, replica_groups=mesh['x'=4,'zh'=8,'zl'=2,'tp'=8] {'tp'}, dimensions={0} | all-to-all | bytes 786432 | tf_op jit(solution)/shard_map/all_to_all | solution.py:257
  21.1 10.5 %all_to_all.31.got_ref = bf16[8,72,384]{2,1,0:T(8,128)(2,1)S(1)} all-to-all(bf16[8,72,384]{2,1,0:T(8,128)(2,1)S(1)} %get-tuple-element.16), channel_id=1, replica_groups=mesh['x'=4,'zh'=8,'zl'=2,'tp'=8] {'x','zl'}, dimensions={0} | all-to-all | bytes 884736 | tf_op jit(solution)/shard_map/all_to_all | solution.py:257
  31.7 15.3 %all_to_all.32 = bf16[8,64,640]{2,1,0:T(8,128)(2,1)S(1)} all-to-all(bf16[8,64,640]{2,1,0:T(8,128)(2,1)S(1)} %get-tuple-element.21), channel_id=1, replica_groups=mesh['x'=4,'zh'=8,'zl'=2,'tp'=8] {'tp'}, dimensions={0} | all-to-all | bytes 1310720 | tf_op jit(solution)/shard_map/all_to_all | solution.py:257
  47.0 1.4 sort_queries.1
  48.4 4.2 %all-to-all-start.3 = ((bf16[8,64,640]{2,1,0:T(8,128)(2,1)}), bf16[8,64,640]{2,1,0:T(8,128)(2,1)}, u32[]{:S(2)}, u32[]{:S(2)}) async-start(bf16[8,64,640]{2,1,0:T(8,128)(2,1)} %bitcast.5), calls=%async_computation.3 | async-start | bytes 1310720 | tf_op jit(solution)/shard_map/all_to_all | solution.py:257
  52.8 4.2 %collective-permute-start = (bf16[592,256]{1,0:T(8,128)(2,1)S(1)}, bf16[592,256]{1,0:T(8,128)(2,1)S(1)}, u32[]{:S(2)}, u32[]{:S(2)}) collective-permute-start(bf16[592,256]{1,0:T(8,128)(2,1)S(1)} %get-tuple-element.22.refs_0_), channel_id=1, source_target_pairs={{0,16},{8,120},{16,32},{24,8},{32,48},{40,24},{48,64},{56,40},{64,... | collective-permute-start | bytes 909320 | tf_op jit(solution)/shard_map/ppermute | solution.py:291
  57.0 17.5 %collective-permute-done.refs_1_ = bf16[592,256]{1,0:T(8,128)(2,1)S(1)} collective-permute-done((bf16[592,256]{1,0:T(8,128)(2,1)S(1)}, bf16[592,256]{1,0:T(8,128)(2,1)S(1)}, u32[]{:S(2)}, u32[]{:S(2)}) %collective-permute-start) | collective-permute-done | bytes 303136 | tf_op jit(solution)/shard_map/ppermute | solution.py:291
  74.6 1.9 %collective-permute-start.1 = (bf16[592,256]{1,0:T(8,128)(2,1)S(1)}, bf16[592,256]{1,0:T(8,128)(2,1)S(1)}, u32[]{:S(2)}, u32[]{:S(2)}) collective-permute-start(bf16[592,256]{1,0:T(8,128)(2,1)S(1)} %collective-permute-done.refs_1_), channel_id=1, source_target_pairs={{0,16},{8,120},{16,32},{24,8},{32,48},{40,24},{48,64},{56,40},{64,... | collective-permute-start | bytes 909320 | tf_op jit(solution)/shard_map/ppermute | solution.py:291
  76.5 9.4 %collective-permute-done.1.refs_2_ = bf16[592,256]{1,0:T(8,128)(2,1)S(1)} collective-permute-done((bf16[592,256]{1,0:T(8,128)(2,1)S(1)}, bf16[592,256]{1,0:T(8,128)(2,1)S(1)}, u32[]{:S(2)}, u32[]{:S(2)}) %collective-permute-start.1) | collective-permute-done | bytes 303136 | tf_op jit(solution)/shard_map/ppermute | solution.py:291
  85.9 1.9 %collective-permute-start.2 = (bf16[592,256]{1,0:T(8,128)(2,1)S(1)}, bf16[592,256]{1,0:T(8,128)(2,1)S(1)}, u32[]{:S(2)}, u32[]{:S(2)}) collective-permute-start(bf16[592,256]{1,0:T(8,128)(2,1)S(1)} %collective-permute-done.1.refs_2_), channel_id=1, source_target_pairs={{0,16},{8,120},{16,32},{24,8},{32,48},{40,24},{48,64},{56,40},{64,... | collective-permute-start | bytes 909320 | tf_op jit(solution)/shard_map/ppermute | solution.py:291
  87.8 8.5 %collective-permute-done.2.refs_3_ = bf16[592,256]{1,0:T(8,128)(2,1)S(1)} collective-permute-done((bf16[592,256]{1,0:T(8,128)(2,1)S(1)}, bf16[592,256]{1,0:T(8,128)(2,1)S(1)}, u32[]{:S(2)}, u32[]{:S(2)}) %collective-permute-start.2) | collective-permute-done | bytes 303136 | tf_op jit(solution)/shard_map/ppermute | solution.py:291
  96.3 1.9 %collective-permute-start.3 = (bf16[592,256]{1,0:T(8,128)(2,1)S(1)}, bf16[592,256]{1,0:T(8,128)(2,1)S(1)}, u32[]{:S(2)}, u32[]{:S(2)}) collective-permute-start(bf16[592,256]{1,0:T(8,128)(2,1)S(1)} %collective-permute-done.2.refs_3_), channel_id=1, source_target_pairs={{0,16},{8,120},{16,32},{24,8},{32,48},{40,24},{48,64},{56,40},{64,... | collective-permute-start | bytes 909320 | tf_op jit(solution)/shard_map/ppermute | solution.py:291
  98.2 7.7 %collective-permute-done.3.refs_4_ = bf16[592,256]{1,0:T(8,128)(2,1)S(1)} collective-permute-done((bf16[592,256]{1,0:T(8,128)(2,1)S(1)}, bf16[592,256]{1,0:T(8,128)(2,1)S(1)}, u32[]{:S(2)}, u32[]{:S(2)}) %collective-permute-start.3) | collective-permute-done | bytes 303136 | tf_op jit(solution)/shard_map/ppermute | solution.py:291
  105.9 1.9 %collective-permute-start.4 = (bf16[592,256]{1,0:T(8,128)(2,1)S(1)}, bf16[592,256]{1,0:T(8,128)(2,1)S(1)}, u32[]{:S(2)}, u32[]{:S(2)}) collective-permute-start(bf16[592,256]{1,0:T(8,128)(2,1)S(1)} %collective-permute-done.3.refs_4_), channel_id=1, source_target_pairs={{0,16},{8,120},{16,32},{24,8},{32,48},{40,24},{48,64},{56,40},{64,... | collective-permute-start | bytes 909320 | tf_op jit(solution)/shard_map/ppermute | solution.py:291
  107.9 7.7 %collective-permute-done.4.refs_5_ = bf16[592,256]{1,0:T(8,128)(2,1)S(1)} collective-permute-done((bf16[592,256]{1,0:T(8,128)(2,1)S(1)}, bf16[592,256]{1,0:T(8,128)(2,1)S(1)}, u32[]{:S(2)}, u32[]{:S(2)}) %collective-permute-start.4) | collective-permute-done | bytes 303136 | tf_op jit(solution)/shard_map/ppermute | solution.py:291
  115.6 1.9 %collective-permute-start.5 = (bf16[592,256]{1,0:T(8,128)(2,1)S(1)}, bf16[592,256]{1,0:T(8,128)(2,1)S(1)}, u32[]{:S(2)}, u32[]{:S(2)}) collective-permute-start(bf16[592,256]{1,0:T(8,128)(2,1)S(1)} %collective-permute-done.4.refs_5_), channel_id=1, source_target_pairs={{0,16},{8,120},{16,32},{24,8},{32,48},{40,24},{48,64},{56,40},{64,... | collective-permute-start | bytes 909320 | tf_op jit(solution)/shard_map/ppermute | solution.py:291
  117.5 7.7 %collective-permute-done.5.refs_6_ = bf16[592,256]{1,0:T(8,128)(2,1)S(1)} collective-permute-done((bf16[592,256]{1,0:T(8,128)(2,1)S(1)}, bf16[592,256]{1,0:T(8,128)(2,1)S(1)}, u32[]{:S(2)}, u32[]{:S(2)}) %collective-permute-start.5) | collective-permute-done | bytes 303136 | tf_op jit(solution)/shard_map/ppermute | solution.py:291
  125.3 1.9 %collective-permute-start.6 = (bf16[592,256]{1,0:T(8,128)(2,1)S(1)}, bf16[592,256]{1,0:T(8,128)(2,1)S(1)}, u32[]{:S(2)}, u32[]{:S(2)}) collective-permute-start(bf16[592,256]{1,0:T(8,128)(2,1)S(1)} %collective-permute-done.5.refs_6_), channel_id=1, source_target_pairs={{0,16},{8,120},{16,32},{24,8},{32,48},{40,24},{48,64},{56,40},{64,... | collective-permute-start | bytes 909320 | tf_op jit(solution)/shard_map/ppermute | solution.py:291
  128.3 1.1 copy.7
  129.4 5.5 %collective-permute-done.6.refs_7_ = bf16[592,256]{1,0:T(8,128)(2,1)S(1)} collective-permute-done((bf16[592,256]{1,0:T(8,128)(2,1)S(1)}, bf16[592,256]{1,0:T(8,128)(2,1)S(1)}, u32[]{:S(2)}, u32[]{:S(2)}) %collective-permute-start.6) | collective-permute-done | bytes 303136 | tf_op jit(solution)/shard_map/ppermute | solution.py:291
  134.9 4.9 %attend.1 = bf16[8,64,640]{2,1,0:T(8,128)(2,1)S(1)} custom-call(f32[1,128]{1,0:T(1,128)S(1)} %convert_bitcast_fusion.starts_ref, f32[576,128]{1,0:T(8,128)S(1)} %get-tuple-element.19.place_ref, bf16[512,640]{1,0:T(8,128)(2,1)S(1)} %bitcast.19, bf16[592,256]{1,0:T(8,128)(2,1)S(1)} %get-tuple-element.22.refs_0_, ...), custom_call_target="tpu_custom_call" | custom-call | flops 1342177280 | bytes 1310720 | tf_op jit(solution)/shard_map/attend/pallas_call | solution.py:240
  139.8 11.5 %all_to_all.33 = bf16[8,64,640]{2,1,0:T(8,128)(2,1)S(1)} all-to-all(bf16[8,64,640]{2,1,0:T(8,128)(2,1)S(1)} %attend.1), channel_id=1, replica_groups=mesh['x'=4,'zh'=8,'zl'=2,'tp'=8] {'x','zl'}, dimensions={0} | all-to-all | bytes 1310720 | tf_op jit(solution)/shard_map/all_to_all | solution.py:257
  151.9 22.8 %all_to_all.34 = bf16[8,64,640]{2,1,0:T(8,128)(2,1)S(1)} all-to-all(bf16[8,64,640]{2,1,0:T(8,128)(2,1)S(1)} %bitcast.18), channel_id=1, replica_groups=mesh['x'=4,'zh'=8,'zl'=2,'tp'=8] {'tp'}, dimensions={0} | all-to-all | bytes 1310720 | tf_op jit(solution)/shard_map/all_to_all | solution.py:257
  (15 shorter events, 5.3 us)
Async XLA Ops:
  0.0 0.7 copy-start.1
  0.7 1.2 copy-start
  48.4 79.8 %all-to-all-start.3 = ((bf16[8,64,640]{2,1,0:T(8,128)(2,1)}), bf16[8,64,640]{2,1,0:T(8,128)(2,1)}, u32[]{:S(2)}, u32[]{:S(2)}) async-start(bf16[8,64,640]{2,1,0:T(8,128)(2,1)} %bitcast.5), calls=%async_computation.3 | async-start | bytes 1310720 | tf_op jit(solution)/shard_map/all_to_all | solution.py:257
  52.8 21.8 %collective-permute-start = (bf16[592,256]{1,0:T(8,128)(2,1)S(1)}, bf16[592,256]{1,0:T(8,128)(2,1)S(1)}, u32[]{:S(2)}, u32[]{:S(2)}) collective-permute-start(bf16[592,256]{1,0:T(8,128)(2,1)S(1)} %get-tuple-element.22.refs_0_), channel_id=1, source_target_pairs={{0,16},{8,120},{16,32},{24,8},{32,48},{40,24},{48,64},{56,40},{64,... | collective-permute-start | bytes 909320 | tf_op jit(solution)/shard_map/ppermute | solution.py:291
  74.6 11.3 %collective-permute-start.1 = (bf16[592,256]{1,0:T(8,128)(2,1)S(1)}, bf16[592,256]{1,0:T(8,128)(2,1)S(1)}, u32[]{:S(2)}, u32[]{:S(2)}) collective-permute-start(bf16[592,256]{1,0:T(8,128)(2,1)S(1)} %collective-permute-done.refs_1_), channel_id=1, source_target_pairs={{0,16},{8,120},{16,32},{24,8},{32,48},{40,24},{48,64},{56,40},{64,... | collective-permute-start | bytes 909320 | tf_op jit(solution)/shard_map/ppermute | solution.py:291
  85.9 10.4 %collective-permute-start.2 = (bf16[592,256]{1,0:T(8,128)(2,1)S(1)}, bf16[592,256]{1,0:T(8,128)(2,1)S(1)}, u32[]{:S(2)}, u32[]{:S(2)}) collective-permute-start(bf16[592,256]{1,0:T(8,128)(2,1)S(1)} %collective-permute-done.1.refs_2_), channel_id=1, source_target_pairs={{0,16},{8,120},{16,32},{24,8},{32,48},{40,24},{48,64},{56,40},{64,... | collective-permute-start | bytes 909320 | tf_op jit(solution)/shard_map/ppermute | solution.py:291
  96.3 9.7 %collective-permute-start.3 = (bf16[592,256]{1,0:T(8,128)(2,1)S(1)}, bf16[592,256]{1,0:T(8,128)(2,1)S(1)}, u32[]{:S(2)}, u32[]{:S(2)}) collective-permute-start(bf16[592,256]{1,0:T(8,128)(2,1)S(1)} %collective-permute-done.2.refs_3_), channel_id=1, source_target_pairs={{0,16},{8,120},{16,32},{24,8},{32,48},{40,24},{48,64},{56,40},{64,... | collective-permute-start | bytes 909320 | tf_op jit(solution)/shard_map/ppermute | solution.py:291
  105.9 9.7 %collective-permute-start.4 = (bf16[592,256]{1,0:T(8,128)(2,1)S(1)}, bf16[592,256]{1,0:T(8,128)(2,1)S(1)}, u32[]{:S(2)}, u32[]{:S(2)}) collective-permute-start(bf16[592,256]{1,0:T(8,128)(2,1)S(1)} %collective-permute-done.3.refs_4_), channel_id=1, source_target_pairs={{0,16},{8,120},{16,32},{24,8},{32,48},{40,24},{48,64},{56,40},{64,... | collective-permute-start | bytes 909320 | tf_op jit(solution)/shard_map/ppermute | solution.py:291
  115.6 9.7 %collective-permute-start.5 = (bf16[592,256]{1,0:T(8,128)(2,1)S(1)}, bf16[592,256]{1,0:T(8,128)(2,1)S(1)}, u32[]{:S(2)}, u32[]{:S(2)}) collective-permute-start(bf16[592,256]{1,0:T(8,128)(2,1)S(1)} %collective-permute-done.4.refs_5_), channel_id=1, source_target_pairs={{0,16},{8,120},{16,32},{24,8},{32,48},{40,24},{48,64},{56,40},{64,... | collective-permute-start | bytes 909320 | tf_op jit(solution)/shard_map/ppermute | solution.py:291
  125.3 9.7 %collective-permute-start.6 = (bf16[592,256]{1,0:T(8,128)(2,1)S(1)}, bf16[592,256]{1,0:T(8,128)(2,1)S(1)}, u32[]{:S(2)}, u32[]{:S(2)}) collective-permute-start(bf16[592,256]{1,0:T(8,128)(2,1)S(1)} %collective-permute-done.5.refs_6_), channel_id=1, source_target_pairs={{0,16},{8,120},{16,32},{24,8},{32,48},{40,24},{48,64},{56,40},{64,... | collective-permute-start | bytes 909320 | tf_op jit(solution)/shard_map/ppermute | solution.py:291
  127.2 0.7 copy-start.2

commit v4 on v3

--- a/solution.py
+++ b/solution.py
@@ -21,6 +21,7 @@
 AXES = ("x", "zh", "zl", "tp")
 PART = ("x", "zl")
 RING = ("zh", "zl")
+MEETINGS = (3, 6)
 
 
 def whole(n):
@@ -145,7 +146,7 @@
     )(order, chunk)
 
 
-def arrange_kernel(per_pair, got_ref, load_ref, place_ref):
+def arrange_kernel(per_pair, got_ref, key_ref, value_ref, place_ref):
     sources, padded, _ = got_ref.shape
     blocks = padded // per_pair
     span = sources * per_pair
@@ -154,15 +155,16 @@
     for b in range(blocks):
         rows = slice(b * per_pair, (b + 1) * per_pair)
         block = jnp.concatenate([piece[rows] for piece in pieces], axis=0)
-        load_ref[b * span : (b + 1) * span, :] = block[:, :KV_WIDTH].astype(load_ref.dtype)
+        at = slice(b * span, (b + 1) * span)
+        key_ref[at, :] = block[:, :HEAD_SIZE].astype(key_ref.dtype)
+        value_ref[at, :] = block[:, HEAD_SIZE:KV_WIDTH].astype(value_ref.dtype)
         places.append(block[:, KV_WIDTH:])
-        place_ref[b * span : (b + 1) * span, :] = places[b]
+        place_ref[at, :] = places[b]
     rows = jnp.zeros((16, LANES), jnp.float32)
     for b in range(1, blocks):
         pair = jnp.concatenate([places[b - 1], places[b]], axis=0)[:, 0:1]
         rows = jnp.where(iota((16, LANES), 0) == b - 1, column_to_row(pair), rows)
-    load_ref[blocks * span :, :LANES] = rows.astype(load_ref.dtype)
-    load_ref[blocks * span :, LANES:] = jnp.zeros((16, LANES), load_ref.dtype)
+    key_ref[blocks * span :, :] = rows.astype(key_ref.dtype)
 
 
 def arrange(got, per_pair):
@@ -171,9 +173,10 @@
     return pl.pallas_call(
         functools.partial(arrange_kernel, per_pair),
         in_specs=whole(1),
-        out_specs=whole(2),
+        out_specs=whole(3),
         out_shape=[
-            jax.ShapeDtypeStruct((rows + 16, KV_WIDTH), got.dtype),
+            jax.ShapeDtypeStruct((rows + 16, HEAD_SIZE), got.dtype),
+            jax.ShapeDtypeStruct((rows, HEAD_SIZE), got.dtype),
             jax.ShapeDtypeStruct((rows, LANES), jnp.float32),
         ],
         compiler_params=params(),
@@ -183,7 +186,8 @@
 
 
 def attend_kernel(per_pair, loads, starts_ref, place_ref, query_ref, *refs):
-    load_refs, (out_ref, key_ref, value_ref, done_ref) = refs[:loads], refs[loads:]
+    load_refs, value_refs = refs[:loads], refs[loads : 2 * loads]
+    out_ref, key_ref, value_ref, done_ref = refs[2 * loads :]
     sources = out_ref.shape[0]
     span = sources * per_pair
     blocks = out_ref.shape[1] // per_pair
@@ -195,12 +199,12 @@
     starts = starts_ref[...]
     for b in range(blocks):
         rows = slice(b * span, b * span + pair)
-        for at, load_ref in enumerate(load_refs):
-            key_ref[at * pair : (at + 1) * pair, :] = load_ref[rows, :HEAD_SIZE]
-            value_ref[at * pair : (at + 1) * pair, :] = load_ref[rows, HEAD_SIZE:]
+        for at in range(loads):
+            key_ref[at * pair : (at + 1) * pair, :] = load_refs[at][rows, :]
+            value_ref[at * pair : (at + 1) * pair, :] = value_refs[at][rows, :]
         key_place = jnp.concatenate(
             [
-                load_ref[(blocks + 1) * span :, :LANES].astype(jnp.float32)[b : b + 1] + shift
+                load_ref[(blocks + 1) * span :, :].astype(jnp.float32)[b : b + 1] + shift
                 for load_ref in load_refs
             ],
             axis=1,
@@ -233,13 +237,13 @@
     out_ref[...] = done_ref[...].astype(out_ref.dtype)
 
 
-def attend(starts, places, queries, loads, sources, per_pair):
+def attend(starts, places, queries, loads, values, sources, per_pair):
     n = queries.shape[0]
     keys = len(loads) * 2 * sources * per_pair
     shape = (sources, n // sources, QUERY_WIDTH)
     return pl.pallas_call(
         functools.partial(attend_kernel, per_pair, len(loads)),
-        in_specs=whole(3 + len(loads)),
+        in_specs=whole(3 + 2 * len(loads)),
         out_specs=pl.BlockSpec(memory_space=pltpu.VMEM),
         out_shape=jax.ShapeDtypeStruct(shape, queries.dtype),
         scratch_shapes=[
@@ -250,7 +254,7 @@
         compiler_params=params(),
         cost_estimate=cost(4 * n * keys * QUERY_WIDTH, 4 * n * QUERY_WIDTH),
         name="attend",
-    )(starts, places, queries, *loads)
+    )(starts, places, queries, *loads, *values)
 
 
 def exchange(blocks, axis):
@@ -271,26 +275,30 @@
     keys, queries = split_rows(section_token_rows, row_target, tp_count)
     keys = exchange(keys, "tp").reshape(tok_dev, KEY_CHUNK)
     keys, forward, backward = sort_rows(keys, parts, per_pair)
-    got = exchange(keys, PART)
-    got, queries = lax.optimization_barrier((got, queries))
-    load, places = arrange(got, per_pair)
-
-    queries = exchange(queries, "tp").reshape(tok_dev, QUERY_WIDTH)
-    queries = permute_rows(forward, queries, "sort_queries")
-    queries = exchange(queries.reshape(parts, tok_dev // parts, QUERY_WIDTH), PART)
-    queries = queries.reshape(parts, slabs, per_pair, QUERY_WIDTH).transpose(1, 0, 2, 3)
-    queries = queries.reshape(tok_dev, QUERY_WIDTH)
+    load, value, places = arrange(exchange(keys, PART), per_pair)
+    load, value, queries = lax.optimization_barrier((load, value, queries))
 
     route = []
     for at in range(slabs):
         for low in range(2):
             to = (at + 1 - 2 * low) % slabs
             route.append((at * 2 + low, to * 2 + low))
-    loads = [load]
-    for _ in range(slabs - 1):
+    loads, values = [load], [value]
+    queries = exchange(queries, "tp").reshape(tok_dev, QUERY_WIDTH)
+    for step in range(1, slabs):
         loads.append(lax.ppermute(loads[-1], RING, route))
-
-    done = attend(starts, places, queries, loads, parts, per_pair)
+        values.append(lax.ppermute(values[-1], RING, route))
+        if step in MEETINGS:
+            loads[-1], values[-1], queries = lax.optimization_barrier(
+                (loads[-1], values[-1], queries)
+            )
+        if step == MEETINGS[0]:
+            queries = permute_rows(forward, queries, "sort_queries")
+            queries = exchange(queries.reshape(parts, tok_dev // parts, QUERY_WIDTH), PART)
+    queries = queries.reshape(parts, slabs, per_pair, QUERY_WIDTH).transpose(1, 0, 2, 3)
+    queries = queries.reshape(tok_dev, QUERY_WIDTH)
+
+    done = attend(starts, places, queries, loads, values, parts, per_pair)
     back = exchange(done, PART).reshape(tok_dev, QUERY_WIDTH)
     back = permute_rows(backward, back, "unsort").reshape(tp_count, local_rows, QUERY_WIDTH)
     back = exchange(back, "tp")

time: 176 us -> 166 us (0.943)
  starting transfers between devices: 19.9 us -> 56.1 us
  waiting for transfers between devices: 64.1 us -> 28.3 us
  blocking collectives: 77.4 us -> 65.3 us
    ppermute x7, waiting for transfers between devices: 64.1 us -> 14.1 us  [per_device(): loads.append(lax.ppermute(loads[-1], RING, route))]
    ppermute x0 -> x7, starting transfers between devices: none -> 27 us  [per_device(): values.append(lax.ppermute(values[-1], RING, route))]
    ppermute x0 -> x7, waiting for transfers between devices: none -> 14.2 us  [per_device(): values.append(lax.ppermute(values[-1], RING, route))]
    all_to_all x5 -> x4, blocking collectives: 77.4 us -> 65.3 us  [exchange(): return lax.all_to_all(blocks, axis, split_axis=0, concat_axis=0, tiled=True)]
    all_to_all x1 -> x2, starting transfers between devices: 4.2 us -> 9.73 us  [exchange(): return lax.all_to_all(blocks, axis, split_axis=0, concat_axis=0, tiled=True)]
    ppermute x7, starting transfers between devices: 15.7 us -> 19.4 us  [per_device(): loads.append(lax.ppermute(loads[-1], RING, route))]
    pallas_call x1, Pallas kernels: 1 us -> 2.78 us  [split_rows(): pl.pallas_call(split_kernel, grid=(groups,), in_specs=[pl.BlockSpec((1, n...]
  transfers between devices with their start and end apart: 8 -> 16, of which waited for: 7 -> 11; matrix products, arithmetic and copies ran while one was open for 1% -> 1% of each run, Pallas kernels for 0% -> 0%
where the time goes in v4:
time: 166 us; the launch traced here: 165 us
  blocking collectives  65.3 us (39%)
  starting transfers between devices  56.1 us (34%)
  waiting for transfers between devices  28.3 us (17%)
  Pallas kernels  10.5 us (6%)
  local copies, waits for them, and re-layouts  4.64 us (3%)
    all_to_all x4, blocking collectives, exchange(): return lax.all_to_all(blocks, axis, split_axis=0, concat_axis=0, tiled=True)  65.3 us
    ppermute x7, starting transfers between devices, per_device(): values.append(lax.ppermute(values[-1], RING, route))  27 us
    ppermute x7, starting transfers between devices, per_device(): loads.append(lax.ppermute(loads[-1], RING, route))  19.4 us
    ppermute x7, waiting for transfers between devices, per_device(): values.append(lax.ppermute(values[-1], RING, route))  14.2 us
    ppermute x7, waiting for transfers between devices, per_device(): loads.append(lax.ppermute(loads[-1], RING, route))  14.1 us
    all_to_all x2, starting transfers between devices, exchange(): return lax.all_to_all(blocks, axis, split_axis=0, concat_axis=0, tiled=True)  9.73 us
    pallas_call x1, Pallas kernels, attend(): pl.pallas_call(functools.partial(attend_kernel, per_pair, len(loads)), in...  4.53 us
  transfers between devices with their start and end apart: 16, of which 11 were waited for; matrix products, arithmetic and copies ran while one was open for 1% of the time, Pallas kernels for 0%

profile of v4, /device:TPU:1, one launch (start us, length us, event | category | flops | bytes accessed | tf_op | source)
XLA Modules:
  0.0 165.3 jit_solution(4849308695628943761)
XLA Ops:
  1.8 2.8 %split_rows.1 = (bf16[8,64,384]{2,1,0:T(8,128)(2,1)S(1)}, bf16[8,64,640]{2,1,0:T(8,128)(2,1)}) custom-call(s32[1,64]{1,0:T(1,128)S(1)} %bitcast.21, bf16[64,7168]{1,0:T(8,128)(2,1)S(1)} %copy-done), custom_call_target="tpu_custom_call" | custom-call | bytes 1835008 | tf_op jit(solution)/shard_map/split_rows/pallas_call | solution.py:64
  4.6 17.3 %all_to_all.30 = bf16[8,64,384]{2,1,0:T(8,128)(2,1)S(1)} all-to-all(bf16[8,64,384]{2,1,0:T(8,128)(2,1)S(1)} %get-tuple-element.22), channel_id=1, replica_groups=mesh['x'=4,'zh'=8,'zl'=2,'tp'=8] {'tp'}, dimensions={0} | all-to-all | bytes 786432 | tf_op jit(solution)/shard_map/all_to_all | solution.py:261
  22.9 10.5 %all_to_all.31.got_ref = bf16[8,72,384]{2,1,0:T(8,128)(2,1)S(1)} all-to-all(bf16[8,72,384]{2,1,0:T(8,128)(2,1)S(1)} %get-tuple-element.24), channel_id=1, replica_groups=mesh['x'=4,'zh'=8,'zl'=2,'tp'=8] {'x','zl'}, dimensions={0} | all-to-all | bytes 884736 | tf_op jit(solution)/shard_map/all_to_all | solution.py:261
  33.6 5.5 %all-to-all-start.2 = ((bf16[8,64,640]{2,1,0:T(8,128)(2,1)}), bf16[8,64,640]{2,1,0:T(8,128)(2,1)S(1)}, u32[]{:S(2)}, u32[]{:S(2)}) async-start(bf16[8,64,640]{2,1,0:T(8,128)(2,1)} %get-tuple-element.31), calls=%async_computation.2 | async-start | bytes 1310720 | tf_op jit(solution)/shard_map/all_to_all | solution.py:261
  39.1 4.2 %collective-permute-start = (bf16[592,128]{1,0:T(8,128)(2,1)S(1)}, bf16[592,128]{1,0:T(8,128)(2,1)S(1)}, u32[]{:S(2)}, u32[]{:S(2)}) collective-permute-start(bf16[592,128]{1,0:T(8,128)(2,1)S(1)} %get-tuple-element.29.refs_0_), channel_id=1, source_target_pairs={{0,16},{8,120},{16,32},{24,8},{32,48},{40,24},{48,64},{56,40},{64,... | collective-permute-start | bytes 454664 | tf_op jit(solution)/shard_map/ppermute | solution.py:289
  43.3 6.1 %collective-permute-start.3 = (bf16[576,128]{1,0:T(8,128)(2,1)S(1)}, bf16[576,128]{1,0:T(8,128)(2,1)S(1)}, u32[]{:S(2)}, u32[]{:S(2)}) collective-permute-start(bf16[576,128]{1,0:T(8,128)(2,1)S(1)} %get-tuple-element.30.refs_8_), channel_id=1, source_target_pairs={{0,16},{8,120},{16,32},{24,8},{32,48},{40,24},{48,64},{56,40},{64,... | collective-permute-start | bytes 442376 | tf_op jit(solution)/shard_map/ppermute | solution.py:290
  49.4 3.8 %collective-permute-done.refs_1_ = bf16[592,128]{1,0:T(8,128)(2,1)S(1)} collective-permute-done((bf16[592,128]{1,0:T(8,128)(2,1)S(1)}, bf16[592,128]{1,0:T(8,128)(2,1)S(1)}, u32[]{:S(2)}, u32[]{:S(2)}) %collective-permute-start) | collective-permute-done | bytes 151584 | tf_op jit(solution)/shard_map/ppermute | solution.py:289
  56.4 3.1 %collective-permute-start.4 = (bf16[576,128]{1,0:T(8,128)(2,1)S(1)}, bf16[576,128]{1,0:T(8,128)(2,1)S(1)}, u32[]{:S(2)}, u32[]{:S(2)}) collective-permute-start(bf16[576,128]{1,0:T(8,128)(2,1)S(1)} %collective-permute-done.3.refs_9_), channel_id=1, source_target_pairs={{0,16},{8,120},{16,32},{24,8},{32,48},{40,24},{48,64},{56,40},{64,... | collective-permute-start | bytes 442376 | tf_op jit(solution)/shard_map/ppermute | solution.py:290
  59.6 2.2 %collective-permute-done.1.refs_2_ = bf16[592,128]{1,0:T(8,128)(2,1)S(1)} collective-permute-done((bf16[592,128]{1,0:T(8,128)(2,1)S(1)}, bf16[592,128]{1,0:T(8,128)(2,1)S(1)}, u32[]{:S(2)}, u32[]{:S(2)}) %collective-permute-start.1) | collective-permute-done | bytes 151584 | tf_op jit(solution)/shard_map/ppermute | solution.py:289
  65.3 3.6 %collective-permute-start.5 = (bf16[576,128]{1,0:T(8,128)(2,1)S(1)}, bf16[576,128]{1,0:T(8,128)(2,1)S(1)}, u32[]{:S(2)}, u32[]{:S(2)}) collective-permute-start(bf16[576,128]{1,0:T(8,128)(2,1)S(1)} %collective-permute-done.4.refs_10_), channel_id=1, source_target_pairs={{0,16},{8,120},{16,32},{24,8},{32,48},{40,24},{48,64},{56,40},{64,... | collective-permute-start | bytes 442376 | tf_op jit(solution)/shard_map/ppermute | solution.py:290
  69.0 5.2 %collective-permute-done.5.refs_11_ = bf16[576,128]{1,0:T(8,128)(2,1)S(1)} collective-permute-done((bf16[576,128]{1,0:T(8,128)(2,1)S(1)}, bf16[576,128]{1,0:T(8,128)(2,1)S(1)}, u32[]{:S(2)}, u32[]{:S(2)}) %collective-permute-start.5) | collective-permute-done | bytes 147488 | tf_op jit(solution)/shard_map/ppermute | solution.py:290
  75.6 4.2 %all-to-all-start.3 = ((bf16[8,64,640]{2,1,0:T(8,128)(2,1)}), bf16[8,64,640]{2,1,0:T(8,128)(2,1)}, u32[]{:S(2)}, u32[]{:S(2)}) async-start(bf16[8,64,640]{2,1,0:T(8,128)(2,1)} %bitcast.5), calls=%async_computation.3 | async-start | bytes 1310720 | tf_op jit(solution)/shard_map/all_to_all | solution.py:261
  81.8 5.0 %collective-permute-start.9 = (bf16[576,128]{1,0:T(8,128)(2,1)S(1)}, bf16[576,128]{1,0:T(8,128)(2,1)S(1)}, u32[]{:S(2)}, u32[]{:S(2)}) collective-permute-start(bf16[576,128]{1,0:T(8,128)(2,1)S(1)} %collective-permute-done.5.refs_11_), channel_id=1, source_target_pairs={{0,16},{8,120},{16,32},{24,8},{32,48},{40,24},{48,64},{56,40},{64,... | collective-permute-start | bytes 442376 | tf_op jit(solution)/shard_map/ppermute | solution.py:290
  86.7 4.2 %collective-permute-done.6.refs_4_ = bf16[592,128]{1,0:T(8,128)(2,1)S(1)} collective-permute-done((bf16[592,128]{1,0:T(8,128)(2,1)S(1)}, bf16[592,128]{1,0:T(8,128)(2,1)S(1)}, u32[]{:S(2)}, u32[]{:S(2)}) %collective-permute-start.6) | collective-permute-done | bytes 151584 | tf_op jit(solution)/shard_map/ppermute | solution.py:289
  91.0 2.5 %collective-permute-start.7 = (bf16[592,128]{1,0:T(8,128)(2,1)S(1)}, bf16[592,128]{1,0:T(8,128)(2,1)S(1)}, u32[]{:S(2)}, u32[]{:S(2)}) collective-permute-start(bf16[592,128]{1,0:T(8,128)(2,1)S(1)} %collective-permute-done.6.refs_4_), channel_id=1, source_target_pairs={{0,16},{8,120},{16,32},{24,8},{32,48},{40,24},{48,64},{56,40},{64,... | collective-permute-start | bytes 454664 | tf_op jit(solution)/shard_map/ppermute | solution.py:289
  94.2 2.7 %collective-permute-start.10 = (bf16[576,128]{1,0:T(8,128)(2,1)S(1)}, bf16[576,128]{1,0:T(8,128)(2,1)S(1)}, u32[]{:S(2)}, u32[]{:S(2)}) collective-permute-start(bf16[576,128]{1,0:T(8,128)(2,1)S(1)} %collective-permute-done.9.refs_12_), channel_id=1, source_target_pairs={{0,16},{8,120},{16,32},{24,8},{32,48},{40,24},{48,64},{56,40},{64,... | collective-permute-start | bytes 442376 | tf_op jit(solution)/shard_map/ppermute | solution.py:290
  97.0 2.0 %collective-permute-done.7.refs_5_ = bf16[592,128]{1,0:T(8,128)(2,1)S(1)} collective-permute-done((bf16[592,128]{1,0:T(8,128)(2,1)S(1)}, bf16[592,128]{1,0:T(8,128)(2,1)S(1)}, u32[]{:S(2)}, u32[]{:S(2)}) %collective-permute-start.7) | collective-permute-done | bytes 151584 | tf_op jit(solution)/shard_map/ppermute | solution.py:289
  102.6 3.2 %collective-permute-start.11 = (bf16[576,128]{1,0:T(8,128)(2,1)S(1)}, bf16[576,128]{1,0:T(8,128)(2,1)S(1)}, u32[]{:S(2)}, u32[]{:S(2)}) collective-permute-start(bf16[576,128]{1,0:T(8,128)(2,1)S(1)} %collective-permute-done.10.refs_13_), channel_id=1, source_target_pairs={{0,16},{8,120},{16,32},{24,8},{32,48},{40,24},{48,64},{56,40},{64,... | collective-permute-start | bytes 442376 | tf_op jit(solution)/shard_map/ppermute | solution.py:290
  106.9 3.7 %collective-permute-done.11.refs_14_ = bf16[576,128]{1,0:T(8,128)(2,1)S(1)} collective-permute-done((bf16[576,128]{1,0:T(8,128)(2,1)S(1)}, bf16[576,128]{1,0:T(8,128)(2,1)S(1)}, u32[]{:S(2)}, u32[]{:S(2)}) %collective-permute-start.11) | collective-permute-done | bytes 147488 | tf_op jit(solution)/shard_map/ppermute | solution.py:290
  110.6 3.1 %collective-permute-start.13 = (bf16[576,128]{1,0:T(8,128)(2,1)S(1)}, bf16[576,128]{1,0:T(8,128)(2,1)S(1)}, u32[]{:S(2)}, u32[]{:S(2)}) collective-permute-start(bf16[576,128]{1,0:T(8,128)(2,1)S(1)} %collective-permute-done.11.refs_14_), channel_id=1, source_target_pairs={{0,16},{8,120},{16,32},{24,8},{32,48},{40,24},{48,64},{56,40},{64,... | collective-permute-start | bytes 442376 | tf_op jit(solution)/shard_map/ppermute | solution.py:290
  113.7 5.0 %collective-permute-start.12 = (bf16[592,128]{1,0:T(8,128)(2,1)S(1)}, bf16[592,128]{1,0:T(8,128)(2,1)S(1)}, u32[]{:S(2)}, u32[]{:S(2)}) collective-permute-start(bf16[592,128]{1,0:T(8,128)(2,1)S(1)} %collective-permute-done.8.refs_6_), channel_id=1, source_target_pairs={{0,16},{8,120},{16,32},{24,8},{32,48},{40,24},{48,64},{56,40},{64,... | collective-permute-start | bytes 454664 | tf_op jit(solution)/shard_map/ppermute | solution.py:289
  121.8 4.5 %attend.1 = bf16[8,64,640]{2,1,0:T(8,128)(2,1)S(1)} custom-call(f32[1,128]{1,0:T(1,128)S(1)} %convert_bitcast_fusion.starts_ref, f32[576,128]{1,0:T(8,128)S(1)} %get-tuple-element.25.place_ref, bf16[512,640]{1,0:T(8,128)(2,1)S(1)} %bitcast.19, bf16[592,128]{1,0:T(8,128)(2,1)S(1)} %get-tuple-element.29.refs_0_, ...), custom_call_target="tpu_custom_call" | custom-call | flops 1342177280 | bytes 1310720 | tf_op jit(solution)/shard_map/attend/pallas_call | solution.py:244
  126.3 13.5 %all_to_all.32 = bf16[8,64,640]{2,1,0:T(8,128)(2,1)S(1)} all-to-all(bf16[8,64,640]{2,1,0:T(8,128)(2,1)S(1)} %attend.1), channel_id=1, replica_groups=mesh['x'=4,'zh'=8,'zl'=2,'tp'=8] {'x','zl'}, dimensions={0} | all-to-all | bytes 1310720 | tf_op jit(solution)/shard_map/all_to_all | solution.py:261
  140.4 23.9 %all_to_all.33 = bf16[8,64,640]{2,1,0:T(8,128)(2,1)S(1)} all-to-all(bf16[8,64,640]{2,1,0:T(8,128)(2,1)S(1)} %bitcast.18), channel_id=1, replica_groups=mesh['x'=4,'zh'=8,'zl'=2,'tp'=8] {'tp'}, dimensions={0} | all-to-all | bytes 1310720 | tf_op jit(solution)/shard_map/all_to_all | solution.py:261
  (30 shorter events, 22.9 us)
Async XLA Ops:
  0.0 0.7 copy-start.1
  0.7 1.2 copy-start
  33.6 40.6 %all-to-all-start.2 = ((bf16[8,64,640]{2,1,0:T(8,128)(2,1)}), bf16[8,64,640]{2,1,0:T(8,128)(2,1)S(1)}, u32[]{:S(2)}, u32[]{:S(2)}) async-start(bf16[8,64,640]{2,1,0:T(8,128)(2,1)} %get-tuple-element.31), calls=%async_computation.2 | async-start | bytes 1310720 | tf_op jit(solution)/shard_map/all_to_all | solution.py:261
  39.1 14.2 %collective-permute-start = (bf16[592,128]{1,0:T(8,128)(2,1)S(1)}, bf16[592,128]{1,0:T(8,128)(2,1)S(1)}, u32[]{:S(2)}, u32[]{:S(2)}) collective-permute-start(bf16[592,128]{1,0:T(8,128)(2,1)S(1)} %get-tuple-element.29.refs_0_), channel_id=1, source_target_pairs={{0,16},{8,120},{16,32},{24,8},{32,48},{40,24},{48,64},{56,40},{64,... | collective-permute-start | bytes 454664 | tf_op jit(solution)/shard_map/ppermute | solution.py:289
  43.3 13.1 %collective-permute-start.3 = (bf16[576,128]{1,0:T(8,128)(2,1)S(1)}, bf16[576,128]{1,0:T(8,128)(2,1)S(1)}, u32[]{:S(2)}, u32[]{:S(2)}) collective-permute-start(bf16[576,128]{1,0:T(8,128)(2,1)S(1)} %get-tuple-element.30.refs_8_), channel_id=1, source_target_pairs={{0,16},{8,120},{16,32},{24,8},{32,48},{40,24},{48,64},{56,40},{64,... | collective-permute-start | bytes 442376 | tf_op jit(solution)/shard_map/ppermute | solution.py:290
  53.3 8.5 %collective-permute-start.1 = (bf16[592,128]{1,0:T(8,128)(2,1)S(1)}, bf16[592,128]{1,0:T(8,128)(2,1)S(1)}, u32[]{:S(2)}, u32[]{:S(2)}) collective-permute-start(bf16[592,128]{1,0:T(8,128)(2,1)S(1)} %collective-permute-done.refs_1_), channel_id=1, source_target_pairs={{0,16},{8,120},{16,32},{24,8},{32,48},{40,24},{48,64},{56,40},{64,... | collective-permute-start | bytes 454664 | tf_op jit(solution)/shard_map/ppermute | solution.py:289
  56.4 8.9 %collective-permute-start.4 = (bf16[576,128]{1,0:T(8,128)(2,1)S(1)}, bf16[576,128]{1,0:T(8,128)(2,1)S(1)}, u32[]{:S(2)}, u32[]{:S(2)}) collective-permute-start(bf16[576,128]{1,0:T(8,128)(2,1)S(1)} %collective-permute-done.3.refs_9_), channel_id=1, source_target_pairs={{0,16},{8,120},{16,32},{24,8},{32,48},{40,24},{48,64},{56,40},{64,... | collective-permute-start | bytes 442376 | tf_op jit(solution)/shard_map/ppermute | solution.py:290
  61.8 12.4 %collective-permute-start.2 = (bf16[592,128]{1,0:T(8,128)(2,1)S(1)}, bf16[592,128]{1,0:T(8,128)(2,1)S(1)}, u32[]{:S(2)}, u32[]{:S(2)}) collective-permute-start(bf16[592,128]{1,0:T(8,128)(2,1)S(1)} %collective-permute-done.1.refs_2_), channel_id=1, source_target_pairs={{0,16},{8,120},{16,32},{24,8},{32,48},{40,24},{48,64},{56,40},{64,... | collective-permute-start | bytes 454664 | tf_op jit(solution)/shard_map/ppermute | solution.py:289
  65.3 8.9 %collective-permute-start.5 = (bf16[576,128]{1,0:T(8,128)(2,1)S(1)}, bf16[576,128]{1,0:T(8,128)(2,1)S(1)}, u32[]{:S(2)}, u32[]{:S(2)}) collective-permute-start(bf16[576,128]{1,0:T(8,128)(2,1)S(1)} %collective-permute-done.4.refs_10_), channel_id=1, source_target_pairs={{0,16},{8,120},{16,32},{24,8},{32,48},{40,24},{48,64},{56,40},{64,... | collective-permute-start | bytes 442376 | tf_op jit(solution)/shard_map/ppermute | solution.py:290
  75.6 35.0 %all-to-all-start.3 = ((bf16[8,64,640]{2,1,0:T(8,128)(2,1)}), bf16[8,64,640]{2,1,0:T(8,128)(2,1)}, u32[]{:S(2)}, u32[]{:S(2)}) async-start(bf16[8,64,640]{2,1,0:T(8,128)(2,1)} %bitcast.5), calls=%async_computation.3 | async-start | bytes 1310720 | tf_op jit(solution)/shard_map/all_to_all | solution.py:261
  79.8 11.1 %collective-permute-start.6 = (bf16[592,128]{1,0:T(8,128)(2,1)S(1)}, bf16[592,128]{1,0:T(8,128)(2,1)S(1)}, u32[]{:S(2)}, u32[]{:S(2)}) collective-permute-start(bf16[592,128]{1,0:T(8,128)(2,1)S(1)} %collective-permute-done.2.refs_3_), channel_id=1, source_target_pairs={{0,16},{8,120},{16,32},{24,8},{32,48},{40,24},{48,64},{56,40},{64,... | collective-permute-start | bytes 454664 | tf_op jit(solution)/shard_map/ppermute | solution.py:289
  81.8 12.5 %collective-permute-start.9 = (bf16[576,128]{1,0:T(8,128)(2,1)S(1)}, bf16[576,128]{1,0:T(8,128)(2,1)S(1)}, u32[]{:S(2)}, u32[]{:S(2)}) collective-permute-start(bf16[576,128]{1,0:T(8,128)(2,1)S(1)} %collective-permute-done.5.refs_11_), channel_id=1, source_target_pairs={{0,16},{8,120},{16,32},{24,8},{32,48},{40,24},{48,64},{56,40},{64,... | collective-permute-start | bytes 442376 | tf_op jit(solution)/shard_map/ppermute | solution.py:290
  91.0 8.0 %collective-permute-start.7 = (bf16[592,128]{1,0:T(8,128)(2,1)S(1)}, bf16[592,128]{1,0:T(8,128)(2,1)S(1)}, u32[]{:S(2)}, u32[]{:S(2)}) collective-permute-start(bf16[592,128]{1,0:T(8,128)(2,1)S(1)} %collective-permute-done.6.refs_4_), channel_id=1, source_target_pairs={{0,16},{8,120},{16,32},{24,8},{32,48},{40,24},{48,64},{56,40},{64,... | collective-permute-start | bytes 454664 | tf_op jit(solution)/shard_map/ppermute | solution.py:289
  94.2 8.4 %collective-permute-start.10 = (bf16[576,128]{1,0:T(8,128)(2,1)S(1)}, bf16[576,128]{1,0:T(8,128)(2,1)S(1)}, u32[]{:S(2)}, u32[]{:S(2)}) collective-permute-start(bf16[576,128]{1,0:T(8,128)(2,1)S(1)} %collective-permute-done.9.refs_12_), channel_id=1, source_target_pairs={{0,16},{8,120},{16,32},{24,8},{32,48},{40,24},{48,64},{56,40},{64,... | collective-permute-start | bytes 442376 | tf_op jit(solution)/shard_map/ppermute | solution.py:290
  99.0 11.6 %collective-permute-start.8 = (bf16[592,128]{1,0:T(8,128)(2,1)S(1)}, bf16[592,128]{1,0:T(8,128)(2,1)S(1)}, u32[]{:S(2)}, u32[]{:S(2)}) collective-permute-start(bf16[592,128]{1,0:T(8,128)(2,1)S(1)} %collective-permute-done.7.refs_5_), channel_id=1, source_target_pairs={{0,16},{8,120},{16,32},{24,8},{32,48},{40,24},{48,64},{56,40},{64,... | collective-permute-start | bytes 454664 | tf_op jit(solution)/shard_map/ppermute | solution.py:289
  102.6 8.0 %collective-permute-start.11 = (bf16[576,128]{1,0:T(8,128)(2,1)S(1)}, bf16[576,128]{1,0:T(8,128)(2,1)S(1)}, u32[]{:S(2)}, u32[]{:S(2)}) collective-permute-start(bf16[576,128]{1,0:T(8,128)(2,1)S(1)} %collective-permute-done.10.refs_13_), channel_id=1, source_target_pairs={{0,16},{8,120},{16,32},{24,8},{32,48},{40,24},{48,64},{56,40},{64,... | collective-permute-start | bytes 442376 | tf_op jit(solution)/shard_map/ppermute | solution.py:290
  105.9 0.7 copy-start.2
  110.6 9.3 %collective-permute-start.13 = (bf16[576,128]{1,0:T(8,128)(2,1)S(1)}, bf16[576,128]{1,0:T(8,128)(2,1)S(1)}, u32[]{:S(2)}, u32[]{:S(2)}) collective-permute-start(bf16[576,128]{1,0:T(8,128)(2,1)S(1)} %collective-permute-done.11.refs_14_), channel_id=1, source_target_pairs={{0,16},{8,120},{16,32},{24,8},{32,48},{40,24},{48,64},{56,40},{64,... | collective-permute-start | bytes 442376 | tf_op jit(solution)/shard_map/ppermute | solution.py:290
  113.7 8.0 %collective-permute-start.12 = (bf16[592,128]{1,0:T(8,128)(2,1)S(1)}, bf16[592,128]{1,0:T(8,128)(2,1)S(1)}, u32[]{:S(2)}, u32[]{:S(2)}) collective-permute-start(bf16[592,128]{1,0:T(8,128)(2,1)S(1)} %collective-permute-done.8.refs_6_), channel_id=1, source_target_pairs={{0,16},{8,120},{16,32},{24,8},{32,48},{40,24},{48,64},{56,40},{64,... | collective-permute-start | bytes 454664 | tf_op jit(solution)/shard_map/ppermute | solution.py:289

commit v5 on v4

--- a/solution.py
+++ b/solution.py
@@ -21,7 +21,7 @@
 AXES = ("x", "zh", "zl", "tp")
 PART = ("x", "zl")
 RING = ("zh", "zl")
-MEETINGS = (3, 6)
+MEETINGS = (1, 3)
 
 
 def whole(n):
@@ -49,37 +49,51 @@
     return jnp.sum(jnp.where(eye(n), column, 0.0), axis=0, keepdims=True)
 
 
-def split_kernel(target_ref, rows_ref, keys_ref, queries_ref):
-    n = rows_ref.shape[0]
+def split_keys_kernel(target_ref, key_ref, value_ref, out_ref):
+    n = key_ref.shape[0]
     target = jnp.sum(jnp.where(eye(n), target_ref[...], 0), axis=1, keepdims=True)
     lane = iota((n, LANES), 1)
     coded = jnp.where(lane == 0, target >> 8, jnp.where(lane == 1, target & 255, 0))
-    queries_ref[0] = rows_ref[:, :QUERY_WIDTH]
-    keys_ref[0, :, :KV_WIDTH] = rows_ref[:, QUERY_WIDTH:]
-    keys_ref[0, :, KV_WIDTH:] = coded.astype(jnp.float32).astype(jnp.bfloat16)
-
-
-def split_rows(rows, target, groups):
-    n, width = rows.shape
-    return pl.pallas_call(
-        split_kernel,
+    out_ref[0, :, :HEAD_SIZE] = key_ref[...]
+    out_ref[0, :, HEAD_SIZE:KV_WIDTH] = value_ref[...]
+    out_ref[0, :, KV_WIDTH:] = coded.astype(jnp.float32).astype(jnp.bfloat16)
+
+
+def split_keys(rows, target, groups):
+    n = rows.shape[0]
+    heads = QUERY_PER_KEY + 2
+    return pl.pallas_call(
+        split_keys_kernel,
         grid=(groups,),
         in_specs=[
             pl.BlockSpec((1, n), lambda g: (0, 0)),
-            pl.BlockSpec((n, width // groups), lambda g: (0, g)),
+            pl.BlockSpec((n, HEAD_SIZE), lambda g: (0, heads * g + QUERY_PER_KEY)),
+            pl.BlockSpec((n, HEAD_SIZE), lambda g: (0, heads * g + QUERY_PER_KEY + 1)),
         ],
-        out_specs=[
-            pl.BlockSpec((1, n, KEY_CHUNK), lambda g: (g, 0, 0)),
-            pl.BlockSpec((1, n, QUERY_WIDTH), lambda g: (g, 0, 0)),
-        ],
-        out_shape=[
-            jax.ShapeDtypeStruct((groups, n, KEY_CHUNK), rows.dtype),
-            jax.ShapeDtypeStruct((groups, n, QUERY_WIDTH), rows.dtype),
-        ],
-        compiler_params=params(),
-        cost_estimate=cost(0, 2 * rows.size * 2),
-        name="split_rows",
-    )(target.reshape(1, n), rows)
+        out_specs=pl.BlockSpec((1, n, KEY_CHUNK), lambda g: (g, 0, 0)),
+        out_shape=jax.ShapeDtypeStruct((groups, n, KEY_CHUNK), rows.dtype),
+        compiler_params=params(),
+        cost_estimate=cost(0, 4 * groups * n * KEY_CHUNK),
+        name="split_keys",
+    )(target.reshape(1, n), rows, rows)
+
+
+def split_queries_kernel(rows_ref, out_ref):
+    out_ref[0] = rows_ref[:, :QUERY_WIDTH]
+
+
+def split_queries(rows, groups):
+    n, width = rows.shape
+    return pl.pallas_call(
+        split_queries_kernel,
+        grid=(groups,),
+        in_specs=[pl.BlockSpec((n, width // groups), lambda g: (0, g))],
+        out_specs=pl.BlockSpec((1, n, QUERY_WIDTH), lambda g: (g, 0, 0)),
+        out_shape=jax.ShapeDtypeStruct((groups, n, QUERY_WIDTH), rows.dtype),
+        compiler_params=params(),
+        cost_estimate=cost(0, 4 * rows.size),
+        name="split_queries",
+    )(rows)
 
 
 def sort_kernel(per_pair, chunk_ref, keys_ref, forward_ref, backward_ref):
@@ -272,29 +286,38 @@
     starts = (jnp.cumsum(doc_lengths) - doc_lengths - part * (slabs * tok_dev)).reshape(1, -1)
     starts = starts.astype(jnp.float32)
 
-    keys, queries = split_rows(section_token_rows, row_target, tp_count)
+    keys = split_keys(section_token_rows, row_target, tp_count)
     keys = exchange(keys, "tp").reshape(tok_dev, KEY_CHUNK)
     keys, forward, backward = sort_rows(keys, parts, per_pair)
     load, value, places = arrange(exchange(keys, PART), per_pair)
-    load, value, queries = lax.optimization_barrier((load, value, queries))
-
-    route = []
-    for at in range(slabs):
-        for low in range(2):
-            to = (at + 1 - 2 * low) % slabs
-            route.append((at * 2 + low, to * 2 + low))
+    load, value, rows = lax.optimization_barrier((load, value, section_token_rows))
+    queries = exchange(split_queries(rows, tp_count), "tp").reshape(tok_dev, QUERY_WIDTH)
+
+    def passed(block, sign):
+        route = []
+        for at in range(slabs):
+            for low in range(2):
+                to = (at + sign * (1 - 2 * low)) % slabs
+                route.append((at * 2 + low, to * 2 + low))
+        return lax.ppermute(block, RING, route)
+
     loads, values = [load], [value]
-    queries = exchange(queries, "tp").reshape(tok_dev, QUERY_WIDTH)
-    for step in range(1, slabs):
-        loads.append(lax.ppermute(loads[-1], RING, route))
-        values.append(lax.ppermute(values[-1], RING, route))
+    load_a, load_b, value_a, value_b = load, load, value, value
+    for step in range(1, slabs // 2):
+        load_a = passed(load_a, 1)
+        load_b = passed(load_b, -1)
+        value_a, value_b = passed(value_a, 1), passed(value_b, -1)
         if step in MEETINGS:
-            loads[-1], values[-1], queries = lax.optimization_barrier(
-                (loads[-1], values[-1], queries)
+            load_a, load_b, value_a, value_b, queries = lax.optimization_barrier(
+                (load_a, load_b, value_a, value_b, queries)
             )
         if step == MEETINGS[0]:
             queries = permute_rows(forward, queries, "sort_queries")
             queries = exchange(queries.reshape(parts, tok_dev // parts, QUERY_WIDTH), PART)
+        loads += [load_a, load_b]
+        values += [value_a, value_b]
+    loads.append(passed(load_a, 1))
+    values.append(passed(value_b, -1))
     queries = queries.reshape(parts, slabs, per_pair, QUERY_WIDTH).transpose(1, 0, 2, 3)
     queries = queries.reshape(tok_dev, QUERY_WIDTH)
 

time: 166 us -> 163 us (0.982)
  waiting for transfers between devices: 28.3 us -> 17.1 us
  starting transfers between devices: 56.1 us -> 66.2 us
  blocking collectives: 65.3 us -> 61.8 us
    ppermute x14, waiting for transfers between devices: 28.3 us -> 17.1 us  [passed(): return lax.ppermute(block, RING, route)]
    ppermute x14, starting transfers between devices: 46.3 us -> 56.5 us  [passed(): return lax.ppermute(block, RING, route)]
    all_to_all x4, blocking collectives: 65.3 us -> 61.8 us  [exchange(): return lax.all_to_all(blocks, axis, split_axis=0, concat_axis=0, tiled=True)]
    pallas_call x1 -> x2, Pallas kernels: 2.78 us -> 3.72 us  [the longest x1 2.68 us: split_queries(): pl.pallas_call(split_queries_kernel, grid=(groups,), in_specs=[pl.BlockSp...]
  transfers between devices with their start and end apart: 16 -> 16, of which waited for: 11 -> 6; matrix products, arithmetic and copies ran while one was open for 1% -> 1% of each run, Pallas kernels for 0% -> 0%
where the time goes in v5:
time: 163 us; the launch traced here: 162 us
  starting transfers between devices  66.2 us (41%)
  blocking collectives  61.8 us (38%)
  waiting for transfers between devices  17.1 us (10%)
  Pallas kernels  11.5 us (7%)
  local copies, waits for them, and re-layouts  4.65 us (3%)
    all_to_all x4, blocking collectives, exchange(): return lax.all_to_all(blocks, axis, split_axis=0, concat_axis=0, tiled=True)  61.8 us
    ppermute x14, starting transfers between devices, passed(): return lax.ppermute(block, RING, route)  56.5 us
    ppermute x14, waiting for transfers between devices, passed(): return lax.ppermute(block, RING, route)  17.1 us
    all_to_all x2, starting transfers between devices, exchange(): return lax.all_to_all(blocks, axis, split_axis=0, concat_axis=0, tiled=True)  9.72 us
    pallas_call x1, Pallas kernels, attend(): pl.pallas_call(functools.partial(attend_kernel, per_pair, len(loads)), in...  4.61 us
  transfers between devices with their start and end apart: 16, of which 6 were waited for; matrix products, arithmetic and copies ran while one was open for 1% of the time, Pallas kernels for 0%

profile of v5, /device:TPU:1, one launch (start us, length us, event | category | flops | bytes accessed | tf_op | source)
XLA Modules:
  0.0 161.8 jit_solution(16317780463627193446)
XLA Ops:
  2.9 17.3 %all_to_all.30 = bf16[8,64,384]{2,1,0:T(8,128)(2,1)S(1)} all-to-all(bf16[8,64,384]{2,1,0:T(8,128)(2,1)S(1)} %split_keys.1), channel_id=1, replica_groups=mesh['x'=4,'zh'=8,'zl'=2,'tp'=8] {'tp'}, dimensions={0} | all-to-all | bytes 786432 | tf_op jit(solution)/shard_map/all_to_all | solution.py:275
  21.2 10.5 %all_to_all.31.got_ref = bf16[8,72,384]{2,1,0:T(8,128)(2,1)S(1)} all-to-all(bf16[8,72,384]{2,1,0:T(8,128)(2,1)S(1)} %get-tuple-element.25), channel_id=1, replica_groups=mesh['x'=4,'zh'=8,'zl'=2,'tp'=8] {'x','zl'}, dimensions={0} | all-to-all | bytes 884736 | tf_op jit(solution)/shard_map/all_to_all | solution.py:275
  31.9 2.7 %split_queries.1 = bf16[8,64,640]{2,1,0:T(8,128)(2,1)} custom-call(bf16[64,7168]{1,0:T(8,128)(2,1)S(1)} %copy-done.1), custom_call_target="tpu_custom_call" | custom-call | bytes 1835008 | tf_op jit(solution)/shard_map/split_queries/pallas_call | solution.py:87
  34.6 5.5 %all-to-all-start.2 = ((bf16[8,64,640]{2,1,0:T(8,128)(2,1)}), bf16[8,64,640]{2,1,0:T(8,128)(2,1)S(1)}, u32[]{:S(2)}, u32[]{:S(2)}) async-start(bf16[8,64,640]{2,1,0:T(8,128)(2,1)} %split_queries.1), calls=%async_computation.2 | async-start | bytes 1310720 | tf_op jit(solution)/shard_map/all_to_all | solution.py:275
  40.1 10.0 %collective-permute-start.1 = (bf16[592,128]{1,0:T(8,128)(2,1)S(1)}, bf16[592,128]{1,0:T(8,128)(2,1)S(1)}, u32[]{:S(2)}, u32[]{:S(2)}) collective-permute-start(bf16[592,128]{1,0:T(8,128)(2,1)S(1)} %get-tuple-element.29.refs_0_), channel_id=1, source_target_pairs={{0,112},{8,24},{16,0},{24,40},{32,16},{40,56},{48,32},{56,72},{64,... | collective-permute-start | bytes 454664 | tf_op jit(solution)/shard_map/ppermute | solution.py:302
  50.0 1.9 %collective-permute-start = (bf16[592,128]{1,0:T(8,128)(2,1)S(1)}, bf16[592,128]{1,0:T(8,128)(2,1)S(1)}, u32[]{:S(2)}, u32[]{:S(2)}) collective-permute-start(bf16[592,128]{1,0:T(8,128)(2,1)S(1)} %get-tuple-element.29.refs_0_), channel_id=1, source_target_pairs={{0,16},{8,120},{16,32},{24,8},{32,48},{40,24},{48,64},{56,40},{64,... | collective-permute-start | bytes 454664 | tf_op jit(solution)/shard_map/ppermute | solution.py:302
  52.0 5.5 %collective-permute-start.3 = (bf16[576,128]{1,0:T(8,128)(2,1)S(1)}, bf16[576,128]{1,0:T(8,128)(2,1)S(1)}, u32[]{:S(2)}, u32[]{:S(2)}) collective-permute-start(bf16[576,128]{1,0:T(8,128)(2,1)S(1)} %get-tuple-element.30.refs_8_), channel_id=1, source_target_pairs={{0,112},{8,24},{16,0},{24,40},{32,16},{40,56},{48,32},{56,72},{64,... | collective-permute-start | bytes 442376 | tf_op jit(solution)/shard_map/ppermute | solution.py:302
  57.4 1.9 %collective-permute-start.2 = (bf16[576,128]{1,0:T(8,128)(2,1)S(1)}, bf16[576,128]{1,0:T(8,128)(2,1)S(1)}, u32[]{:S(2)}, u32[]{:S(2)}) collective-permute-start(bf16[576,128]{1,0:T(8,128)(2,1)S(1)} %get-tuple-element.30.refs_8_), channel_id=1, source_target_pairs={{0,16},{8,120},{16,32},{24,8},{32,48},{40,24},{48,64},{56,40},{64,... | collective-permute-start | bytes 442376 | tf_op jit(solution)/shard_map/ppermute | solution.py:302
  60.0 6.6 %collective-permute-done.2.refs_9_ = bf16[576,128]{1,0:T(8,128)(2,1)S(1)} collective-permute-done((bf16[576,128]{1,0:T(8,128)(2,1)S(1)}, bf16[576,128]{1,0:T(8,128)(2,1)S(1)}, u32[]{:S(2)}, u32[]{:S(2)}) %collective-permute-start.2) | collective-permute-done | bytes 147488 | tf_op jit(solution)/shard_map/ppermute | solution.py:302
  67.9 4.2 %all-to-all-start.3 = ((bf16[8,64,640]{2,1,0:T(8,128)(2,1)}), bf16[8,64,640]{2,1,0:T(8,128)(2,1)}, u32[]{:S(2)}, u32[]{:S(2)}) async-start(bf16[8,64,640]{2,1,0:T(8,128)(2,1)} %bitcast.5), calls=%async_computation.3 | async-start | bytes 1310720 | tf_op jit(solution)/shard_map/all_to_all | solution.py:275
  72.2 3.7 %collective-permute-start.4 = (bf16[592,128]{1,0:T(8,128)(2,1)S(1)}, bf16[592,128]{1,0:T(8,128)(2,1)S(1)}, u32[]{:S(2)}, u32[]{:S(2)}) collective-permute-start(bf16[592,128]{1,0:T(8,128)(2,1)S(1)} %collective-permute-done.refs_1_), channel_id=1, source_target_pairs={{0,16},{8,120},{16,32},{24,8},{32,48},{40,24},{48,64},{56,40},{64,... | collective-permute-start | bytes 454664 | tf_op jit(solution)/shard_map/ppermute | solution.py:302
  75.9 3.7 %collective-permute-start.6 = (bf16[592,128]{1,0:T(8,128)(2,1)S(1)}, bf16[592,128]{1,0:T(8,128)(2,1)S(1)}, u32[]{:S(2)}, u32[]{:S(2)}) collective-permute-start(bf16[592,128]{1,0:T(8,128)(2,1)S(1)} %collective-permute-done.1.refs_2_), channel_id=1, source_target_pairs={{0,112},{8,24},{16,0},{24,40},{32,16},{40,56},{48,32},{56,72},{64,... | collective-permute-start | bytes 454664 | tf_op jit(solution)/shard_map/ppermute | solution.py:302
  79.6 2.5 %collective-permute-start.8 = (bf16[576,128]{1,0:T(8,128)(2,1)S(1)}, bf16[576,128]{1,0:T(8,128)(2,1)S(1)}, u32[]{:S(2)}, u32[]{:S(2)}) collective-permute-start(bf16[576,128]{1,0:T(8,128)(2,1)S(1)} %collective-permute-done.2.refs_9_), channel_id=1, source_target_pairs={{0,16},{8,120},{16,32},{24,8},{32,48},{40,24},{48,64},{56,40},{64,... | collective-permute-start | bytes 442376 | tf_op jit(solution)/shard_map/ppermute | solution.py:302
  82.1 4.9 %collective-permute-start.10 = (bf16[576,128]{1,0:T(8,128)(2,1)S(1)}, bf16[576,128]{1,0:T(8,128)(2,1)S(1)}, u32[]{:S(2)}, u32[]{:S(2)}) collective-permute-start(bf16[576,128]{1,0:T(8,128)(2,1)S(1)} %collective-permute-done.3.refs_10_), channel_id=1, source_target_pairs={{0,112},{8,24},{16,0},{24,40},{32,16},{40,56},{48,32},{56,72},{64,... | collective-permute-start | bytes 442376 | tf_op jit(solution)/shard_map/ppermute | solution.py:302
  90.3 5.5 %collective-permute-start.7 = (bf16[592,128]{1,0:T(8,128)(2,1)S(1)}, bf16[592,128]{1,0:T(8,128)(2,1)S(1)}, u32[]{:S(2)}, u32[]{:S(2)}) collective-permute-start(bf16[592,128]{1,0:T(8,128)(2,1)S(1)} %collective-permute-done.6.refs_4_), channel_id=1, source_target_pairs={{0,112},{8,24},{16,0},{24,40},{32,16},{40,56},{48,32},{56,72},{64,... | collective-permute-start | bytes 454664 | tf_op jit(solution)/shard_map/ppermute | solution.py:302
  95.8 1.9 %collective-permute-start.9 = (bf16[576,128]{1,0:T(8,128)(2,1)S(1)}, bf16[576,128]{1,0:T(8,128)(2,1)S(1)}, u32[]{:S(2)}, u32[]{:S(2)}) collective-permute-start(bf16[576,128]{1,0:T(8,128)(2,1)S(1)} %collective-permute-done.8.refs_11_), channel_id=1, source_target_pairs={{0,16},{8,120},{16,32},{24,8},{32,48},{40,24},{48,64},{56,40},{64,... | collective-permute-start | bytes 442376 | tf_op jit(solution)/shard_map/ppermute | solution.py:302
  97.8 5.5 %collective-permute-start.11 = (bf16[576,128]{1,0:T(8,128)(2,1)S(1)}, bf16[576,128]{1,0:T(8,128)(2,1)S(1)}, u32[]{:S(2)}, u32[]{:S(2)}) collective-permute-start(bf16[576,128]{1,0:T(8,128)(2,1)S(1)} %collective-permute-done.10.refs_12_), channel_id=1, source_target_pairs={{0,112},{8,24},{16,0},{24,40},{32,16},{40,56},{48,32},{56,72},{64,... | collective-permute-start | bytes 442376 | tf_op jit(solution)/shard_map/ppermute | solution.py:302
  104.6 3.8 %collective-permute-done.11.refs_14_ = bf16[576,128]{1,0:T(8,128)(2,1)S(1)} collective-permute-done((bf16[576,128]{1,0:T(8,128)(2,1)S(1)}, bf16[576,128]{1,0:T(8,128)(2,1)S(1)}, u32[]{:S(2)}, u32[]{:S(2)}) %collective-permute-start.11) | collective-permute-done | bytes 147488 | tf_op jit(solution)/shard_map/ppermute | solution.py:302
  108.4 4.4 %collective-permute-start.13 = (bf16[576,128]{1,0:T(8,128)(2,1)S(1)}, bf16[576,128]{1,0:T(8,128)(2,1)S(1)}, u32[]{:S(2)}, u32[]{:S(2)}) collective-permute-start(bf16[576,128]{1,0:T(8,128)(2,1)S(1)} %collective-permute-done.11.refs_14_), channel_id=1, source_target_pairs={{0,112},{8,24},{16,0},{24,40},{32,16},{40,56},{48,32},{56,72},{64,... | collective-permute-start | bytes 442376 | tf_op jit(solution)/shard_map/ppermute | solution.py:302
  112.8 3.2 %collective-permute-start.12 = (bf16[592,128]{1,0:T(8,128)(2,1)S(1)}, bf16[592,128]{1,0:T(8,128)(2,1)S(1)}, u32[]{:S(2)}, u32[]{:S(2)}) collective-permute-start(bf16[592,128]{1,0:T(8,128)(2,1)S(1)} %collective-permute-done.5.refs_5_), channel_id=1, source_target_pairs={{0,16},{8,120},{16,32},{24,8},{32,48},{40,24},{48,64},{56,40},{64,... | collective-permute-start | bytes 454664 | tf_op jit(solution)/shard_map/ppermute | solution.py:302
  117.2 4.4 %collective-permute-done.12.refs_7_ = bf16[592,128]{1,0:T(8,128)(2,1)S(1)} collective-permute-done((bf16[592,128]{1,0:T(8,128)(2,1)S(1)}, bf16[592,128]{1,0:T(8,128)(2,1)S(1)}, u32[]{:S(2)}, u32[]{:S(2)}) %collective-permute-start.12) | collective-permute-done | bytes 151584 | tf_op jit(solution)/shard_map/ppermute | solution.py:302
  121.7 4.6 %attend.1 = bf16[8,64,640]{2,1,0:T(8,128)(2,1)S(1)} custom-call(f32[1,128]{1,0:T(1,128)S(1)} %convert_bitcast_fusion.starts_ref, f32[576,128]{1,0:T(8,128)S(1)} %get-tuple-element.26.place_ref, bf16[512,640]{1,0:T(8,128)(2,1)S(1)} %bitcast.19, bf16[592,128]{1,0:T(8,128)(2,1)S(1)} %get-tuple-element.29.refs_0_, ...), custom_call_target="tpu_custom_call" | custom-call | flops 1342177280 | bytes 1310720 | tf_op jit(solution)/shard_map/attend/pallas_call | solution.py:258
  126.3 11.1 %all_to_all.32 = bf16[8,64,640]{2,1,0:T(8,128)(2,1)S(1)} all-to-all(bf16[8,64,640]{2,1,0:T(8,128)(2,1)S(1)} %attend.1), channel_id=1, replica_groups=mesh['x'=4,'zh'=8,'zl'=2,'tp'=8] {'x','zl'}, dimensions={0} | all-to-all | bytes 1310720 | tf_op jit(solution)/shard_map/all_to_all | solution.py:275
  137.9 22.9 %all_to_all.33 = bf16[8,64,640]{2,1,0:T(8,128)(2,1)S(1)} all-to-all(bf16[8,64,640]{2,1,0:T(8,128)(2,1)S(1)} %bitcast.18), channel_id=1, replica_groups=mesh['x'=4,'zh'=8,'zl'=2,'tp'=8] {'tp'}, dimensions={0} | all-to-all | bytes 1310720 | tf_op jit(solution)/shard_map/all_to_all | solution.py:275
  (33 shorter events, 13.4 us)
Async XLA Ops:
  0.0 0.7 copy-start.2
  0.7 1.2 copy-start
  20.2 11.7 %copy-start.1 = (bf16[64,7168]{1,0:T(8,128)(2,1)S(1)}, bf16[64,7168]{1,0:T(8,128)(2,1)}, u32[]{:S(2)}) copy-start(bf16[64,7168]{1,0:T(8,128)(2,1)} %rows_ref) | copy-start | bytes 2752516
  34.6 32.0 %all-to-all-start.2 = ((bf16[8,64,640]{2,1,0:T(8,128)(2,1)}), bf16[8,64,640]{2,1,0:T(8,128)(2,1)S(1)}, u32[]{:S(2)}, u32[]{:S(2)}) async-start(bf16[8,64,640]{2,1,0:T(8,128)(2,1)} %split_queries.1), calls=%async_computation.2 | async-start | bytes 1310720 | tf_op jit(solution)/shard_map/all_to_all | solution.py:275
  40.1 26.5 %collective-permute-start.1 = (bf16[592,128]{1,0:T(8,128)(2,1)S(1)}, bf16[592,128]{1,0:T(8,128)(2,1)S(1)}, u32[]{:S(2)}, u32[]{:S(2)}) collective-permute-start(bf16[592,128]{1,0:T(8,128)(2,1)S(1)} %get-tuple-element.29.refs_0_), channel_id=1, source_target_pairs={{0,112},{8,24},{16,0},{24,40},{32,16},{40,56},{48,32},{56,72},{64,... | collective-permute-start | bytes 454664 | tf_op jit(solution)/shard_map/ppermute | solution.py:302
  50.0 16.5 %collective-permute-start = (bf16[592,128]{1,0:T(8,128)(2,1)S(1)}, bf16[592,128]{1,0:T(8,128)(2,1)S(1)}, u32[]{:S(2)}, u32[]{:S(2)}) collective-permute-start(bf16[592,128]{1,0:T(8,128)(2,1)S(1)} %get-tuple-element.29.refs_0_), channel_id=1, source_target_pairs={{0,16},{8,120},{16,32},{24,8},{32,48},{40,24},{48,64},{56,40},{64,... | collective-permute-start | bytes 454664 | tf_op jit(solution)/shard_map/ppermute | solution.py:302
  52.0 8.0 %collective-permute-start.3 = (bf16[576,128]{1,0:T(8,128)(2,1)S(1)}, bf16[576,128]{1,0:T(8,128)(2,1)S(1)}, u32[]{:S(2)}, u32[]{:S(2)}) collective-permute-start(bf16[576,128]{1,0:T(8,128)(2,1)S(1)} %get-tuple-element.30.refs_8_), channel_id=1, source_target_pairs={{0,112},{8,24},{16,0},{24,40},{32,16},{40,56},{48,32},{56,72},{64,... | collective-permute-start | bytes 442376 | tf_op jit(solution)/shard_map/ppermute | solution.py:302
  57.4 9.1 %collective-permute-start.2 = (bf16[576,128]{1,0:T(8,128)(2,1)S(1)}, bf16[576,128]{1,0:T(8,128)(2,1)S(1)}, u32[]{:S(2)}, u32[]{:S(2)}) collective-permute-start(bf16[576,128]{1,0:T(8,128)(2,1)S(1)} %get-tuple-element.30.refs_8_), channel_id=1, source_target_pairs={{0,16},{8,120},{16,32},{24,8},{32,48},{40,24},{48,64},{56,40},{64,... | collective-permute-start | bytes 442376 | tf_op jit(solution)/shard_map/ppermute | solution.py:302
  67.9 40.4 %all-to-all-start.3 = ((bf16[8,64,640]{2,1,0:T(8,128)(2,1)}), bf16[8,64,640]{2,1,0:T(8,128)(2,1)}, u32[]{:S(2)}, u32[]{:S(2)}) async-start(bf16[8,64,640]{2,1,0:T(8,128)(2,1)} %bitcast.5), calls=%async_computation.3 | async-start | bytes 1310720 | tf_op jit(solution)/shard_map/all_to_all | solution.py:275
  72.2 16.2 %collective-permute-start.4 = (bf16[592,128]{1,0:T(8,128)(2,1)S(1)}, bf16[592,128]{1,0:T(8,128)(2,1)S(1)}, u32[]{:S(2)}, u32[]{:S(2)}) collective-permute-start(bf16[592,128]{1,0:T(8,128)(2,1)S(1)} %collective-permute-done.refs_1_), channel_id=1, source_target_pairs={{0,16},{8,120},{16,32},{24,8},{32,48},{40,24},{48,64},{56,40},{64,... | collective-permute-start | bytes 454664 | tf_op jit(solution)/shard_map/ppermute | solution.py:302
  75.9 14.4 %collective-permute-start.6 = (bf16[592,128]{1,0:T(8,128)(2,1)S(1)}, bf16[592,128]{1,0:T(8,128)(2,1)S(1)}, u32[]{:S(2)}, u32[]{:S(2)}) collective-permute-start(bf16[592,128]{1,0:T(8,128)(2,1)S(1)} %collective-permute-done.1.refs_2_), channel_id=1, source_target_pairs={{0,112},{8,24},{16,0},{24,40},{32,16},{40,56},{48,32},{56,72},{64,... | collective-permute-start | bytes 454664 | tf_op jit(solution)/shard_map/ppermute | solution.py:302
  79.6 16.2 %collective-permute-start.8 = (bf16[576,128]{1,0:T(8,128)(2,1)S(1)}, bf16[576,128]{1,0:T(8,128)(2,1)S(1)}, u32[]{:S(2)}, u32[]{:S(2)}) collective-permute-start(bf16[576,128]{1,0:T(8,128)(2,1)S(1)} %collective-permute-done.2.refs_9_), channel_id=1, source_target_pairs={{0,16},{8,120},{16,32},{24,8},{32,48},{40,24},{48,64},{56,40},{64,... | collective-permute-start | bytes 442376 | tf_op jit(solution)/shard_map/ppermute | solution.py:302
  82.1 15.7 %collective-permute-start.10 = (bf16[576,128]{1,0:T(8,128)(2,1)S(1)}, bf16[576,128]{1,0:T(8,128)(2,1)S(1)}, u32[]{:S(2)}, u32[]{:S(2)}) collective-permute-start(bf16[576,128]{1,0:T(8,128)(2,1)S(1)} %collective-permute-done.3.refs_10_), channel_id=1, source_target_pairs={{0,112},{8,24},{16,0},{24,40},{32,16},{40,56},{48,32},{56,72},{64,... | collective-permute-start | bytes 442376 | tf_op jit(solution)/shard_map/ppermute | solution.py:302
  88.4 20.0 %collective-permute-start.5 = (bf16[592,128]{1,0:T(8,128)(2,1)S(1)}, bf16[592,128]{1,0:T(8,128)(2,1)S(1)}, u32[]{:S(2)}, u32[]{:S(2)}) collective-permute-start(bf16[592,128]{1,0:T(8,128)(2,1)S(1)} %collective-permute-done.4.refs_3_), channel_id=1, source_target_pairs={{0,16},{8,120},{16,32},{24,8},{32,48},{40,24},{48,64},{56,40},{64,... | collective-permute-start | bytes 454664 | tf_op jit(solution)/shard_map/ppermute | solution.py:302
  90.3 18.1 %collective-permute-start.7 = (bf16[592,128]{1,0:T(8,128)(2,1)S(1)}, bf16[592,128]{1,0:T(8,128)(2,1)S(1)}, u32[]{:S(2)}, u32[]{:S(2)}) collective-permute-start(bf16[592,128]{1,0:T(8,128)(2,1)S(1)} %collective-permute-done.6.refs_4_), channel_id=1, source_target_pairs={{0,112},{8,24},{16,0},{24,40},{32,16},{40,56},{48,32},{56,72},{64,... | collective-permute-start | bytes 454664 | tf_op jit(solution)/shard_map/ppermute | solution.py:302
  95.8 8.8 %collective-permute-start.9 = (bf16[576,128]{1,0:T(8,128)(2,1)S(1)}, bf16[576,128]{1,0:T(8,128)(2,1)S(1)}, u32[]{:S(2)}, u32[]{:S(2)}) collective-permute-start(bf16[576,128]{1,0:T(8,128)(2,1)S(1)} %collective-permute-done.8.refs_11_), channel_id=1, source_target_pairs={{0,16},{8,120},{16,32},{24,8},{32,48},{40,24},{48,64},{56,40},{64,... | collective-permute-start | bytes 442376 | tf_op jit(solution)/shard_map/ppermute | solution.py:302
  97.8 10.6 %collective-permute-start.11 = (bf16[576,128]{1,0:T(8,128)(2,1)S(1)}, bf16[576,128]{1,0:T(8,128)(2,1)S(1)}, u32[]{:S(2)}, u32[]{:S(2)}) collective-permute-start(bf16[576,128]{1,0:T(8,128)(2,1)S(1)} %collective-permute-done.10.refs_12_), channel_id=1, source_target_pairs={{0,112},{8,24},{16,0},{24,40},{32,16},{40,56},{48,32},{56,72},{64,... | collective-permute-start | bytes 442376 | tf_op jit(solution)/shard_map/ppermute | solution.py:302
  103.2 0.7 copy-start.3
  108.4 8.8 %collective-permute-start.13 = (bf16[576,128]{1,0:T(8,128)(2,1)S(1)}, bf16[576,128]{1,0:T(8,128)(2,1)S(1)}, u32[]{:S(2)}, u32[]{:S(2)}) collective-permute-start(bf16[576,128]{1,0:T(8,128)(2,1)S(1)} %collective-permute-done.11.refs_14_), channel_id=1, source_target_pairs={{0,112},{8,24},{16,0},{24,40},{32,16},{40,56},{48,32},{56,72},{64,... | collective-permute-start | bytes 442376 | tf_op jit(solution)/shard_map/ppermute | solution.py:302
  112.8 8.8 %collective-permute-start.12 = (bf16[592,128]{1,0:T(8,128)(2,1)S(1)}, bf16[592,128]{1,0:T(8,128)(2,1)S(1)}, u32[]{:S(2)}, u32[]{:S(2)}) collective-permute-start(bf16[592,128]{1,0:T(8,128)(2,1)S(1)} %collective-permute-done.5.refs_5_), channel_id=1, source_target_pairs={{0,16},{8,120},{16,32},{24,8},{32,48},{40,24},{48,64},{56,40},{64,... | collective-permute-start | bytes 454664 | tf_op jit(solution)/shard_map/ppermute | solution.py:302

commit v6 on v5

--- a/solution.py
+++ b/solution.py
@@ -21,7 +21,6 @@
 AXES = ("x", "zh", "zl", "tp")
 PART = ("x", "zl")
 RING = ("zh", "zl")
-MEETINGS = (1, 3)
 
 
 def whole(n):
@@ -148,7 +147,7 @@
     ).astype(out_ref.dtype)
 
 
-def permute_rows(order, chunk, name):
+def permute_rows(order, chunk):
     return pl.pallas_call(
         permute_kernel,
         in_specs=whole(2),
@@ -156,7 +155,6 @@
         out_shape=jax.ShapeDtypeStruct(chunk.shape, chunk.dtype),
         compiler_params=params(),
         cost_estimate=cost(2 * chunk.shape[0] * chunk.size, 4 * chunk.size),
-        name=name,
     )(order, chunk)
 
 
@@ -290,8 +288,14 @@
     keys = exchange(keys, "tp").reshape(tok_dev, KEY_CHUNK)
     keys, forward, backward = sort_rows(keys, parts, per_pair)
     load, value, places = arrange(exchange(keys, PART), per_pair)
+
     load, value, rows = lax.optimization_barrier((load, value, section_token_rows))
-    queries = exchange(split_queries(rows, tp_count), "tp").reshape(tok_dev, QUERY_WIDTH)
+    queries = split_queries(rows, tp_count)
+    queries = exchange(queries, "tp").reshape(tok_dev, QUERY_WIDTH)
+    queries = permute_rows(forward, queries)
+    queries = exchange(queries.reshape(parts, tok_dev // parts, QUERY_WIDTH), PART)
+    queries = queries.reshape(parts, slabs, per_pair, QUERY_WIDTH).transpose(1, 0, 2, 3)
+    queries = queries.reshape(tok_dev, QUERY_WIDTH)
 
     def passed(block, sign):
         route = []
@@ -303,27 +307,17 @@
 
     loads, values = [load], [value]
     load_a, load_b, value_a, value_b = load, load, value, value
-    for step in range(1, slabs // 2):
-        load_a = passed(load_a, 1)
-        load_b = passed(load_b, -1)
+    for _ in range(1, slabs // 2):
+        load_a, load_b = passed(load_a, 1), passed(load_b, -1)
         value_a, value_b = passed(value_a, 1), passed(value_b, -1)
-        if step in MEETINGS:
-            load_a, load_b, value_a, value_b, queries = lax.optimization_barrier(
-                (load_a, load_b, value_a, value_b, queries)
-            )
-        if step == MEETINGS[0]:
-            queries = permute_rows(forward, queries, "sort_queries")
-            queries = exchange(queries.reshape(parts, tok_dev // parts, QUERY_WIDTH), PART)
         loads += [load_a, load_b]
         values += [value_a, value_b]
     loads.append(passed(load_a, 1))
     values.append(passed(value_b, -1))
-    queries = queries.reshape(parts, slabs, per_pair, QUERY_WIDTH).transpose(1, 0, 2, 3)
-    queries = queries.reshape(tok_dev, QUERY_WIDTH)
 
     done = attend(starts, places, queries, loads, values, parts, per_pair)
     back = exchange(done, PART).reshape(tok_dev, QUERY_WIDTH)
-    back = permute_rows(backward, back, "unsort").reshape(tp_count, local_rows, QUERY_WIDTH)
+    back = permute_rows(backward, back).reshape(tp_count, local_rows, QUERY_WIDTH)
     back = exchange(back, "tp")
     return back.transpose(1, 0, 2).reshape(local_rows, tp_count * QUERY_WIDTH)
 

time: 163 us -> 163 us (level)
  blocking collectives: 61.8 us -> 75.1 us
  starting transfers between devices: 66.2 us -> 58.8 us
  waiting for transfers between devices: 17.1 us -> 13.5 us
  Pallas kernels: 11.5 us -> 9.13 us
    all_to_all x4 -> x5, blocking collectives: 61.8 us -> 75.1 us  [exchange(): return lax.all_to_all(blocks, axis, split_axis=0, concat_axis=0, tiled=True)]
    all_to_all x2 -> x1, starting transfers between devices: 9.72 us -> 4.21 us  [exchange(): return lax.all_to_all(blocks, axis, split_axis=0, concat_axis=0, tiled=True)]
    ppermute x14, waiting for transfers between devices: 17.1 us -> 13.5 us  [passed(): return lax.ppermute(block, RING, route)]
    pallas_call x1, Pallas kernels: 2.68 us -> 0.32 us  [split_queries(): pl.pallas_call(split_queries_kernel, grid=(groups,), in_specs=[pl.BlockSp...]
    ppermute x14, starting transfers between devices: 56.5 us -> 54.5 us  [passed(): return lax.ppermute(block, RING, route)]
  transfers between devices with their start and end apart: 16 -> 15, of which waited for: 6 -> 4; matrix products, arithmetic and copies ran while one was open for 1% -> 1% of each run, Pallas kernels for 0% -> 0%
where the time goes in v6:
time: 163 us; the launch traced here: 162 us
  blocking collectives  75.1 us (46%)
  starting transfers between devices  58.8 us (36%)
  waiting for transfers between devices  13.5 us (8%)
  Pallas kernels  9.13 us (6%)
  local copies, waits for them, and re-layouts  4.65 us (3%)
    all_to_all x5, blocking collectives, exchange(): return lax.all_to_all(blocks, axis, split_axis=0, concat_axis=0, tiled=True)  75.1 us
    ppermute x14, starting transfers between devices, passed(): return lax.ppermute(block, RING, route)  54.5 us
    ppermute x14, waiting for transfers between devices, passed(): return lax.ppermute(block, RING, route)  13.5 us
    pallas_call x1, Pallas kernels, attend(): pl.pallas_call(functools.partial(attend_kernel, per_pair, len(loads)), in...  4.62 us
    all_to_all x1, starting transfers between devices, exchange(): return lax.all_to_all(blocks, axis, split_axis=0, concat_axis=0, tiled=True)  4.21 us
  transfers between devices with their start and end apart: 15, of which 4 were waited for; matrix products, arithmetic and copies ran while one was open for 1% of the time, Pallas kernels for 0%

profile of v6, /device:TPU:1, one launch (start us, length us, event | category | flops | bytes accessed | tf_op | source)
XLA Modules:
  0.0 161.7 jit_solution(2209871201167226873)
XLA Ops:
  2.9 17.3 %all_to_all.30 = bf16[8,64,384]{2,1,0:T(8,128)(2,1)S(1)} all-to-all(bf16[8,64,384]{2,1,0:T(8,128)(2,1)S(1)} %split_keys.1), channel_id=1, replica_groups=mesh['x'=4,'zh'=8,'zl'=2,'tp'=8] {'tp'}, dimensions={0} | all-to-all | bytes 786432 | tf_op jit(solution)/shard_map/all_to_all | solution.py:273
  21.2 10.5 %all_to_all.31.got_ref = bf16[8,72,384]{2,1,0:T(8,128)(2,1)S(1)} all-to-all(bf16[8,72,384]{2,1,0:T(8,128)(2,1)S(1)} %get-tuple-element.15), channel_id=1, replica_groups=mesh['x'=4,'zh'=8,'zl'=2,'tp'=8] {'x','zl'}, dimensions={0} | all-to-all | bytes 884736 | tf_op jit(solution)/shard_map/all_to_all | solution.py:273
  32.2 15.4 %all_to_all.32 = bf16[8,64,640]{2,1,0:T(8,128)(2,1)S(1)} all-to-all(bf16[8,64,640]{2,1,0:T(8,128)(2,1)S(1)} %split_queries.1), channel_id=1, replica_groups=mesh['x'=4,'zh'=8,'zl'=2,'tp'=8] {'tp'}, dimensions={0} | all-to-all | bytes 1310720 | tf_op jit(solution)/shard_map/all_to_all | solution.py:273
  49.0 4.2 %all-to-all-start.3 = ((bf16[8,64,640]{2,1,0:T(8,128)(2,1)}), bf16[8,64,640]{2,1,0:T(8,128)(2,1)}, u32[]{:S(2)}, u32[]{:S(2)}) async-start(bf16[8,64,640]{2,1,0:T(8,128)(2,1)} %bitcast.5), calls=%async_computation.3 | async-start | bytes 1310720 | tf_op jit(solution)/shard_map/all_to_all | solution.py:273
  53.2 4.2 %collective-permute-start = (bf16[592,128]{1,0:T(8,128)(2,1)S(1)}, bf16[592,128]{1,0:T(8,128)(2,1)S(1)}, u32[]{:S(2)}, u32[]{:S(2)}) collective-permute-start(bf16[592,128]{1,0:T(8,128)(2,1)S(1)} %get-tuple-element.21.refs_0_), channel_id=1, source_target_pairs={{0,16},{8,120},{16,32},{24,8},{32,48},{40,24},{48,64},{56,40},{64,... | collective-permute-start | bytes 454664 | tf_op jit(solution)/shard_map/ppermute | solution.py:306
  57.4 7.7 %collective-permute-start.8 = (bf16[576,128]{1,0:T(8,128)(2,1)S(1)}, bf16[576,128]{1,0:T(8,128)(2,1)S(1)}, u32[]{:S(2)}, u32[]{:S(2)}) collective-permute-start(bf16[576,128]{1,0:T(8,128)(2,1)S(1)} %get-tuple-element.22.refs_8_), channel_id=1, source_target_pairs={{0,112},{8,24},{16,0},{24,40},{32,16},{40,56},{48,32},{56,72},{64,... | collective-permute-start | bytes 442376 | tf_op jit(solution)/shard_map/ppermute | solution.py:306
  65.1 4.3 %collective-permute-start.1 = (bf16[592,128]{1,0:T(8,128)(2,1)S(1)}, bf16[592,128]{1,0:T(8,128)(2,1)S(1)}, u32[]{:S(2)}, u32[]{:S(2)}) collective-permute-start(bf16[592,128]{1,0:T(8,128)(2,1)S(1)} %get-tuple-element.21.refs_0_), channel_id=1, source_target_pairs={{0,112},{8,24},{16,0},{24,40},{32,16},{40,56},{48,32},{56,72},{64,... | collective-permute-start | bytes 454664 | tf_op jit(solution)/shard_map/ppermute | solution.py:306
  69.4 3.5 %collective-permute-done.refs_1_ = bf16[592,128]{1,0:T(8,128)(2,1)S(1)} collective-permute-done((bf16[592,128]{1,0:T(8,128)(2,1)S(1)}, bf16[592,128]{1,0:T(8,128)(2,1)S(1)}, u32[]{:S(2)}, u32[]{:S(2)}) %collective-permute-start) | collective-permute-done | bytes 151584 | tf_op jit(solution)/shard_map/ppermute | solution.py:306
  72.9 1.9 %collective-permute-start.2 = (bf16[592,128]{1,0:T(8,128)(2,1)S(1)}, bf16[592,128]{1,0:T(8,128)(2,1)S(1)}, u32[]{:S(2)}, u32[]{:S(2)}) collective-permute-start(bf16[592,128]{1,0:T(8,128)(2,1)S(1)} %collective-permute-done.refs_1_), channel_id=1, source_target_pairs={{0,16},{8,120},{16,32},{24,8},{32,48},{40,24},{48,64},{56,40},{64,... | collective-permute-start | bytes 454664 | tf_op jit(solution)/shard_map/ppermute | solution.py:306
  74.8 1.9 %collective-permute-start.7 = (bf16[576,128]{1,0:T(8,128)(2,1)S(1)}, bf16[576,128]{1,0:T(8,128)(2,1)S(1)}, u32[]{:S(2)}, u32[]{:S(2)}) collective-permute-start(bf16[576,128]{1,0:T(8,128)(2,1)S(1)} %get-tuple-element.22.refs_8_), channel_id=1, source_target_pairs={{0,16},{8,120},{16,32},{24,8},{32,48},{40,24},{48,64},{56,40},{64,... | collective-permute-start | bytes 442376 | tf_op jit(solution)/shard_map/ppermute | solution.py:306
  76.7 5.5 %collective-permute-start.10 = (bf16[576,128]{1,0:T(8,128)(2,1)S(1)}, bf16[576,128]{1,0:T(8,128)(2,1)S(1)}, u32[]{:S(2)}, u32[]{:S(2)}) collective-permute-start(bf16[576,128]{1,0:T(8,128)(2,1)S(1)} %collective-permute-done.8.refs_10_), channel_id=1, source_target_pairs={{0,112},{8,24},{16,0},{24,40},{32,16},{40,56},{48,32},{56,72},{64,... | collective-permute-start | bytes 442376 | tf_op jit(solution)/shard_map/ppermute | solution.py:306
  82.2 6.2 %collective-permute-start.3 = (bf16[592,128]{1,0:T(8,128)(2,1)S(1)}, bf16[592,128]{1,0:T(8,128)(2,1)S(1)}, u32[]{:S(2)}, u32[]{:S(2)}) collective-permute-start(bf16[592,128]{1,0:T(8,128)(2,1)S(1)} %collective-permute-done.1.refs_2_), channel_id=1, source_target_pairs={{0,112},{8,24},{16,0},{24,40},{32,16},{40,56},{48,32},{56,72},{64,... | collective-permute-start | bytes 454664 | tf_op jit(solution)/shard_map/ppermute | solution.py:306
  88.5 1.9 %collective-permute-start.4 = (bf16[592,128]{1,0:T(8,128)(2,1)S(1)}, bf16[592,128]{1,0:T(8,128)(2,1)S(1)}, u32[]{:S(2)}, u32[]{:S(2)}) collective-permute-start(bf16[592,128]{1,0:T(8,128)(2,1)S(1)} %collective-permute-done.2.refs_3_), channel_id=1, source_target_pairs={{0,16},{8,120},{16,32},{24,8},{32,48},{40,24},{48,64},{56,40},{64,... | collective-permute-start | bytes 454664 | tf_op jit(solution)/shard_map/ppermute | solution.py:306
  90.4 4.3 %collective-permute-start.9 = (bf16[576,128]{1,0:T(8,128)(2,1)S(1)}, bf16[576,128]{1,0:T(8,128)(2,1)S(1)}, u32[]{:S(2)}, u32[]{:S(2)}) collective-permute-start(bf16[576,128]{1,0:T(8,128)(2,1)S(1)} %collective-permute-done.7.refs_9_), channel_id=1, source_target_pairs={{0,16},{8,120},{16,32},{24,8},{32,48},{40,24},{48,64},{56,40},{64,... | collective-permute-start | bytes 442376 | tf_op jit(solution)/shard_map/ppermute | solution.py:306
  94.8 3.1 %collective-permute-start.12 = (bf16[576,128]{1,0:T(8,128)(2,1)S(1)}, bf16[576,128]{1,0:T(8,128)(2,1)S(1)}, u32[]{:S(2)}, u32[]{:S(2)}) collective-permute-start(bf16[576,128]{1,0:T(8,128)(2,1)S(1)} %collective-permute-done.10.refs_12_), channel_id=1, source_target_pairs={{0,112},{8,24},{16,0},{24,40},{32,16},{40,56},{48,32},{56,72},{64,... | collective-permute-start | bytes 442376 | tf_op jit(solution)/shard_map/ppermute | solution.py:306
  98.9 5.1 %collective-permute-done.9.refs_11_ = bf16[576,128]{1,0:T(8,128)(2,1)S(1)} collective-permute-done((bf16[576,128]{1,0:T(8,128)(2,1)S(1)}, bf16[576,128]{1,0:T(8,128)(2,1)S(1)}, u32[]{:S(2)}, u32[]{:S(2)}) %collective-permute-start.9) | collective-permute-done | bytes 147488 | tf_op jit(solution)/shard_map/ppermute | solution.py:306
  103.9 3.5 %collective-permute-start.11 = (bf16[576,128]{1,0:T(8,128)(2,1)S(1)}, bf16[576,128]{1,0:T(8,128)(2,1)S(1)}, u32[]{:S(2)}, u32[]{:S(2)}) collective-permute-start(bf16[576,128]{1,0:T(8,128)(2,1)S(1)} %collective-permute-done.9.refs_11_), channel_id=1, source_target_pairs={{0,16},{8,120},{16,32},{24,8},{32,48},{40,24},{48,64},{56,40},{64,... | collective-permute-start | bytes 442376 | tf_op jit(solution)/shard_map/ppermute | solution.py:306
  107.4 3.9 %collective-permute-start.5 = (bf16[592,128]{1,0:T(8,128)(2,1)S(1)}, bf16[592,128]{1,0:T(8,128)(2,1)S(1)}, u32[]{:S(2)}, u32[]{:S(2)}) collective-permute-start(bf16[592,128]{1,0:T(8,128)(2,1)S(1)} %collective-permute-done.3.refs_4_), channel_id=1, source_target_pairs={{0,112},{8,24},{16,0},{24,40},{32,16},{40,56},{48,32},{56,72},{64,... | collective-permute-start | bytes 454664 | tf_op jit(solution)/shard_map/ppermute | solution.py:306
  111.4 4.1 %collective-permute-start.13 = (bf16[576,128]{1,0:T(8,128)(2,1)S(1)}, bf16[576,128]{1,0:T(8,128)(2,1)S(1)}, u32[]{:S(2)}, u32[]{:S(2)}) collective-permute-start(bf16[576,128]{1,0:T(8,128)(2,1)S(1)} %collective-permute-done.12.refs_14_), channel_id=1, source_target_pairs={{0,112},{8,24},{16,0},{24,40},{32,16},{40,56},{48,32},{56,72},{64,... | collective-permute-start | bytes 442376 | tf_op jit(solution)/shard_map/ppermute | solution.py:306
  115.5 2.0 %collective-permute-start.6 = (bf16[592,128]{1,0:T(8,128)(2,1)S(1)}, bf16[592,128]{1,0:T(8,128)(2,1)S(1)}, u32[]{:S(2)}, u32[]{:S(2)}) collective-permute-start(bf16[592,128]{1,0:T(8,128)(2,1)S(1)} %collective-permute-done.4.refs_5_), channel_id=1, source_target_pairs={{0,16},{8,120},{16,32},{24,8},{32,48},{40,24},{48,64},{56,40},{64,... | collective-permute-start | bytes 454664 | tf_op jit(solution)/shard_map/ppermute | solution.py:306
  119.0 4.6 %collective-permute-done.6.refs_7_ = bf16[592,128]{1,0:T(8,128)(2,1)S(1)} collective-permute-done((bf16[592,128]{1,0:T(8,128)(2,1)S(1)}, bf16[592,128]{1,0:T(8,128)(2,1)S(1)}, u32[]{:S(2)}, u32[]{:S(2)}) %collective-permute-start.6) | collective-permute-done | bytes 151584 | tf_op jit(solution)/shard_map/ppermute | solution.py:306
  123.7 4.6 %attend.1 = bf16[8,64,640]{2,1,0:T(8,128)(2,1)S(1)} custom-call(f32[1,128]{1,0:T(1,128)S(1)} %convert_bitcast_fusion.starts_ref, f32[576,128]{1,0:T(8,128)S(1)} %get-tuple-element.16.place_ref, bf16[512,640]{1,0:T(8,128)(2,1)S(1)} %bitcast.19, bf16[592,128]{1,0:T(8,128)(2,1)S(1)} %get-tuple-element.21.refs_0_, ...), custom_call_target="tpu_custom_call" | custom-call | flops 1342177280 | bytes 1310720 | tf_op jit(solution)/shard_map/attend/pallas_call | solution.py:256
  128.3 13.7 %all_to_all.33 = bf16[8,64,640]{2,1,0:T(8,128)(2,1)S(1)} all-to-all(bf16[8,64,640]{2,1,0:T(8,128)(2,1)S(1)} %attend.1), channel_id=1, replica_groups=mesh['x'=4,'zh'=8,'zl'=2,'tp'=8] {'x','zl'}, dimensions={0} | all-to-all | bytes 1310720 | tf_op jit(solution)/shard_map/all_to_all | solution.py:273
  142.6 18.2 %all_to_all.34 = bf16[8,64,640]{2,1,0:T(8,128)(2,1)S(1)} all-to-all(bf16[8,64,640]{2,1,0:T(8,128)(2,1)S(1)} %bitcast.18), channel_id=1, replica_groups=mesh['x'=4,'zh'=8,'zl'=2,'tp'=8] {'tp'}, dimensions={0} | all-to-all | bytes 1310720 | tf_op jit(solution)/shard_map/all_to_all | solution.py:273
  (32 shorter events, 9.7 us)
Async XLA Ops:
  0.0 0.7 copy-start.2
  0.7 1.2 copy-start
  20.2 11.7 %copy-start.1 = (bf16[64,7168]{1,0:T(8,128)(2,1)S(1)}, bf16[64,7168]{1,0:T(8,128)(2,1)}, u32[]{:S(2)}) copy-start(bf16[64,7168]{1,0:T(8,128)(2,1)} %rows_ref) | copy-start | bytes 2752516
  49.0 68.6 %all-to-all-start.3 = ((bf16[8,64,640]{2,1,0:T(8,128)(2,1)}), bf16[8,64,640]{2,1,0:T(8,128)(2,1)}, u32[]{:S(2)}, u32[]{:S(2)}) async-start(bf16[8,64,640]{2,1,0:T(8,128)(2,1)} %bitcast.5), calls=%async_computation.3 | async-start | bytes 1310720 | tf_op jit(solution)/shard_map/all_to_all | solution.py:273
  53.2 19.7 %collective-permute-start = (bf16[592,128]{1,0:T(8,128)(2,1)S(1)}, bf16[592,128]{1,0:T(8,128)(2,1)S(1)}, u32[]{:S(2)}, u32[]{:S(2)}) collective-permute-start(bf16[592,128]{1,0:T(8,128)(2,1)S(1)} %get-tuple-element.21.refs_0_), channel_id=1, source_target_pairs={{0,16},{8,120},{16,32},{24,8},{32,48},{40,24},{48,64},{56,40},{64,... | collective-permute-start | bytes 454664 | tf_op jit(solution)/shard_map/ppermute | solution.py:306
  57.4 19.3 %collective-permute-start.8 = (bf16[576,128]{1,0:T(8,128)(2,1)S(1)}, bf16[576,128]{1,0:T(8,128)(2,1)S(1)}, u32[]{:S(2)}, u32[]{:S(2)}) collective-permute-start(bf16[576,128]{1,0:T(8,128)(2,1)S(1)} %get-tuple-element.22.refs_8_), channel_id=1, source_target_pairs={{0,112},{8,24},{16,0},{24,40},{32,16},{40,56},{48,32},{56,72},{64,... | collective-permute-start | bytes 442376 | tf_op jit(solution)/shard_map/ppermute | solution.py:306
  65.1 17.1 %collective-permute-start.1 = (bf16[592,128]{1,0:T(8,128)(2,1)S(1)}, bf16[592,128]{1,0:T(8,128)(2,1)S(1)}, u32[]{:S(2)}, u32[]{:S(2)}) collective-permute-start(bf16[592,128]{1,0:T(8,128)(2,1)S(1)} %get-tuple-element.21.refs_0_), channel_id=1, source_target_pairs={{0,112},{8,24},{16,0},{24,40},{32,16},{40,56},{48,32},{56,72},{64,... | collective-permute-start | bytes 454664 | tf_op jit(solution)/shard_map/ppermute | solution.py:306
  72.9 15.6 %collective-permute-start.2 = (bf16[592,128]{1,0:T(8,128)(2,1)S(1)}, bf16[592,128]{1,0:T(8,128)(2,1)S(1)}, u32[]{:S(2)}, u32[]{:S(2)}) collective-permute-start(bf16[592,128]{1,0:T(8,128)(2,1)S(1)} %collective-permute-done.refs_1_), channel_id=1, source_target_pairs={{0,16},{8,120},{16,32},{24,8},{32,48},{40,24},{48,64},{56,40},{64,... | collective-permute-start | bytes 454664 | tf_op jit(solution)/shard_map/ppermute | solution.py:306
  74.8 15.6 %collective-permute-start.7 = (bf16[576,128]{1,0:T(8,128)(2,1)S(1)}, bf16[576,128]{1,0:T(8,128)(2,1)S(1)}, u32[]{:S(2)}, u32[]{:S(2)}) collective-permute-start(bf16[576,128]{1,0:T(8,128)(2,1)S(1)} %get-tuple-element.22.refs_8_), channel_id=1, source_target_pairs={{0,16},{8,120},{16,32},{24,8},{32,48},{40,24},{48,64},{56,40},{64,... | collective-permute-start | bytes 442376 | tf_op jit(solution)/shard_map/ppermute | solution.py:306
  76.7 18.0 %collective-permute-start.10 = (bf16[576,128]{1,0:T(8,128)(2,1)S(1)}, bf16[576,128]{1,0:T(8,128)(2,1)S(1)}, u32[]{:S(2)}, u32[]{:S(2)}) collective-permute-start(bf16[576,128]{1,0:T(8,128)(2,1)S(1)} %collective-permute-done.8.refs_10_), channel_id=1, source_target_pairs={{0,112},{8,24},{16,0},{24,40},{32,16},{40,56},{48,32},{56,72},{64,... | collective-permute-start | bytes 442376 | tf_op jit(solution)/shard_map/ppermute | solution.py:306
  82.2 25.2 %collective-permute-start.3 = (bf16[592,128]{1,0:T(8,128)(2,1)S(1)}, bf16[592,128]{1,0:T(8,128)(2,1)S(1)}, u32[]{:S(2)}, u32[]{:S(2)}) collective-permute-start(bf16[592,128]{1,0:T(8,128)(2,1)S(1)} %collective-permute-done.1.refs_2_), channel_id=1, source_target_pairs={{0,112},{8,24},{16,0},{24,40},{32,16},{40,56},{48,32},{56,72},{64,... | collective-permute-start | bytes 454664 | tf_op jit(solution)/shard_map/ppermute | solution.py:306
  88.5 27.1 %collective-permute-start.4 = (bf16[592,128]{1,0:T(8,128)(2,1)S(1)}, bf16[592,128]{1,0:T(8,128)(2,1)S(1)}, u32[]{:S(2)}, u32[]{:S(2)}) collective-permute-start(bf16[592,128]{1,0:T(8,128)(2,1)S(1)} %collective-permute-done.2.refs_3_), channel_id=1, source_target_pairs={{0,16},{8,120},{16,32},{24,8},{32,48},{40,24},{48,64},{56,40},{64,... | collective-permute-start | bytes 454664 | tf_op jit(solution)/shard_map/ppermute | solution.py:306
  90.4 13.5 %collective-permute-start.9 = (bf16[576,128]{1,0:T(8,128)(2,1)S(1)}, bf16[576,128]{1,0:T(8,128)(2,1)S(1)}, u32[]{:S(2)}, u32[]{:S(2)}) collective-permute-start(bf16[576,128]{1,0:T(8,128)(2,1)S(1)} %collective-permute-done.7.refs_9_), channel_id=1, source_target_pairs={{0,16},{8,120},{16,32},{24,8},{32,48},{40,24},{48,64},{56,40},{64,... | collective-permute-start | bytes 442376 | tf_op jit(solution)/shard_map/ppermute | solution.py:306
  94.8 16.6 %collective-permute-start.12 = (bf16[576,128]{1,0:T(8,128)(2,1)S(1)}, bf16[576,128]{1,0:T(8,128)(2,1)S(1)}, u32[]{:S(2)}, u32[]{:S(2)}) collective-permute-start(bf16[576,128]{1,0:T(8,128)(2,1)S(1)} %collective-permute-done.10.refs_12_), channel_id=1, source_target_pairs={{0,112},{8,24},{16,0},{24,40},{32,16},{40,56},{48,32},{56,72},{64,... | collective-permute-start | bytes 442376 | tf_op jit(solution)/shard_map/ppermute | solution.py:306
  97.8 0.7 copy-start.3
  103.9 14.8 %collective-permute-start.11 = (bf16[576,128]{1,0:T(8,128)(2,1)S(1)}, bf16[576,128]{1,0:T(8,128)(2,1)S(1)}, u32[]{:S(2)}, u32[]{:S(2)}) collective-permute-start(bf16[576,128]{1,0:T(8,128)(2,1)S(1)} %collective-permute-done.9.refs_11_), channel_id=1, source_target_pairs={{0,16},{8,120},{16,32},{24,8},{32,48},{40,24},{48,64},{56,40},{64,... | collective-permute-start | bytes 442376 | tf_op jit(solution)/shard_map/ppermute | solution.py:306
  107.4 11.3 %collective-permute-start.5 = (bf16[592,128]{1,0:T(8,128)(2,1)S(1)}, bf16[592,128]{1,0:T(8,128)(2,1)S(1)}, u32[]{:S(2)}, u32[]{:S(2)}) collective-permute-start(bf16[592,128]{1,0:T(8,128)(2,1)S(1)} %collective-permute-done.3.refs_4_), channel_id=1, source_target_pairs={{0,112},{8,24},{16,0},{24,40},{32,16},{40,56},{48,32},{56,72},{64,... | collective-permute-start | bytes 454664 | tf_op jit(solution)/shard_map/ppermute | solution.py:306
  111.4 7.7 %collective-permute-start.13 = (bf16[576,128]{1,0:T(8,128)(2,1)S(1)}, bf16[576,128]{1,0:T(8,128)(2,1)S(1)}, u32[]{:S(2)}, u32[]{:S(2)}) collective-permute-start(bf16[576,128]{1,0:T(8,128)(2,1)S(1)} %collective-permute-done.12.refs_14_), channel_id=1, source_target_pairs={{0,112},{8,24},{16,0},{24,40},{32,16},{40,56},{48,32},{56,72},{64,... | collective-permute-start | bytes 442376 | tf_op jit(solution)/shard_map/ppermute | solution.py:306
  115.5 8.1 %collective-permute-start.6 = (bf16[592,128]{1,0:T(8,128)(2,1)S(1)}, bf16[592,128]{1,0:T(8,128)(2,1)S(1)}, u32[]{:S(2)}, u32[]{:S(2)}) collective-permute-start(bf16[592,128]{1,0:T(8,128)(2,1)S(1)} %collective-permute-done.4.refs_5_), channel_id=1, source_target_pairs={{0,16},{8,120},{16,32},{24,8},{32,48},{40,24},{48,64},{56,40},{64,... | collective-permute-start | bytes 454664 | tf_op jit(solution)/shard_map/ppermute | solution.py:306

commit v7 on v6

--- a/solution.py
+++ b/solution.py
@@ -158,7 +158,7 @@
     )(order, chunk)
 
 
-def arrange_kernel(per_pair, got_ref, key_ref, value_ref, place_ref):
+def arrange_kernel(per_pair, got_ref, load_ref, place_ref):
     sources, padded, _ = got_ref.shape
     blocks = padded // per_pair
     span = sources * per_pair
@@ -168,15 +168,15 @@
         rows = slice(b * per_pair, (b + 1) * per_pair)
         block = jnp.concatenate([piece[rows] for piece in pieces], axis=0)
         at = slice(b * span, (b + 1) * span)
-        key_ref[at, :] = block[:, :HEAD_SIZE].astype(key_ref.dtype)
-        value_ref[at, :] = block[:, HEAD_SIZE:KV_WIDTH].astype(value_ref.dtype)
+        load_ref[at, :] = block[:, :KV_WIDTH].astype(load_ref.dtype)
         places.append(block[:, KV_WIDTH:])
         place_ref[at, :] = places[b]
     rows = jnp.zeros((16, LANES), jnp.float32)
     for b in range(1, blocks):
         pair = jnp.concatenate([places[b - 1], places[b]], axis=0)[:, 0:1]
         rows = jnp.where(iota((16, LANES), 0) == b - 1, column_to_row(pair), rows)
-    key_ref[blocks * span :, :] = rows.astype(key_ref.dtype)
+    load_ref[blocks * span :, :HEAD_SIZE] = rows.astype(load_ref.dtype)
+    load_ref[blocks * span :, HEAD_SIZE:] = jnp.zeros((16, HEAD_SIZE), load_ref.dtype)
 
 
 def arrange(got, per_pair):
@@ -185,10 +185,9 @@
     return pl.pallas_call(
         functools.partial(arrange_kernel, per_pair),
         in_specs=whole(1),
-        out_specs=whole(3),
+        out_specs=whole(2),
         out_shape=[
-            jax.ShapeDtypeStruct((rows + 16, HEAD_SIZE), got.dtype),
-            jax.ShapeDtypeStruct((rows, HEAD_SIZE), got.dtype),
+            jax.ShapeDtypeStruct((rows + 16, KV_WIDTH), got.dtype),
             jax.ShapeDtypeStruct((rows, LANES), jnp.float32),
         ],
         compiler_params=params(),
@@ -212,11 +211,11 @@
     for b in range(blocks):
         rows = slice(b * span, b * span + pair)
         for at in range(loads):
-            key_ref[at * pair : (at + 1) * pair, :] = load_refs[at][rows, :]
-            value_ref[at * pair : (at + 1) * pair, :] = value_refs[at][rows, :]
+            key_ref[at * pair : (at + 1) * pair, :] = load_refs[at][rows, :HEAD_SIZE]
+            value_ref[at * pair : (at + 1) * pair, :] = value_refs[at][rows, -HEAD_SIZE:]
         key_place = jnp.concatenate(
             [
-                load_ref[(blocks + 1) * span :, :].astype(jnp.float32)[b : b + 1] + shift
+                load_ref[(blocks + 1) * span :, :LANES].astype(jnp.float32)[b : b + 1] + shift
                 for load_ref in load_refs
             ],
             axis=1,
@@ -287,9 +286,9 @@
     keys = split_keys(section_token_rows, row_target, tp_count)
     keys = exchange(keys, "tp").reshape(tok_dev, KEY_CHUNK)
     keys, forward, backward = sort_rows(keys, parts, per_pair)
-    load, value, places = arrange(exchange(keys, PART), per_pair)
-
-    load, value, rows = lax.optimization_barrier((load, value, section_token_rows))
+    load, places = arrange(exchange(keys, PART), per_pair)
+
+    load, rows = lax.optimization_barrier((load, section_token_rows))
     queries = split_queries(rows, tp_count)
     queries = exchange(queries, "tp").reshape(tok_dev, QUERY_WIDTH)
     queries = permute_rows(forward, queries)
@@ -305,15 +304,13 @@
                 route.append((at * 2 + low, to * 2 + low))
         return lax.ppermute(block, RING, route)
 
-    loads, values = [load], [value]
-    load_a, load_b, value_a, value_b = load, load, value, value
+    loads = [load]
+    load_a, load_b = load, load
     for _ in range(1, slabs // 2):
         load_a, load_b = passed(load_a, 1), passed(load_b, -1)
-        value_a, value_b = passed(value_a, 1), passed(value_b, -1)
         loads += [load_a, load_b]
-        values += [value_a, value_b]
-    loads.append(passed(load_a, 1))
-    values.append(passed(value_b, -1))
+    values = loads + [passed(load_b[:, HEAD_SIZE:], -1)]
+    loads = loads + [passed(load_a[:, :HEAD_SIZE], 1)]
 
     done = attend(starts, places, queries, loads, values, parts, per_pair)
     back = exchange(done, PART).reshape(tok_dev, QUERY_WIDTH)

time: 163 us -> 166 us (1.018)
  starting transfers between devices: 58.8 us -> 33.9 us
  waiting for transfers between devices: 13.5 us -> 35.8 us
  blocking collectives: 75.1 us -> 80.9 us
    ppermute x14 -> x8, starting transfers between devices: 54.5 us -> 29.7 us  [passed(): return lax.ppermute(block, RING, route)]
    ppermute x14 -> x8, waiting for transfers between devices: 13.5 us -> 35.8 us  [passed(): return lax.ppermute(block, RING, route)]
    all_to_all x5, blocking collectives: 75.1 us -> 80.9 us  [exchange(): return lax.all_to_all(blocks, axis, split_axis=0, concat_axis=0, tiled=True)]
  transfers between devices with their start and end apart: 15 -> 9, of which waited for: 4 -> 6; matrix products, arithmetic and copies ran while one was open for 1% -> 1% of each run, Pallas kernels for 0% -> 0%
where the time goes in v7:
time: 166 us
  blocking collectives  80.9 us (49%)
  waiting for transfers between devices  35.8 us (22%)
  starting transfers between devices  33.9 us (20%)
  Pallas kernels  9.34 us (6%)
  local copies, waits for them, and re-layouts  4.67 us (3%)
    all_to_all x5, blocking collectives, exchange(): return lax.all_to_all(blocks, axis, split_axis=0, concat_axis=0, tiled=True)  80.9 us
    ppermute x8, waiting for transfers between devices, passed(): return lax.ppermute(block, RING, route)  35.8 us
    ppermute x8, starting transfers between devices, passed(): return lax.ppermute(block, RING, route)  29.7 us
    pallas_call x1, Pallas kernels, attend(): pl.pallas_call(functools.partial(attend_kernel, per_pair, len(loads)), in...  4.82 us
    all_to_all x1, starting transfers between devices, exchange(): return lax.all_to_all(blocks, axis, split_axis=0, concat_axis=0, tiled=True)  4.2 us
  transfers between devices with their start and end apart: 9, of which 6 were waited for; matrix products, arithmetic and copies ran while one was open for 1% of the time, Pallas kernels for 0%

profile of v7, /device:TPU:1, one launch (start us, length us, event | category | flops | bytes accessed | tf_op | source)
XLA Modules:
  0.0 165.7 jit_solution(17999369614194272195)
XLA Ops:
  0.7 1.2 copy-done
  2.9 17.3 %all_to_all.30 = bf16[8,64,384]{2,1,0:T(8,128)(2,1)S(1)} all-to-all(bf16[8,64,384]{2,1,0:T(8,128)(2,1)S(1)} %split_keys.1), channel_id=1, replica_groups=mesh['x'=4,'zh'=8,'zl'=2,'tp'=8] {'tp'}, dimensions={0} | all-to-all | bytes 786432 | tf_op jit(solution)/shard_map/all_to_all | solution.py:272
  21.2 10.5 %all_to_all.31.got_ref = bf16[8,72,384]{2,1,0:T(8,128)(2,1)S(1)} all-to-all(bf16[8,72,384]{2,1,0:T(8,128)(2,1)S(1)} %get-tuple-element.13), channel_id=1, replica_groups=mesh['x'=4,'zh'=8,'zl'=2,'tp'=8] {'x','zl'}, dimensions={0} | all-to-all | bytes 884736 | tf_op jit(solution)/shard_map/all_to_all | solution.py:272
  32.2 15.4 %all_to_all.32 = bf16[8,64,640]{2,1,0:T(8,128)(2,1)S(1)} all-to-all(bf16[8,64,640]{2,1,0:T(8,128)(2,1)S(1)} %split_queries.1), channel_id=1, replica_groups=mesh['x'=4,'zh'=8,'zl'=2,'tp'=8] {'tp'}, dimensions={0} | all-to-all | bytes 1310720 | tf_op jit(solution)/shard_map/all_to_all | solution.py:272
  47.6 1.4 shard_map.37
  49.0 4.2 %all-to-all-start.3 = ((bf16[8,64,640]{2,1,0:T(8,128)(2,1)}), bf16[8,64,640]{2,1,0:T(8,128)(2,1)}, u32[]{:S(2)}, u32[]{:S(2)}) async-start(bf16[8,64,640]{2,1,0:T(8,128)(2,1)} %bitcast.5), calls=%async_computation.3 | async-start | bytes 1310720 | tf_op jit(solution)/shard_map/all_to_all | solution.py:272
  53.2 4.2 %collective-permute-start = (bf16[592,256]{1,0:T(8,128)(2,1)S(1)}, bf16[592,256]{1,0:T(8,128)(2,1)S(1)}, u32[]{:S(2)}, u32[]{:S(2)}) collective-permute-start(bf16[592,256]{1,0:T(8,128)(2,1)S(1)} %get-tuple-element.18.refs_0_.refs_8_), channel_id=1, source_target_pairs={{0,16},{8,120},{16,32},{24,8},{32,48},{40,24},{48,64},{56,40},{64,... | collective-permute-start | bytes 909320 | tf_op jit(solution)/shard_map/ppermute | solution.py:305
  57.4 7.7 %collective-permute-start.1 = (bf16[592,256]{1,0:T(8,128)(2,1)S(1)}, bf16[592,256]{1,0:T(8,128)(2,1)S(1)}, u32[]{:S(2)}, u32[]{:S(2)}) collective-permute-start(bf16[592,256]{1,0:T(8,128)(2,1)S(1)} %get-tuple-element.18.refs_0_.refs_8_), channel_id=1, source_target_pairs={{0,112},{8,24},{16,0},{24,40},{32,16},{40,56},{48,32},{56,72},{64,... | collective-permute-start | bytes 909320 | tf_op jit(solution)/shard_map/ppermute | solution.py:305
  65.1 13.0 %collective-permute-done.refs_1_.refs_9_ = bf16[592,256]{1,0:T(8,128)(2,1)S(1)} collective-permute-done((bf16[592,256]{1,0:T(8,128)(2,1)S(1)}, bf16[592,256]{1,0:T(8,128)(2,1)S(1)}, u32[]{:S(2)}, u32[]{:S(2)}) %collective-permute-start) | collective-permute-done | bytes 303136 | tf_op jit(solution)/shard_map/ppermute | solution.py:305
  78.2 1.9 %collective-permute-start.2 = (bf16[592,256]{1,0:T(8,128)(2,1)S(1)}, bf16[592,256]{1,0:T(8,128)(2,1)S(1)}, u32[]{:S(2)}, u32[]{:S(2)}) collective-permute-start(bf16[592,256]{1,0:T(8,128)(2,1)S(1)} %collective-permute-done.refs_1_.refs_9_), channel_id=1, source_target_pairs={{0,16},{8,120},{16,32},{24,8},{32,48},{40,24},{48,64},{56,40},{64,... | collective-permute-start | bytes 909320 | tf_op jit(solution)/shard_map/ppermute | solution.py:305
  80.1 5.5 %collective-permute-start.3 = (bf16[592,256]{1,0:T(8,128)(2,1)S(1)}, bf16[592,256]{1,0:T(8,128)(2,1)S(1)}, u32[]{:S(2)}, u32[]{:S(2)}) collective-permute-start(bf16[592,256]{1,0:T(8,128)(2,1)S(1)} %collective-permute-done.1.refs_2_.refs_10_), channel_id=1, source_target_pairs={{0,112},{8,24},{16,0},{24,40},{32,16},{40,56},{48,32},{56,72},{64,... | collective-permute-start | bytes 909320 | tf_op jit(solution)/shard_map/ppermute | solution.py:305
  85.6 2.2 %collective-permute-done.2.refs_3_.refs_11_ = bf16[592,256]{1,0:T(8,128)(2,1)S(1)} collective-permute-done((bf16[592,256]{1,0:T(8,128)(2,1)S(1)}, bf16[592,256]{1,0:T(8,128)(2,1)S(1)}, u32[]{:S(2)}, u32[]{:S(2)}) %collective-permute-start.2) | collective-permute-done | bytes 303136 | tf_op jit(solution)/shard_map/ppermute | solution.py:305
  87.8 1.9 %collective-permute-start.4 = (bf16[592,256]{1,0:T(8,128)(2,1)S(1)}, bf16[592,256]{1,0:T(8,128)(2,1)S(1)}, u32[]{:S(2)}, u32[]{:S(2)}) collective-permute-start(bf16[592,256]{1,0:T(8,128)(2,1)S(1)} %collective-permute-done.2.refs_3_.refs_11_), channel_id=1, source_target_pairs={{0,16},{8,120},{16,32},{24,8},{32,48},{40,24},{48,64},{56,40},{64,... | collective-permute-start | bytes 909320 | tf_op jit(solution)/shard_map/ppermute | solution.py:305
  89.7 7.0 %collective-permute-done.3.refs_4_.refs_12_ = bf16[592,256]{1,0:T(8,128)(2,1)S(1)} collective-permute-done((bf16[592,256]{1,0:T(8,128)(2,1)S(1)}, bf16[592,256]{1,0:T(8,128)(2,1)S(1)}, u32[]{:S(2)}, u32[]{:S(2)}) %collective-permute-start.3) | collective-permute-done | bytes 303136 | tf_op jit(solution)/shard_map/ppermute | solution.py:305
  96.8 4.7 %collective-permute-start.5 = (bf16[592,256]{1,0:T(8,128)(2,1)S(1)}, bf16[592,256]{1,0:T(8,128)(2,1)S(1)}, u32[]{:S(2)}, u32[]{:S(2)}) collective-permute-start(bf16[592,256]{1,0:T(8,128)(2,1)S(1)} %collective-permute-done.3.refs_4_.refs_12_), channel_id=1, source_target_pairs={{0,112},{8,24},{16,0},{24,40},{32,16},{40,56},{48,32},{56,72},{64,... | collective-permute-start | bytes 909320 | tf_op jit(solution)/shard_map/ppermute | solution.py:305
  103.1 4.4 %collective-permute-done.4.refs_5_.refs_13_ = bf16[592,256]{1,0:T(8,128)(2,1)S(1)} collective-permute-done((bf16[592,256]{1,0:T(8,128)(2,1)S(1)}, bf16[592,256]{1,0:T(8,128)(2,1)S(1)}, u32[]{:S(2)}, u32[]{:S(2)}) %collective-permute-start.4) | collective-permute-done | bytes 303136 | tf_op jit(solution)/shard_map/ppermute | solution.py:305
  107.5 1.9 %collective-permute-start.6 = (bf16[592,128]{1,0:T(8,128)(2,1)S(1)}, bf16[592,128]{1,0:T(8,128)(2,1)S(1)}, u32[]{:S(2)}, u32[]{:S(2)}) collective-permute-start(bf16[592,128]{1,0:T(8,128)(2,1)S(1)} %slice.8), channel_id=1, source_target_pairs={{0,16},{8,120},{16,32},{24,8},{32,48},{40,24},{48,64},{56,40},{64,... | collective-permute-start | bytes 454664 | tf_op jit(solution)/shard_map/ppermute | solution.py:305
  109.4 3.9 %collective-permute-done.5.refs_6_.refs_14_ = bf16[592,256]{1,0:T(8,128)(2,1)S(1)} collective-permute-done((bf16[592,256]{1,0:T(8,128)(2,1)S(1)}, bf16[592,256]{1,0:T(8,128)(2,1)S(1)}, u32[]{:S(2)}, u32[]{:S(2)}) %collective-permute-start.5) | collective-permute-done | bytes 303136 | tf_op jit(solution)/shard_map/ppermute | solution.py:305
  113.3 1.9 %collective-permute-start.7 = (bf16[592,128]{1,0:T(8,128)(2,1)S(1)}, bf16[592,128]{1,0:T(8,128)(2,1)S(1)}, u32[]{:S(2)}, u32[]{:S(2)}) collective-permute-start(bf16[592,128]{1,0:T(8,128)(2,1)S(1)} %slice.9), channel_id=1, source_target_pairs={{0,112},{8,24},{16,0},{24,40},{32,16},{40,56},{48,32},{56,72},{64,... | collective-permute-start | bytes 454664 | tf_op jit(solution)/shard_map/ppermute | solution.py:305
  115.2 1.1 copy.7
  116.4 5.2 %collective-permute-done.7.refs_15_ = bf16[592,128]{1,0:T(8,128)(2,1)S(1)} collective-permute-done((bf16[592,128]{1,0:T(8,128)(2,1)S(1)}, bf16[592,128]{1,0:T(8,128)(2,1)S(1)}, u32[]{:S(2)}, u32[]{:S(2)}) %collective-permute-start.7) | collective-permute-done | bytes 151584 | tf_op jit(solution)/shard_map/ppermute | solution.py:305
  121.6 4.8 %attend.1 = bf16[8,64,640]{2,1,0:T(8,128)(2,1)S(1)} custom-call(f32[1,128]{1,0:T(1,128)S(1)} %convert_bitcast_fusion.starts_ref, f32[576,128]{1,0:T(8,128)S(1)} %get-tuple-element.14.place_ref, bf16[512,640]{1,0:T(8,128)(2,1)S(1)} %bitcast.16, bf16[592,256]{1,0:T(8,128)(2,1)S(1)} %get-tuple-element.18.refs_0_.refs_8_, ...), custom_call_target="tpu_custom_call" | custom-call | flops 1342177280 | bytes 1310720 | tf_op jit(solution)/shard_map/attend/pallas_call | solution.py:255
  126.5 16.1 %all_to_all.33 = bf16[8,64,640]{2,1,0:T(8,128)(2,1)S(1)} all-to-all(bf16[8,64,640]{2,1,0:T(8,128)(2,1)S(1)} %attend.1), channel_id=1, replica_groups=mesh['x'=4,'zh'=8,'zl'=2,'tp'=8] {'x','zl'}, dimensions={0} | all-to-all | bytes 1310720 | tf_op jit(solution)/shard_map/all_to_all | solution.py:272
  143.1 21.6 %all_to_all.34 = bf16[8,64,640]{2,1,0:T(8,128)(2,1)S(1)} all-to-all(bf16[8,64,640]{2,1,0:T(8,128)(2,1)S(1)} %bitcast.19), channel_id=1, replica_groups=mesh['x'=4,'zh'=8,'zl'=2,'tp'=8] {'tp'}, dimensions={0} | all-to-all | bytes 1310720 | tf_op jit(solution)/shard_map/all_to_all | solution.py:272
  (24 shorter events, 6.3 us)
Async XLA Ops:
  0.0 0.7 copy-start.2
  0.7 1.2 copy-start
  20.2 11.7 %copy-start.1 = (bf16[64,7168]{1,0:T(8,128)(2,1)S(1)}, bf16[64,7168]{1,0:T(8,128)(2,1)}, u32[]{:S(2)}) copy-start(bf16[64,7168]{1,0:T(8,128)(2,1)} %rows_ref) | copy-start | bytes 2752516
  49.0 66.2 %all-to-all-start.3 = ((bf16[8,64,640]{2,1,0:T(8,128)(2,1)}), bf16[8,64,640]{2,1,0:T(8,128)(2,1)}, u32[]{:S(2)}, u32[]{:S(2)}) async-start(bf16[8,64,640]{2,1,0:T(8,128)(2,1)} %bitcast.5), calls=%async_computation.3 | async-start | bytes 1310720 | tf_op jit(solution)/shard_map/all_to_all | solution.py:272
  53.2 24.9 %collective-permute-start = (bf16[592,256]{1,0:T(8,128)(2,1)S(1)}, bf16[592,256]{1,0:T(8,128)(2,1)S(1)}, u32[]{:S(2)}, u32[]{:S(2)}) collective-permute-start(bf16[592,256]{1,0:T(8,128)(2,1)S(1)} %get-tuple-element.18.refs_0_.refs_8_), channel_id=1, source_target_pairs={{0,16},{8,120},{16,32},{24,8},{32,48},{40,24},{48,64},{56,40},{64,... | collective-permute-start | bytes 909320 | tf_op jit(solution)/shard_map/ppermute | solution.py:305
  57.4 22.6 %collective-permute-start.1 = (bf16[592,256]{1,0:T(8,128)(2,1)S(1)}, bf16[592,256]{1,0:T(8,128)(2,1)S(1)}, u32[]{:S(2)}, u32[]{:S(2)}) collective-permute-start(bf16[592,256]{1,0:T(8,128)(2,1)S(1)} %get-tuple-element.18.refs_0_.refs_8_), channel_id=1, source_target_pairs={{0,112},{8,24},{16,0},{24,40},{32,16},{40,56},{48,32},{56,72},{64,... | collective-permute-start | bytes 909320 | tf_op jit(solution)/shard_map/ppermute | solution.py:305
  78.2 9.7 %collective-permute-start.2 = (bf16[592,256]{1,0:T(8,128)(2,1)S(1)}, bf16[592,256]{1,0:T(8,128)(2,1)S(1)}, u32[]{:S(2)}, u32[]{:S(2)}) collective-permute-start(bf16[592,256]{1,0:T(8,128)(2,1)S(1)} %collective-permute-done.refs_1_.refs_9_), channel_id=1, source_target_pairs={{0,16},{8,120},{16,32},{24,8},{32,48},{40,24},{48,64},{56,40},{64,... | collective-permute-start | bytes 909320 | tf_op jit(solution)/shard_map/ppermute | solution.py:305
  80.1 16.7 %collective-permute-start.3 = (bf16[592,256]{1,0:T(8,128)(2,1)S(1)}, bf16[592,256]{1,0:T(8,128)(2,1)S(1)}, u32[]{:S(2)}, u32[]{:S(2)}) collective-permute-start(bf16[592,256]{1,0:T(8,128)(2,1)S(1)} %collective-permute-done.1.refs_2_.refs_10_), channel_id=1, source_target_pairs={{0,112},{8,24},{16,0},{24,40},{32,16},{40,56},{48,32},{56,72},{64,... | collective-permute-start | bytes 909320 | tf_op jit(solution)/shard_map/ppermute | solution.py:305
  87.8 19.6 %collective-permute-start.4 = (bf16[592,256]{1,0:T(8,128)(2,1)S(1)}, bf16[592,256]{1,0:T(8,128)(2,1)S(1)}, u32[]{:S(2)}, u32[]{:S(2)}) collective-permute-start(bf16[592,256]{1,0:T(8,128)(2,1)S(1)} %collective-permute-done.2.refs_3_.refs_11_), channel_id=1, source_target_pairs={{0,16},{8,120},{16,32},{24,8},{32,48},{40,24},{48,64},{56,40},{64,... | collective-permute-start | bytes 909320 | tf_op jit(solution)/shard_map/ppermute | solution.py:305
  96.8 16.5 %collective-permute-start.5 = (bf16[592,256]{1,0:T(8,128)(2,1)S(1)}, bf16[592,256]{1,0:T(8,128)(2,1)S(1)}, u32[]{:S(2)}, u32[]{:S(2)}) collective-permute-start(bf16[592,256]{1,0:T(8,128)(2,1)S(1)} %collective-permute-done.3.refs_4_.refs_12_), channel_id=1, source_target_pairs={{0,112},{8,24},{16,0},{24,40},{32,16},{40,56},{48,32},{56,72},{64,... | collective-permute-start | bytes 909320 | tf_op jit(solution)/shard_map/ppermute | solution.py:305
  101.5 0.7 copy-start.3
  107.4 7.8 %copy-start.4 = (s32[128]{0:T(128)S(1)}, s32[128]{0:T(128)}, u32[]{:S(2)}) copy-start(s32[128]{0:T(128)} %reduce) | copy-start | bytes 1540
  107.5 8.9 %collective-permute-start.6 = (bf16[592,128]{1,0:T(8,128)(2,1)S(1)}, bf16[592,128]{1,0:T(8,128)(2,1)S(1)}, u32[]{:S(2)}, u32[]{:S(2)}) collective-permute-start(bf16[592,128]{1,0:T(8,128)(2,1)S(1)} %slice.8), channel_id=1, source_target_pairs={{0,16},{8,120},{16,32},{24,8},{32,48},{40,24},{48,64},{56,40},{64,... | collective-permute-start | bytes 454664 | tf_op jit(solution)/shard_map/ppermute | solution.py:305
  113.3 8.4 %collective-permute-start.7 = (bf16[592,128]{1,0:T(8,128)(2,1)S(1)}, bf16[592,128]{1,0:T(8,128)(2,1)S(1)}, u32[]{:S(2)}, u32[]{:S(2)}) collective-permute-start(bf16[592,128]{1,0:T(8,128)(2,1)S(1)} %slice.9), channel_id=1, source_target_pairs={{0,112},{8,24},{16,0},{24,40},{32,16},{40,56},{48,32},{56,72},{64,... | collective-permute-start | bytes 454664 | tf_op jit(solution)/shard_map/ppermute | solution.py:305

commit v8 on v7

--- a/solution.py
+++ b/solution.py
@@ -74,7 +74,7 @@
         compiler_params=params(),
         cost_estimate=cost(0, 4 * groups * n * KEY_CHUNK),
         name="split_keys",
-    )(target.reshape(1, n), rows, rows)
+    )(target.reshape(1, n), *[pltpu.with_memory_space_constraint(rows, pltpu.HBM)] * 2)
 
 
 def split_queries_kernel(rows_ref, out_ref):
@@ -171,12 +171,12 @@
         load_ref[at, :] = block[:, :KV_WIDTH].astype(load_ref.dtype)
         places.append(block[:, KV_WIDTH:])
         place_ref[at, :] = places[b]
-    rows = jnp.zeros((16, LANES), jnp.float32)
+    rows = jnp.zeros((8, LANES), jnp.float32)
     for b in range(1, blocks):
         pair = jnp.concatenate([places[b - 1], places[b]], axis=0)[:, 0:1]
-        rows = jnp.where(iota((16, LANES), 0) == b - 1, column_to_row(pair), rows)
+        rows = jnp.where(iota((8, LANES), 0) == b - 1, column_to_row(pair), rows)
     load_ref[blocks * span :, :HEAD_SIZE] = rows.astype(load_ref.dtype)
-    load_ref[blocks * span :, HEAD_SIZE:] = jnp.zeros((16, HEAD_SIZE), load_ref.dtype)
+    load_ref[blocks * span :, HEAD_SIZE:] = jnp.zeros((8, HEAD_SIZE), load_ref.dtype)
 
 
 def arrange(got, per_pair):
@@ -187,7 +187,7 @@
         in_specs=whole(1),
         out_specs=whole(2),
         out_shape=[
-            jax.ShapeDtypeStruct((rows + 16, KV_WIDTH), got.dtype),
+            jax.ShapeDtypeStruct((rows + 8, KV_WIDTH), got.dtype),
             jax.ShapeDtypeStruct((rows, LANES), jnp.float32),
         ],
         compiler_params=params(),
@@ -307,10 +307,12 @@
     loads = [load]
     load_a, load_b = load, load
     for _ in range(1, slabs // 2):
-        load_a, load_b = passed(load_a, 1), passed(load_b, -1)
+        load_a = passed(load_a, 1)
+        load_b = passed(load_b, -1)
         loads += [load_a, load_b]
-    values = loads + [passed(load_b[:, HEAD_SIZE:], -1)]
-    loads = loads + [passed(load_a[:, :HEAD_SIZE], 1)]
+    last_keys = passed(load_a[:, :HEAD_SIZE], 1)
+    last_values = passed(load_b[:, HEAD_SIZE:], -1)
+    loads, values = loads + [last_keys], loads + [last_values]
 
     done = attend(starts, places, queries, loads, values, parts, per_pair)
     back = exchange(done, PART).reshape(tok_dev, QUERY_WIDTH)

time: 166 us -> 167 us (level)
  Pallas kernels: 9.34 us -> 11.8 us
    pallas_call x1, Pallas kernels: 1.04 us -> 3.55 us  [split_keys(): pl.pallas_call(split_keys_kernel, grid=(groups,), in_specs=[pl.BlockSpec(...]
where the time goes in v8:
time: 167 us
  blocking collectives  81 us (49%)
  waiting for transfers between devices  35.7 us (21%)
  starting transfers between devices  34 us (20%)
  Pallas kernels  11.8 us (7%)
  local copies, waits for them, and re-layouts  3.49 us (2%)
    all_to_all x5, blocking collectives, exchange(): return lax.all_to_all(blocks, axis, split_axis=0, concat_axis=0, tiled=True)  81 us
    ppermute x8, waiting for transfers between devices, passed(): return lax.ppermute(block, RING, route)  35.7 us
    ppermute x8, starting transfers between devices, passed(): return lax.ppermute(block, RING, route)  29.8 us
    pallas_call x1, Pallas kernels, attend(): pl.pallas_call(functools.partial(attend_kernel, per_pair, len(loads)), in...  4.79 us
    all_to_all x1, starting transfers between devices, exchange(): return lax.all_to_all(blocks, axis, split_axis=0, concat_axis=0, tiled=True)  4.2 us
    pallas_call x1, Pallas kernels, split_keys(): pl.pallas_call(split_keys_kernel, grid=(groups,), in_specs=[pl.BlockSpec(...  3.55 us
  transfers between devices with their start and end apart: 9, of which 6 were waited for; matrix products, arithmetic and copies ran while one was open for 1% of the time, Pallas kernels for 0%

profile of v8, /device:TPU:1, one launch (start us, length us, event | category | flops | bytes accessed | tf_op | source)
XLA Modules:
  0.0 166.5 jit_solution(848886310746758392)
XLA Ops:
  0.7 3.6 %split_keys.1 = bf16[8,64,384]{2,1,0:T(8,128)(2,1)S(1)} custom-call(s32[1,64]{1,0:T(1,128)S(1)} %bitcast.21, bf16[64,7168]{1,0:T(8,128)(2,1)} %rows_ref, bf16[64,7168]{1,0:T(8,128)(2,1)} %rows_ref), custom_call_target="tpu_custom_call" | custom-call | bytes 786432 | tf_op jit(solution)/shard_map/split_keys/pallas_call | solution.py:64
  4.2 17.3 %all_to_all.30 = bf16[8,64,384]{2,1,0:T(8,128)(2,1)S(1)} all-to-all(bf16[8,64,384]{2,1,0:T(8,128)(2,1)S(1)} %split_keys.1), channel_id=1, replica_groups=mesh['x'=4,'zh'=8,'zl'=2,'tp'=8] {'tp'}, dimensions={0} | all-to-all | bytes 786432 | tf_op jit(solution)/shard_map/all_to_all | solution.py:272
  22.5 10.5 %all_to_all.31.got_ref = bf16[8,72,384]{2,1,0:T(8,128)(2,1)S(1)} all-to-all(bf16[8,72,384]{2,1,0:T(8,128)(2,1)S(1)} %get-tuple-element.13), channel_id=1, replica_groups=mesh['x'=4,'zh'=8,'zl'=2,'tp'=8] {'x','zl'}, dimensions={0} | all-to-all | bytes 884736 | tf_op jit(solution)/shard_map/all_to_all | solution.py:272
  33.6 15.4 %all_to_all.32 = bf16[8,64,640]{2,1,0:T(8,128)(2,1)S(1)} all-to-all(bf16[8,64,640]{2,1,0:T(8,128)(2,1)S(1)} %split_queries.1), channel_id=1, replica_groups=mesh['x'=4,'zh'=8,'zl'=2,'tp'=8] {'tp'}, dimensions={0} | all-to-all | bytes 1310720 | tf_op jit(solution)/shard_map/all_to_all | solution.py:272
  48.9 1.4 shard_map.37
  50.3 4.2 %all-to-all-start.3 = ((bf16[8,64,640]{2,1,0:T(8,128)(2,1)}), bf16[8,64,640]{2,1,0:T(8,128)(2,1)}, u32[]{:S(2)}, u32[]{:S(2)}) async-start(bf16[8,64,640]{2,1,0:T(8,128)(2,1)} %bitcast.5), calls=%async_computation.3 | async-start | bytes 1310720 | tf_op jit(solution)/shard_map/all_to_all | solution.py:272
  54.5 4.2 %collective-permute-start = (bf16[584,256]{1,0:T(8,128)(2,1)S(1)}, bf16[584,256]{1,0:T(8,128)(2,1)S(1)}, u32[]{:S(2)}, u32[]{:S(2)}) collective-permute-start(bf16[584,256]{1,0:T(8,128)(2,1)S(1)} %get-tuple-element.18.refs_0_.refs_8_), channel_id=1, source_target_pairs={{0,16},{8,120},{16,32},{24,8},{32,48},{40,24},{48,64},{56,40},{64,... | collective-permute-start | bytes 897032 | tf_op jit(solution)/shard_map/ppermute | solution.py:305
  58.8 7.7 %collective-permute-start.1 = (bf16[584,256]{1,0:T(8,128)(2,1)S(1)}, bf16[584,256]{1,0:T(8,128)(2,1)S(1)}, u32[]{:S(2)}, u32[]{:S(2)}) collective-permute-start(bf16[584,256]{1,0:T(8,128)(2,1)S(1)} %get-tuple-element.18.refs_0_.refs_8_), channel_id=1, source_target_pairs={{0,112},{8,24},{16,0},{24,40},{32,16},{40,56},{48,32},{56,72},{64,... | collective-permute-start | bytes 897032 | tf_op jit(solution)/shard_map/ppermute | solution.py:305
  66.5 12.9 %collective-permute-done.refs_1_.refs_9_ = bf16[584,256]{1,0:T(8,128)(2,1)S(1)} collective-permute-done((bf16[584,256]{1,0:T(8,128)(2,1)S(1)}, bf16[584,256]{1,0:T(8,128)(2,1)S(1)}, u32[]{:S(2)}, u32[]{:S(2)}) %collective-permute-start) | collective-permute-done | bytes 299040 | tf_op jit(solution)/shard_map/ppermute | solution.py:305
  79.4 1.9 %collective-permute-start.2 = (bf16[584,256]{1,0:T(8,128)(2,1)S(1)}, bf16[584,256]{1,0:T(8,128)(2,1)S(1)}, u32[]{:S(2)}, u32[]{:S(2)}) collective-permute-start(bf16[584,256]{1,0:T(8,128)(2,1)S(1)} %collective-permute-done.refs_1_.refs_9_), channel_id=1, source_target_pairs={{0,16},{8,120},{16,32},{24,8},{32,48},{40,24},{48,64},{56,40},{64,... | collective-permute-start | bytes 897032 | tf_op jit(solution)/shard_map/ppermute | solution.py:305
  81.3 5.5 %collective-permute-start.3 = (bf16[584,256]{1,0:T(8,128)(2,1)S(1)}, bf16[584,256]{1,0:T(8,128)(2,1)S(1)}, u32[]{:S(2)}, u32[]{:S(2)}) collective-permute-start(bf16[584,256]{1,0:T(8,128)(2,1)S(1)} %collective-permute-done.1.refs_2_.refs_10_), channel_id=1, source_target_pairs={{0,112},{8,24},{16,0},{24,40},{32,16},{40,56},{48,32},{56,72},{64,... | collective-permute-start | bytes 897032 | tf_op jit(solution)/shard_map/ppermute | solution.py:305
  86.8 2.2 %collective-permute-done.2.refs_3_.refs_11_ = bf16[584,256]{1,0:T(8,128)(2,1)S(1)} collective-permute-done((bf16[584,256]{1,0:T(8,128)(2,1)S(1)}, bf16[584,256]{1,0:T(8,128)(2,1)S(1)}, u32[]{:S(2)}, u32[]{:S(2)}) %collective-permute-start.2) | collective-permute-done | bytes 299040 | tf_op jit(solution)/shard_map/ppermute | solution.py:305
  89.0 1.9 %collective-permute-start.4 = (bf16[584,256]{1,0:T(8,128)(2,1)S(1)}, bf16[584,256]{1,0:T(8,128)(2,1)S(1)}, u32[]{:S(2)}, u32[]{:S(2)}) collective-permute-start(bf16[584,256]{1,0:T(8,128)(2,1)S(1)} %collective-permute-done.2.refs_3_.refs_11_), channel_id=1, source_target_pairs={{0,16},{8,120},{16,32},{24,8},{32,48},{40,24},{48,64},{56,40},{64,... | collective-permute-start | bytes 897032 | tf_op jit(solution)/shard_map/ppermute | solution.py:305
  90.9 6.7 %collective-permute-done.3.refs_4_.refs_12_ = bf16[584,256]{1,0:T(8,128)(2,1)S(1)} collective-permute-done((bf16[584,256]{1,0:T(8,128)(2,1)S(1)}, bf16[584,256]{1,0:T(8,128)(2,1)S(1)}, u32[]{:S(2)}, u32[]{:S(2)}) %collective-permute-start.3) | collective-permute-done | bytes 299040 | tf_op jit(solution)/shard_map/ppermute | solution.py:305
  97.6 4.8 %collective-permute-start.5 = (bf16[584,256]{1,0:T(8,128)(2,1)S(1)}, bf16[584,256]{1,0:T(8,128)(2,1)S(1)}, u32[]{:S(2)}, u32[]{:S(2)}) collective-permute-start(bf16[584,256]{1,0:T(8,128)(2,1)S(1)} %collective-permute-done.3.refs_4_.refs_12_), channel_id=1, source_target_pairs={{0,112},{8,24},{16,0},{24,40},{32,16},{40,56},{48,32},{56,72},{64,... | collective-permute-start | bytes 897032 | tf_op jit(solution)/shard_map/ppermute | solution.py:305
  103.5 4.7 %collective-permute-done.4.refs_5_.refs_13_ = bf16[584,256]{1,0:T(8,128)(2,1)S(1)} collective-permute-done((bf16[584,256]{1,0:T(8,128)(2,1)S(1)}, bf16[584,256]{1,0:T(8,128)(2,1)S(1)}, u32[]{:S(2)}, u32[]{:S(2)}) %collective-permute-start.4) | collective-permute-done | bytes 299040 | tf_op jit(solution)/shard_map/ppermute | solution.py:305
  108.2 1.9 %collective-permute-start.6 = (bf16[584,128]{1,0:T(8,128)(2,1)S(1)}, bf16[584,128]{1,0:T(8,128)(2,1)S(1)}, u32[]{:S(2)}, u32[]{:S(2)}) collective-permute-start(bf16[584,128]{1,0:T(8,128)(2,1)S(1)} %slice.8), channel_id=1, source_target_pairs={{0,16},{8,120},{16,32},{24,8},{32,48},{40,24},{48,64},{56,40},{64,... | collective-permute-start | bytes 448520 | tf_op jit(solution)/shard_map/ppermute | solution.py:305
  110.1 3.9 %collective-permute-done.5.refs_6_.refs_14_ = bf16[584,256]{1,0:T(8,128)(2,1)S(1)} collective-permute-done((bf16[584,256]{1,0:T(8,128)(2,1)S(1)}, bf16[584,256]{1,0:T(8,128)(2,1)S(1)}, u32[]{:S(2)}, u32[]{:S(2)}) %collective-permute-start.5) | collective-permute-done | bytes 299040 | tf_op jit(solution)/shard_map/ppermute | solution.py:305
  114.1 1.9 %collective-permute-start.7 = (bf16[584,128]{1,0:T(8,128)(2,1)S(1)}, bf16[584,128]{1,0:T(8,128)(2,1)S(1)}, u32[]{:S(2)}, u32[]{:S(2)}) collective-permute-start(bf16[584,128]{1,0:T(8,128)(2,1)S(1)} %slice.9), channel_id=1, source_target_pairs={{0,112},{8,24},{16,0},{24,40},{32,16},{40,56},{48,32},{56,72},{64,... | collective-permute-start | bytes 448520 | tf_op jit(solution)/shard_map/ppermute | solution.py:305
  116.0 1.1 copy.7
  117.2 5.2 %collective-permute-done.7.refs_15_ = bf16[584,128]{1,0:T(8,128)(2,1)S(1)} collective-permute-done((bf16[584,128]{1,0:T(8,128)(2,1)S(1)}, bf16[584,128]{1,0:T(8,128)(2,1)S(1)}, u32[]{:S(2)}, u32[]{:S(2)}) %collective-permute-start.7) | collective-permute-done | bytes 149536 | tf_op jit(solution)/shard_map/ppermute | solution.py:305
  122.4 4.8 %attend.1 = bf16[8,64,640]{2,1,0:T(8,128)(2,1)S(1)} custom-call(f32[1,128]{1,0:T(1,128)S(1)} %convert_bitcast_fusion.starts_ref, f32[576,128]{1,0:T(8,128)S(1)} %get-tuple-element.14.place_ref, bf16[512,640]{1,0:T(8,128)(2,1)S(1)} %bitcast.19, bf16[584,256]{1,0:T(8,128)(2,1)S(1)} %get-tuple-element.18.refs_0_.refs_8_, ...), custom_call_target="tpu_custom_call" | custom-call | flops 1342177280 | bytes 1310720 | tf_op jit(solution)/shard_map/attend/pallas_call | solution.py:255
  127.2 16.2 %all_to_all.33 = bf16[8,64,640]{2,1,0:T(8,128)(2,1)S(1)} all-to-all(bf16[8,64,640]{2,1,0:T(8,128)(2,1)S(1)} %attend.1), channel_id=1, replica_groups=mesh['x'=4,'zh'=8,'zl'=2,'tp'=8] {'x','zl'}, dimensions={0} | all-to-all | bytes 1310720 | tf_op jit(solution)/shard_map/all_to_all | solution.py:272
  143.9 21.7 %all_to_all.34 = bf16[8,64,640]{2,1,0:T(8,128)(2,1)S(1)} all-to-all(bf16[8,64,640]{2,1,0:T(8,128)(2,1)S(1)} %bitcast.18), channel_id=1, replica_groups=mesh['x'=4,'zh'=8,'zl'=2,'tp'=8] {'tp'}, dimensions={0} | all-to-all | bytes 1310720 | tf_op jit(solution)/shard_map/all_to_all | solution.py:272
  (20 shorter events, 4.7 us)
Async XLA Ops:
  0.0 0.7 copy-start.1
  21.5 11.7 %copy-start = (bf16[64,7168]{1,0:T(8,128)(2,1)S(1)}, bf16[64,7168]{1,0:T(8,128)(2,1)}, u32[]{:S(2)}) copy-start(bf16[64,7168]{1,0:T(8,128)(2,1)} %rows_ref) | copy-start | bytes 2752516
  50.3 65.7 %all-to-all-start.3 = ((bf16[8,64,640]{2,1,0:T(8,128)(2,1)}), bf16[8,64,640]{2,1,0:T(8,128)(2,1)}, u32[]{:S(2)}, u32[]{:S(2)}) async-start(bf16[8,64,640]{2,1,0:T(8,128)(2,1)} %bitcast.5), calls=%async_computation.3 | async-start | bytes 1310720 | tf_op jit(solution)/shard_map/all_to_all | solution.py:272
  54.5 24.9 %collective-permute-start = (bf16[584,256]{1,0:T(8,128)(2,1)S(1)}, bf16[584,256]{1,0:T(8,128)(2,1)S(1)}, u32[]{:S(2)}, u32[]{:S(2)}) collective-permute-start(bf16[584,256]{1,0:T(8,128)(2,1)S(1)} %get-tuple-element.18.refs_0_.refs_8_), channel_id=1, source_target_pairs={{0,16},{8,120},{16,32},{24,8},{32,48},{40,24},{48,64},{56,40},{64,... | collective-permute-start | bytes 897032 | tf_op jit(solution)/shard_map/ppermute | solution.py:305
  58.8 22.6 %collective-permute-start.1 = (bf16[584,256]{1,0:T(8,128)(2,1)S(1)}, bf16[584,256]{1,0:T(8,128)(2,1)S(1)}, u32[]{:S(2)}, u32[]{:S(2)}) collective-permute-start(bf16[584,256]{1,0:T(8,128)(2,1)S(1)} %get-tuple-element.18.refs_0_.refs_8_), channel_id=1, source_target_pairs={{0,112},{8,24},{16,0},{24,40},{32,16},{40,56},{48,32},{56,72},{64,... | collective-permute-start | bytes 897032 | tf_op jit(solution)/shard_map/ppermute | solution.py:305
  79.4 9.6 %collective-permute-start.2 = (bf16[584,256]{1,0:T(8,128)(2,1)S(1)}, bf16[584,256]{1,0:T(8,128)(2,1)S(1)}, u32[]{:S(2)}, u32[]{:S(2)}) collective-permute-start(bf16[584,256]{1,0:T(8,128)(2,1)S(1)} %collective-permute-done.refs_1_.refs_9_), channel_id=1, source_target_pairs={{0,16},{8,120},{16,32},{24,8},{32,48},{40,24},{48,64},{56,40},{64,... | collective-permute-start | bytes 897032 | tf_op jit(solution)/shard_map/ppermute | solution.py:305
  81.3 16.3 %collective-permute-start.3 = (bf16[584,256]{1,0:T(8,128)(2,1)S(1)}, bf16[584,256]{1,0:T(8,128)(2,1)S(1)}, u32[]{:S(2)}, u32[]{:S(2)}) collective-permute-start(bf16[584,256]{1,0:T(8,128)(2,1)S(1)} %collective-permute-done.1.refs_2_.refs_10_), channel_id=1, source_target_pairs={{0,112},{8,24},{16,0},{24,40},{32,16},{40,56},{48,32},{56,72},{64,... | collective-permute-start | bytes 897032 | tf_op jit(solution)/shard_map/ppermute | solution.py:305
  89.0 19.2 %collective-permute-start.4 = (bf16[584,256]{1,0:T(8,128)(2,1)S(1)}, bf16[584,256]{1,0:T(8,128)(2,1)S(1)}, u32[]{:S(2)}, u32[]{:S(2)}) collective-permute-start(bf16[584,256]{1,0:T(8,128)(2,1)S(1)} %collective-permute-done.2.refs_3_.refs_11_), channel_id=1, source_target_pairs={{0,16},{8,120},{16,32},{24,8},{32,48},{40,24},{48,64},{56,40},{64,... | collective-permute-start | bytes 897032 | tf_op jit(solution)/shard_map/ppermute | solution.py:305
  97.6 16.4 %collective-permute-start.5 = (bf16[584,256]{1,0:T(8,128)(2,1)S(1)}, bf16[584,256]{1,0:T(8,128)(2,1)S(1)}, u32[]{:S(2)}, u32[]{:S(2)}) collective-permute-start(bf16[584,256]{1,0:T(8,128)(2,1)S(1)} %collective-permute-done.3.refs_4_.refs_12_), channel_id=1, source_target_pairs={{0,112},{8,24},{16,0},{24,40},{32,16},{40,56},{48,32},{56,72},{64,... | collective-permute-start | bytes 897032 | tf_op jit(solution)/shard_map/ppermute | solution.py:305
  102.4 0.7 copy-start.2
  108.2 9.0 %collective-permute-start.6 = (bf16[584,128]{1,0:T(8,128)(2,1)S(1)}, bf16[584,128]{1,0:T(8,128)(2,1)S(1)}, u32[]{:S(2)}, u32[]{:S(2)}) collective-permute-start(bf16[584,128]{1,0:T(8,128)(2,1)S(1)} %slice.8), channel_id=1, source_target_pairs={{0,16},{8,120},{16,32},{24,8},{32,48},{40,24},{48,64},{56,40},{64,... | collective-permute-start | bytes 448520 | tf_op jit(solution)/shard_map/ppermute | solution.py:305
  114.1 8.3 %collective-permute-start.7 = (bf16[584,128]{1,0:T(8,128)(2,1)S(1)}, bf16[584,128]{1,0:T(8,128)(2,1)S(1)}, u32[]{:S(2)}, u32[]{:S(2)}) collective-permute-start(bf16[584,128]{1,0:T(8,128)(2,1)S(1)} %slice.9), channel_id=1, source_target_pairs={{0,112},{8,24},{16,0},{24,40},{32,16},{40,56},{48,32},{56,72},{64,... | collective-permute-start | bytes 448520 | tf_op jit(solution)/shard_map/ppermute | solution.py:305
